TPU v7x, 32 devices: a whole 2x2x4 slice. The times are simulated.
32 devices in a mesh: dp: 8 (over z, y), mp: 4 (over x, core).
Axes of the slice: x: 2, y: 2, z: 4, core: 2. Of those that a mesh axis runs over, the one named last changes fastest.
Arguments:
- hidden_in: bfloat16 [32768, 768], P(('dp', 'mp')), may hold values from -37 to 37
- out_grad: bfloat16 [32768, 768], P(('dp', 'mp')), may hold values from -18 to 18
- seq_len: int32 [8], P('dp'), may hold values from 1024 to 4096, as said below
- owner_list: int32 [24], replicated, may hold values from 0 to 7, as said below
- block_master: float32 [4, 8, 768, 194], P('mp', 'dp'), may hold values from -0.4690971 to 0.4690971
- block_first: float32 [4, 8, 768, 194], P('mp', 'dp'), may hold values from -2048 to 2048
- block_second: float32 [4, 8, 768, 194], P('mp', 'dp'), may hold values from 131072 to 524288
- block_ema: float32 [4, 8, 768, 194], P('mp', 'dp'), may hold values from -0.21875 to 0.21875
- head_small: float32 [24, 10, 64], P('mp'), may hold values from -10 to 3
- head_first: float32 [24, 10, 64], P('mp'), may hold values from -1024 to 1024
- head_second: float32 [24, 10, 64], P('mp'), may hold values from 32768 to 131072
- head_ema: float32 [24, 10, 64], P('mp'), may hold values from -6 to 6
- bc_weight: float32 [768, 256], replicated, may hold values from -0.21875 to 0.21875
- bc_first: float32 [768, 256], replicated, may hold values from -1024 to 1024
- bc_second: float32 [768, 256], replicated, may hold values from 32768 to 131072
- bc_ema: float32 [768, 256], replicated, may hold values from -0.21875 to 0.21875
- shared_small: float32 [10, 256], replicated, may hold values from 0.25 to 1.25
- shared_first: float32 [10, 256], replicated, may hold values from -1024 to 1024
- shared_second: float32 [10, 256], replicated, may hold values from 32768 to 131072
- shared_ema: float32 [10, 256], replicated, may hold values from 0.25 to 1.25
Outputs:
- hidden_out: bfloat16 [32768, 768], P(('dp', 'mp'))
- hidden_grad: float32 [32768, 768], P(('dp', 'mp'))
- block_master_new: float32 [4, 8, 768, 194], P('mp', 'dp')
- block_first_new: float32 [4, 8, 768, 194], P('mp', 'dp')
- block_second_new: float32 [4, 8, 768, 194], P('mp', 'dp')
- block_ema_new: float32 [4, 8, 768, 194], P('mp', 'dp')
- head_small_new: float32 [24, 10, 64], P('mp')
- head_first_new: float32 [24, 10, 64], P('mp')
- head_second_new: float32 [24, 10, 64], P('mp')
- head_ema_new: float32 [24, 10, 64], P('mp')
- bc_weight_new: float32 [768, 256], replicated
- bc_first_new: float32 [768, 256], replicated
- bc_second_new: float32 [768, 256], replicated
- bc_ema_new: float32 [768, 256], replicated
- shared_small_new: float32 [10, 256], replicated
- shared_first_new: float32 [10, 256], replicated
- shared_second_new: float32 [10, 256], replicated
- shared_ema_new: float32 [10, 256], replicated
Inputs may be any that keep to these rules, and one draw needn't show every extreme that they name: `seq_len`: all sequences of a group have the same length, one of 1024, 2048, 4096; each of the three occurs in every draw. `owner_list`: the 6 heads of one index of mp (heads i * 6 to (i + 1) * 6 - 1) have distinct owners.
All inputs are finite; a program needn't handle non-finite values.
Results may differ from a plain program's by a relative error of at most 0.01.
Values may be sent and summed in bfloat16 or wider, within the bound.
No kernel may reach another device: no remote copies, remote signals or barrier semaphores. Data moves between devices by JAX's collectives and lax.ppermute only.
A program may use at most 448 MiB of HBM per device.

v0:
```python
import jax
import jax.numpy as jnp
from jax import lax
from jax.sharding import PartitionSpec as P

D = 768
H = 24
P_SIZE = 64
K = 7
BLOCK_LEN = 256
STEP = 3


PRECISE = lax.Precision.HIGHEST
NORM_EPS = 1e-05
BETA_ONE = 0.5
BETA_TWO = 0.5
ADAM_EPS = 1e-08
WEIGHT_DECAY = 0.1
MATRIX_RATE = 0.04
SMALL_RATE = 0.2
AVERAGE_KEEP = 0.75


def conv_centered(signal, filter_taps, seq_length):
    row_count = signal.shape[0]
    tap_count = filter_taps.shape[0]
    half_taps = tap_count // 2
    position = jnp.arange(row_count, dtype=jnp.int32) % seq_length
    padded = jnp.pad(signal, ((half_taps, half_taps), (0, 0)))
    summed = jnp.zeros_like(signal)
    for tap_index in range(tap_count):
        offset = tap_index - half_taps
        shifted = padded[tap_index : tap_index + row_count]
        inside = (position + offset >= 0) & (position + offset < seq_length)
        summed = summed + jnp.where(inside[:, None], shifted, 0.0) * filter_taps[tap_index][None, :]
    return summed


def shift_down(values, seq_length):
    shifted = jnp.concatenate([jnp.zeros_like(values[:1]), values[:-1]], axis=0)
    position = jnp.arange(values.shape[0], dtype=jnp.int32) % seq_length
    return jnp.where((position > 0)[:, None, None], shifted, 0.0)


def within_blocks(values_blk, b_blk, c_blk, rates_blk):
    log_decay = jnp.transpose(jnp.cumsum(-rates_blk, axis=1), (0, 2, 1))
    block_size = rates_blk.shape[1]
    scores = jnp.einsum("bin,bjn->bij", c_blk, b_blk, precision=PRECISE)
    causal_mask = (jnp.arange(block_size)[:, None] >= jnp.arange(block_size)[None, :])[None, None]
    log_gap = log_decay[:, :, :, None] - log_decay[:, :, None, :]
    decay_mat = jnp.where(causal_mask, jnp.exp(jnp.where(causal_mask, log_gap, -60.0)), 0.0)
    weights = decay_mat * scores[:, None] * jnp.transpose(rates_blk, (0, 2, 1))[:, :, None, :]
    inner_part = jnp.einsum("bhij,bjhp->bihp", weights, values_blk, precision=PRECISE)
    tail_decay = jnp.exp(log_decay[:, :, -1:] - log_decay) * jnp.transpose(rates_blk, (0, 2, 1))
    local_state = jnp.einsum("bjn,bhj,bjhp->bhnp", b_blk, tail_decay, values_blk, precision=PRECISE)
    return (inner_part, local_state, log_decay)


def carry_state(state_in, pieces):
    local_state, total_decay, keep_flag = pieces
    entering = state_in * keep_flag
    new_state = entering * jnp.exp(total_decay)[:, None, None] + local_state
    return (new_state, entering)


def state_mix(values, b_vectors, c_vectors, step_rates, seq_length):
    row_count, head_count, head_width = values.shape
    blocks = row_count // BLOCK_LEN
    keep_flags = (jnp.arange(blocks, dtype=jnp.int32) * BLOCK_LEN % seq_length != 0).astype(
        jnp.float32
    )
    values_blk = values.reshape(blocks, BLOCK_LEN, head_count, head_width)
    b_blk = b_vectors.reshape(blocks, BLOCK_LEN, -1)
    c_blk = c_vectors.reshape(blocks, BLOCK_LEN, -1)
    rates_blk = step_rates.reshape(blocks, BLOCK_LEN, head_count)
    inner_part, local_state, log_decay = jax.checkpoint(within_blocks)(
        values_blk, b_blk, c_blk, rates_blk
    )
    initial = jnp.zeros((head_count, b_vectors.shape[1], head_width), jnp.float32)
    _, entering_all = lax.scan(carry_state, initial, (local_state, log_decay[:, :, -1], keep_flags))
    cross_part = jnp.einsum("bin,bhnp->bihp", c_blk, entering_all, precision=PRECISE)
    cross_part = cross_part * jnp.transpose(jnp.exp(log_decay), (0, 2, 1))[:, :, :, None]
    return (inner_part + cross_part).reshape(row_count, head_count, head_width)


def local_mix(proj_heads, proj_keys, head_params, key_taps, seq_length):
    row_count, head_count, _ = proj_heads.shape
    head_width = head_params.shape[2]
    tap_count = key_taps.shape[0]
    gate_part = proj_heads[:, :, :head_width]
    value_part = proj_heads[:, :, head_width : 2 * head_width].reshape(
        row_count, head_count * head_width
    )
    rate_part = proj_heads[:, :, 2 * head_width : 2 * head_width + 2]
    value_taps = jnp.transpose(head_params[:, 1 : 1 + tap_count, :], (1, 0, 2)).reshape(
        tap_count, head_count * head_width
    )
    values = jax.nn.silu(conv_centered(value_part, value_taps, seq_length)).reshape(
        row_count, head_count, head_width
    )
    key_signal = jax.nn.silu(conv_centered(proj_keys, key_taps, seq_length))
    state_size = key_signal.shape[1] // 4
    forward_b = key_signal[:, :state_size]
    forward_c = key_signal[:, state_size : 2 * state_size]
    reverse_b = key_signal[:, 2 * state_size : 3 * state_size]
    reverse_c = key_signal[:, 3 * state_size :]
    step_rates = jax.nn.softplus(rate_part + head_params[None, :, tap_count + 2, :2])
    diagonal = head_params[:, tap_count + 1, :]
    forward = shift_down(
        state_mix(values, forward_b, forward_c, step_rates[:, :, 0], seq_length), seq_length
    )
    backward = shift_down(
        state_mix(
            values[::-1], reverse_b[::-1], reverse_c[::-1], step_rates[::-1, :, 1], seq_length
        ),
        seq_length,
    )[::-1]
    mixture = forward + backward + values * diagonal[None]
    return mixture * jax.nn.silu(gate_part)


def adamw_update(weight, gradient, first_moment, second, average, step_rate):
    first_new = BETA_ONE * first_moment + (1.0 - BETA_ONE) * gradient
    second_new = BETA_TWO * second + (1.0 - BETA_TWO) * gradient * gradient
    correct_one = 1.0 - BETA_ONE**STEP
    correct_two = 1.0 - BETA_TWO**STEP
    normalized = first_new / correct_one / (jnp.sqrt(second_new / correct_two) + ADAM_EPS)
    weight_new = weight - step_rate * (normalized + WEIGHT_DECAY * weight)
    average_new = AVERAGE_KEEP * average + (1.0 - AVERAGE_KEEP) * weight_new
    return (weight_new, first_new, second_new, average_new)


def local(
    hidden_in,
    out_grad,
    seq_len,
    owner_list,
    block_master,
    block_first,
    block_second,
    block_ema,
    head_small,
    head_first,
    head_second,
    head_ema,
    bc_weight,
    bc_first,
    bc_second,
    bc_ema,
    shared_small,
    shared_first,
    shared_second,
    shared_ema,
):
    heads_here = head_small.shape[0]
    mp_index = lax.axis_index("mp")
    dp_index = lax.axis_index("dp")
    seq_length = seq_len[0]
    owners_here = lax.dynamic_slice_in_dim(owner_list, mp_index * heads_here, heads_here)
    slot_low = block_master[0].astype(jnp.bfloat16)
    all_slots = lax.all_gather(slot_low, "dp", axis=0, tiled=True)
    blocks = jnp.take(all_slots, owners_here, axis=0)
    in_width = 2 * P_SIZE + 2
    w_in_flat = jnp.transpose(blocks[:, :, :in_width], (1, 0, 2)).reshape(D, heads_here * in_width)
    w_out_flat = jnp.transpose(blocks[:, :, in_width:], (0, 2, 1)).reshape(heads_here * P_SIZE, D)
    key_low = bc_weight.astype(jnp.bfloat16)
    key_taps = shared_small[:K]
    gain_in = shared_small[K:].reshape(D)
    hidden = hidden_in.astype(jnp.float32)
    scale_in = lax.rsqrt(jnp.mean(hidden * hidden, axis=1, keepdims=True) + NORM_EPS)
    normed_low = (hidden * scale_in * gain_in).astype(jnp.bfloat16)
    features = lax.all_gather(normed_low, "mp", axis=0, tiled=True)
    group_rows = features.shape[0]
    proj_heads = jnp.dot(features, w_in_flat, preferred_element_type=jnp.float32).reshape(
        group_rows, heads_here, in_width
    )
    proj_keys = jnp.dot(features, key_low, preferred_element_type=jnp.float32)

    def mixing(heads_in, keys_in, params_in, taps_in):
        return local_mix(heads_in, keys_in, params_in, taps_in, seq_length)

    gated_mix, mix_pullback = jax.vjp(mixing, proj_heads, proj_keys, head_small, key_taps)
    gain_mix = head_small[:, 0, :]
    square_rows = jnp.sum(gated_mix * gated_mix, axis=(1, 2))
    square_total = lax.psum(square_rows, "mp")
    scale_mix = lax.rsqrt(square_total / (H * P_SIZE) + NORM_EPS)[:, None, None]
    normal_mix = gated_mix * scale_mix
    result_low = (
        (normal_mix * gain_mix[None]).astype(jnp.bfloat16).reshape(group_rows, heads_here * P_SIZE)
    )
    rows_in = result_low
    branch_out = lax.psum_scatter(
        jnp.dot(rows_in, w_out_flat, preferred_element_type=jnp.float32),
        "mp",
        scatter_dimension=0,
        tiled=True,
    )
    hidden_out = (hidden + branch_out).astype(jnp.bfloat16)
    grad_full = lax.all_gather(out_grad, "mp", axis=0, tiled=True)
    out_weight_grad = lax.dot_general(
        result_low, grad_full, (((0,), (0,)), ((), ())), preferred_element_type=jnp.float32
    )
    result_grad = lax.dot_general(
        grad_full, w_out_flat, (((1,), (1,)), ((), ())), preferred_element_type=jnp.float32
    ).reshape(group_rows, heads_here, P_SIZE)
    gain_mix_grad = jnp.sum(result_grad * normal_mix, axis=0)
    normal_grad = result_grad * gain_mix[None]
    cross_rows = jnp.sum(normal_grad * gated_mix, axis=(1, 2))
    cross_total = lax.psum(cross_rows, "mp")
    gated_grad = (
        scale_mix * normal_grad
        - gated_mix * scale_mix**3 * (cross_total / (H * P_SIZE))[:, None, None]
    )
    heads_grad, keys_grad, params_grad, taps_grad = mix_pullback(gated_grad)
    params_grad = params_grad.at[:, 0, :].add(gain_mix_grad)
    heads_low = heads_grad.reshape(group_rows, heads_here * in_width).astype(jnp.bfloat16)
    keys_own = lax.psum_scatter(keys_grad, "mp", scatter_dimension=0, tiled=True)
    keys_low = keys_own.astype(jnp.bfloat16)
    in_weight_grad = lax.dot_general(
        features, heads_low, (((0,), (0,)), ((), ())), preferred_element_type=jnp.float32
    )
    in_weight_grad = jnp.transpose(in_weight_grad.reshape(D, heads_here, in_width), (1, 0, 2))
    block_grad = jnp.concatenate(
        [in_weight_grad, jnp.transpose(out_weight_grad.reshape(heads_here, P_SIZE, D), (0, 2, 1))],
        axis=2,
    )
    key_weight_grad = lax.dot_general(
        normed_low, keys_low, (((0,), (0,)), ((), ())), preferred_element_type=jnp.float32
    )
    rows_in = heads_low
    normed_grad = lax.psum_scatter(
        lax.dot_general(
            rows_in, w_in_flat, (((1,), (1,)), ((), ())), preferred_element_type=jnp.float32
        ),
        "mp",
        scatter_dimension=0,
        tiled=True,
    )
    normed_grad = normed_grad + lax.dot_general(
        keys_low, key_low, (((1,), (1,)), ((), ())), preferred_element_type=jnp.float32
    )
    gain_in_grad = jnp.sum(normed_grad * hidden * scale_in, axis=0)
    scaled_in = normed_grad * gain_in
    cross_in = jnp.sum(scaled_in * hidden, axis=1, keepdims=True)
    hidden_grad = (
        out_grad.astype(jnp.float32) + scale_in * scaled_in - hidden * scale_in**3 * cross_in / D
    )
    shared_grad = jnp.concatenate([taps_grad, gain_in_grad.reshape(-1, taps_grad.shape[1])], axis=0)
    block_total, params_total = lax.psum((block_grad, params_grad), "dp")
    key_total, shared_total = lax.psum((key_weight_grad, shared_grad), ("dp", "mp"))
    head_new = adamw_update(head_small, params_total, head_first, head_second, head_ema, SMALL_RATE)
    key_new = adamw_update(bc_weight, key_total, bc_first, bc_second, bc_ema, MATRIX_RATE)
    shared_new = adamw_update(
        shared_small, shared_total, shared_first, shared_second, shared_ema, SMALL_RATE
    )
    owned_mask = (owners_here == dp_index).astype(jnp.float32)
    own_grad = jnp.tensordot(owned_mask, block_total, axes=1)
    is_owner = jnp.sum(owned_mask) > 0.5
    previous_all = (block_master[0, 0], block_first[0, 0], block_second[0, 0], block_ema[0, 0])
    slot_new = adamw_update(
        previous_all[0], own_grad, previous_all[1], previous_all[2], previous_all[3], MATRIX_RATE
    )
    slot_outs = [
        jnp.where(is_owner, renewed, previous)[None, None]
        for renewed, previous in zip(slot_new, previous_all)
    ]
    return (
        hidden_out,
        hidden_grad,
        slot_outs[0],
        slot_outs[1],
        slot_outs[2],
        slot_outs[3],
        head_new[0],
        head_new[1],
        head_new[2],
        head_new[3],
        key_new[0],
        key_new[1],
        key_new[2],
        key_new[3],
        shared_new[0],
        shared_new[1],
        shared_new[2],
        shared_new[3],
    )


def solution(mesh):
    placed = (
        P(("dp", "mp"), None),
        P(("dp", "mp"), None),
        P("dp"),
        P(),
        P("mp", "dp", None, None),
        P("mp", "dp", None, None),
        P("mp", "dp", None, None),
        P("mp", "dp", None, None),
        P("mp", None, None),
        P("mp", None, None),
        P("mp", None, None),
        P("mp", None, None),
        P(),
        P(),
        P(),
        P(),
        P(),
        P(),
        P(),
        P(),
    )
    return jax.shard_map(
        local,
        mesh=mesh,
        in_specs=placed,
        out_specs=(
            P(("dp", "mp"), None),
            P(("dp", "mp"), None),
            P("mp", "dp", None, None),
            P("mp", "dp", None, None),
            P("mp", "dp", None, None),
            P("mp", "dp", None, None),
            P("mp", None, None),
            P("mp", None, None),
            P("mp", None, None),
            P("mp", None, None),
            P(),
            P(),
            P(),
            P(),
            P(),
            P(),
            P(),
            P(),
        ),
        check_vma=False,
    )
```

profile of v0, /device:TPU:1, one launch (start us, length us, event | category | flops | bytes accessed | tf_op | source)
XLA Modules:
  0.0 1657.8 jit_solution(6648036908415490787)
XLA Ops:
  21.4 43.5 %all-gather.9.cloned.1.call-done = bf16[8,1,768,194]{2,3,1,0:T(8,128)(2,1)} async-done(((bf16[1,1,768,194]{2,3,1,0:T(8,128)(2,1)}), bf16[8,1,768,194]{2,3,1,0:T(8,128)(2,1)}) %all-gather.9.cloned.1.call-update) | async-done | bytes 2383888 | tf_op jit(solution)/shard_map/all_gather | solution.py:162
  72.8 40.8 %all-gather.5.cloned.1.call-done = bf16[4096,768]{1,0:T(8,128)(2,1)} async-done(((bf16[1024,768]{1,0:T(8,128)(2,1)}), bf16[4096,768]{1,0:T(8,128)(2,1)}) %all-gather.5.cloned.1.call-update) | async-done | bytes 6291472 | tf_op jit(solution)/shard_map/all_gather | solution.py:173
  131.9 13.6 rev.33
  173.0 29.0 %fusion.98 = (f32[4096,384]{0,1:T(8,128)}, f32[4096,384]{0,1:T(8,128)}) fusion(f32[384]{0:T(512)S(1)} %mul.996, pred[4096]{0:T(1024)(128)(4,1)S(1)} %get-tuple-element.1093, f32[384]{0:T(512)S(1)} %mul.993, pred[4096]{0:T(1024)(128)(4,1)S(1)} %get-tuple-element.1094, f32[384]{0:T(512)S(1)} %mul.990, pred[4096]{0:T(1024)(128)(4,1)S(1)} %get-tuple-element.1095, ...), kind=kLoop, calls=%fused_computation.187 | loop fusion | flops 37748736 | bytes 18913792 | tf_op jit(solution)/shard_map/jvp(jit(silu))/mul | solution.py:99
  202.0 20.0 %rev.30 = f32[4096,6,64]{0,2,1:T(8,128)} reverse(f32[4096,6,64]{0,2,1:T(8,128)} %bitcast.605), dimensions={0} | reverse | bytes 12582912 | tf_op jit(solution)/shard_map/jvp()/rev | solution.py:115
  233.0 60.8 %while.74 = (s32[]{:T(128)}, f32[6,64,64]{2,1,0:T(8,128)S(1)}, f32[16,6,64,64]{3,2,1,0:T(8,128)}, f32[16,6]{1,0:T(8,128)S(1)}, f32[16,6,1,1]{1,3,2,0:T(1,128)S(1...) while((s32[]{:T(128)}, f32[6,64,64]{2,1,0:T(8,128)S(1)}, ...), condition=%wide.region_8.9_spmd.clone, body=%wide.region_7.8_spmd.clone.sunk | while | flops 147459 | bytes 985312 | solution.py:81
  316.0 60.5 %while.73 = (s32[]{:T(128)}, f32[6,64,64]{2,1,0:T(8,128)S(1)}, f32[16,6,64,64]{3,2,1,0:T(8,128)}, f32[16,6]{1,0:T(8,128)S(1)}, f32[16,6,1,1]{1,3,2,0:T(1,128)S(1...) while((s32[]{:T(128)}, f32[6,64,64]{2,1,0:T(8,128)S(1)}, ...), condition=%wide.region_4.5_spmd.clone, body=%wide.region_3.4_spmd.clone.sunk | while | flops 147459 | bytes 985312 | solution.py:81
  376.6 16.5 rev.32
  410.9 29.4 %fusion.84 = f32[16,6,8,8,256]{4,3,2,1,0:T(8,128)S(1)} fusion(f32[16,256,6,64]{1,3,2,0:T(8,128)S(1)} %bitcast.666, f32[16,256,6]{1,2,0:T(8,128)S(1)} %get-tuple-element.1065, f32[16,6,256]{2,1,0:T(8,128)S(1)} %copy.611, f32[16,256,256]{2,1,0:T(8,128)S(1)} %fusion.278, f32[16,6,256]{2,1,0:T(8,128)S(1)} %get-tuple-element.1064, ...), kind=kOutput, calls=%fused_computation.144 | convolution fusion | flops 4866441216 | bytes 23429120 | tf_op jit(solution)/shard_map/jvp(bhij,bjhp->bihp)/dot_general | solution.py:54
  445.5 20.1 %rev.34 = f32[4096,6,64]{0,2,1:T(8,128)} reverse(f32[4096,6,64]{0,2,1:T(8,128)} %pad_select_fusion), dimensions={0} | reverse | bytes 12582912 | tf_op jit(solution)/shard_map/jvp()/rev | solution.py:113
  484.3 34.6 %fusion.85 = f32[16,6,8,8,256]{4,3,2,1,0:T(8,128)} fusion(f32[16,256,6,64]{1,3,2,0:T(8,128)} %bitcast.668, f32[16,256,6]{1,2,0:T(8,128)S(1)} %get-tuple-element.1063, f32[16,6,256]{2,1,0:T(8,128)S(1)} %copy.593, f32[16,256,256]{2,1,0:T(8,128)} %fusion.276, f32[16,6,256]{2,1,0:T(8,128)S(1)} %get-tuple-element.1062, pred[256,256]{1,0:T(8,128)(4,1)S(1)} %copy-done.79, ...), kind=kOutput, calls=%fused_computation.146 | convolution fusion | flops 4866441216 | bytes 23429120 | tf_op jit(solution)/shard_map/jvp(bhij,bjhp->bihp)/dot_general | solution.py:54
  561.7 17.4 %multiply_reduce_fusion.14 = (f32[6,64]{1,0:T(8,128)}, f32[4096,6,64]{0,2,1:T(8,128)}, f32[4096,6,64]{0,2,1:T(8,128)}) fusion(f32[4096,6,64]{0,2,1:T(8,128)} %bitcast.607, f32[4096,6,130]{0,2,1:T(8,128)} %copy-done.20, f32[4096]{0:T(1024)S(1)} %broadcast_multiply_fusion.1, f32[4096,6,64]{0,2,1:T(8,128)} %get-tuple-element.1013, ...), kind=kLoop, calls=%fused_computation.164 | loop fusion | flops 29884032 | bytes 44092416 | tf_op jit(solution)/shard_map/transpose(jvp())/reduce_sum | solution.py:119
  579.2 20.2 %rev.35 = f32[4096,6,64]{0,2,1:T(8,128)} reverse(f32[4096,6,64]{0,2,1:T(8,128)} %get-tuple-element.1008), dimensions={0} | reverse | bytes 12582912 | tf_op jit(solution)/shard_map/transpose(jvp())/rev | solution.py:113
  599.3 12.5 slice_select_fusion.1
  647.9 77.1 %while.76 = (s32[]{:T(128)}, f32[6,64,64]{2,1,0:T(8,128)S(1)}, f32[16,6,64,64]{3,2,1,0:T(8,128)}, f32[16,6]{1,0:T(8,128)S(1)}, f32[16,6,64,64]{2,3,1,0:T(8,128)}...) while((s32[]{:T(128)}, f32[6,64,64]{2,1,0:T(8,128)S(1)}, ...), condition=%wide.region_28.29_spmd.clone, body=%wide.region_26.28_spmd.clone.sunk | while | flops 172036 | bytes 1081748 | solution.py:81
  753.5 87.2 %while.75 = (s32[]{:T(128)}, f32[6,64,64]{2,1,0:T(8,128)S(1)}, f32[16,6,64,64]{3,2,1,0:T(8,128)}, f32[16,6]{1,0:T(8,128)S(1)}, f32[16,6,64,64]{2,3,1,0:T(8,128)}...) while((s32[]{:T(128)}, f32[6,64,64]{2,1,0:T(8,128)S(1)}, ...), condition=%wide.region_16.17_spmd.clone, body=%wide.region_14.16_spmd.clone.sunk | while | flops 172036 | bytes 1081748 | solution.py:81
  899.2 35.4 %fusion.79 = f32[16,6,256,256]{3,2,1,0:T(8,128)} fusion(f32[16,256,6,64]{1,0,3,2:T(8,128)} %bitcast.598, f32[16,256,6,64]{1,0,3,2:T(8,128)} %bitcast.655), kind=kOutput, calls=%fused_computation.138 | convolution fusion | flops 4831838208 | bytes 37748736 | tf_op jit(solution)/shard_map/transpose(jvp(jvp()))/checkpoint/bhij,bjhp->bihp/dot_general | solution.py:54
  934.6 66.3 %fusion.35 = (f32[16,6,256]{2,1,0:T(8,128)}, f32[16,6,256]{2,1,0:T(8,128)}, f32[16,6,256]{2,1,0:T(8,128)}, f32[16,256,256]{2,1,0:T(8,128)}, f32[16,256,256]{2,1,...) fusion(f32[16,6,256]{2,1,0:T(8,128)S(1)} %bitcast.704, ...), kind=kOutput, calls=%fused_computation.67 | convolution fusion | flops 5018337280 | bytes 55574528 | tf_op jit(solution)/shard_map/transpose(jvp(jvp()))/checkpoint/bhij,bjhp->bihp/dot_general | solution.py:54
  1011.2 27.1 %fusion.76 = f32[16,6,8,8,256]{4,3,2,1,0:T(8,128)} fusion(f32[16,256,6,64]{1,3,2,0:T(8,128)S(1)} %copy-done.38, f32[16,256,6]{1,2,0:T(8,128)S(1)} %get-tuple-element.1055, f32[16,6,256]{2,1,0:T(8,128)S(1)} %bitcast.703, f32[16,256,256]{2,1,0:T(8,128)} %fusion.282, f32[16,6,256]{2,1,0:T(8,128)S(1)} %copy-done.76, pred[256,256]{1,0:T(8,128)(4,1)S(1)} %copy-done.80, ...), kind=kOutput, calls=%fused_computation.134 | convolution fusion | flops 4866441216 | bytes 23429120 | tf_op jit(solution)/shard_map/transpose(jvp(jvp()))/checkpoint/bhij,bjhp->bihp/dot_general | solution.py:54
  1065.7 26.4 %fusion.77 = f32[16,6,8,8,256]{4,3,2,1,0:T(8,128)} fusion(f32[16,256,6,64]{1,3,2,0:T(8,128)S(1)} %bitcast.682, f32[16,256,6]{1,2,0:T(8,128)S(1)} %get-tuple-element.1053, f32[16,6,256]{2,1,0:T(8,128)S(1)} %bitcast.705, f32[16,256,256]{2,1,0:T(8,128)S(1)} %copy-done.41, f32[16,6,256]{2,1,0:T(8,128)S(1)} %copy-done.75, pred[256,256]{1,0:T(8,128)(4,1)S(1)} %copy-done.80, ...), kind=kOutput, calls=%fused_computation.136 | convolution fusion | flops 4866441216 | bytes 23429120 | tf_op jit(solution)/shard_map/transpose(jvp(jvp()))/checkpoint/bhij,bjhp->bihp/dot_general | solution.py:54
  1107.5 20.0 %rev.37 = f32[4096,6,64]{0,2,1:T(8,128)} reverse(f32[4096,6,64]{0,2,1:T(8,128)} %bitcast.665), dimensions={0} | reverse | bytes 12582912 | tf_op jit(solution)/shard_map/transpose(jvp())/rev | solution.py:115
  1127.5 14.9 reduce-window.50
  1142.8 14.9 reduce-window.56
  1186.3 19.2 %multiply_reduce_fusion.23 = (f32[256]{0:T(256)}, f32[256]{0:T(256)}, f32[256]{0:T(256)}, f32[256]{0:T(256)}, f32[256]{0:T(256)}, /*index=5*/f32[256]{0:T(256)}, f32[256]{0:T(256)}, f32[4096,256]{1,0:T(8,128)S(1)}) fusion(f32[4096,256]{1,0:T(8,128)} %copy-done.13, pred[4096]{0:T(1024)(128)(4,1)S(1)} %copy-done.58, pred[4096]{0:T(1024)(128)(4,1)S(1)} %copy-done.64, ...), kind=kLoop, calls=%fused_computation.229 | loop fusion | flops 34601216 | bytes 16813056 | tf_op jit(solution)/shard_map/transpose(jvp())/reduce_sum | solution.py:36
  1225.6 13.6 add_add_fusion
  1239.2 16.2 multiply_reduce_fusion.13
  1255.5 16.6 multiply_select_fusion.8
  1272.1 20.5 %pad_add_fusion = f32[4096,384]{0,1:T(8,128)} fusion(f32[4096,384]{0,1:T(8,128)} %get-tuple-element.1031, f32[4096,384]{0,1:T(8,128)} %get-tuple-element.1032, f32[4096,384]{0,1:T(8,128)} %get-tuple-element.1033, f32[4096,384]{0,1:T(8,128)} %get-tuple-element.1034, f32[4096,384]{0,1:T(8,128)} %get-tuple-element.1035, f32[4096,384]{0,1:T(8,128)} %get-tuple-element.1036, ...), kind=kLoop, calls=%fused_computation.121 | loop fusion | flops 9437184 | bytes 50331648 | tf_op jit(solution)/shard_map/transpose(jvp())/add_any | solution.py:34
  1364.7 152.3 %all-reduce.55 = (bf16[6,768,194]{1,2,0:T(8,128)(2,1)S(1)}, f32[6,10,64]{2,0,1:T(8,128)}) all-reduce(f32[6,768,194]{1,2,0:T(8,128)} %pad_maximum_fusion, f32[6,10,64]{2,0,1:T(8,128)S(1)} %fusion.243), channel_id=1, replica_groups=mesh['dp'=8,'mp'=4] {'dp'}, use_global_device_ids=true, to_apply=%region_44.45 | all-reduce | flops 897792 | bytes 5394432 | tf_op jit(solution)/shard_map/psum | solution.py:250
  1517.0 27.8 %fusion.117 = f32[1,768,194]{0,1,2:T(8,128)} fusion(bf16[6,768,194]{1,2,0:T(8,128)(2,1)S(1)} %get-tuple-element.986, s32[]{:T(128)S(6)} %axis_index.25, s32[24]{0:T(128)S(1)} %copy-done.135, s32[]{:T(128)S(6)} %select_n.236), kind=kOutput, calls=%fused_computation.213 | convolution fusion | flops 1787910 | bytes 2383976 | tf_op jit(solution)/shard_map/dot_general | solution.py:258
  1544.8 44.0 %copy.735 = f32[1,768,194]{1,2,0:T(8,128)S(1)} copy(f32[1,768,194]{0,1,2:T(8,128)} %fusion.117) | data formatting | bytes 1191936 | tf_op jit(solution)/shard_map/dot_general | solution.py:258
  1605.8 38.6 %psum.47 = f32[10,256]{1,0:T(8,128)S(1)} all-reduce(f32[10,256]{1,0:T(8,128)S(1)} %pad_maximum_fusion.1), channel_id=1, replica_groups=mesh['dp'=8,'mp'=4] {'dp','mp'}, use_global_device_ids=true, to_apply=%region_65.66 | all-reduce | flops 2560 | bytes 20480 | tf_op jit(solution)/shard_map/psum | solution.py:251
  (1079 shorter events, 785.5 us)
Async XLA Ops:
  7.2 57.7 %all-gather.9.cloned.1.call-start = ((), (), s32[]{:S(2)}) async-start(), calls=%async_computation.9 | async-start | bytes 2764800 | tf_op jit(solution)/shard_map/all_gather | solution.py:162
  9.1 104.5 %all-gather.5.cloned.1.call-start = ((), (), s32[]{:S(2)}) async-start(), calls=%async_computation.3 | async-start | bytes 7864320 | tf_op jit(solution)/shard_map/all_gather | solution.py:173
  15.9 527.9 %all-gather.7.cloned.1.call-start = ((), (), s32[]{:S(2)}) async-start(), calls=%async_computation.5 | async-start | bytes 7864320 | tf_op jit(solution)/shard_map/all_gather | solution.py:200
  16.6 1285.2 %reduce-scatter.8.cloned.1.call-start = ((), (), s32[]{:S(2)}) async-start(), calls=%async_computation.7 | async-start | bytes 5242880 | tf_op jit(solution)/shard_map/reduce_scatter | solution.py:218
  17.6 100.7 %copy-start.118 = (f32[1,256]{1,0:T(1,128)}, f32[1,256]{1,0:T(1,128)S(1)}, u32[]{:S(2)}) copy-start(f32[1,256]{1,0:T(1,128)S(1)} %get-tuple-element.1077) | copy-start | bytes 3076
  17.6 100.7 %copy-start.120 = (f32[1,256]{1,0:T(1,128)}, f32[1,256]{1,0:T(1,128)S(1)}, u32[]{:S(2)}) copy-start(f32[1,256]{1,0:T(1,128)S(1)} %get-tuple-element.1078) | copy-start | bytes 3076
  17.6 100.7 %copy-start.122 = (f32[1,256]{1,0:T(1,128)}, f32[1,256]{1,0:T(1,128)S(1)}, u32[]{:S(2)}) copy-start(f32[1,256]{1,0:T(1,128)S(1)} %get-tuple-element.1079) | copy-start | bytes 3076
  17.7 100.7 %copy-start.124 = (f32[1,256]{1,0:T(1,128)}, f32[1,256]{1,0:T(1,128)S(1)}, u32[]{:S(2)}) copy-start(f32[1,256]{1,0:T(1,128)S(1)} %get-tuple-element.1080) | copy-start | bytes 3076
  17.7 100.7 %copy-start.126 = (f32[1,256]{1,0:T(1,128)}, f32[1,256]{1,0:T(1,128)S(1)}, u32[]{:S(2)}) copy-start(f32[1,256]{1,0:T(1,128)S(1)} %get-tuple-element.1081) | copy-start | bytes 3076
  17.7 100.7 %copy-start.128 = (f32[1,256]{1,0:T(1,128)}, f32[1,256]{1,0:T(1,128)S(1)}, u32[]{:S(2)}) copy-start(f32[1,256]{1,0:T(1,128)S(1)} %get-tuple-element.1082) | copy-start | bytes 3076
  17.7 100.7 %copy-start.130 = (f32[1,256]{1,0:T(1,128)}, f32[1,256]{1,0:T(1,128)S(1)}, u32[]{:S(2)}) copy-start(f32[1,256]{1,0:T(1,128)S(1)} %get-tuple-element.1083) | copy-start | bytes 3076
  17.7 139.0 %copy-start.90 = (f32[6,2]{1,0:T(8,128)}, f32[6,2]{1,0:T(8,128)S(1)}, u32[]{:S(2)}) copy-start(f32[6,2]{1,0:T(8,128)S(1)} %slice_bitcast_fusion.4) | copy-start | bytes 148
  17.7 507.5 %copy-start.94 = (f32[6,64]{1,0:T(8,128)}, f32[6,64]{1,0:T(8,128)S(1)}, u32[]{:S(2)}) copy-start(f32[6,64]{1,0:T(8,128)S(1)} %get-tuple-element.1067) | copy-start | bytes 4612
  17.7 544.0 %copy-start.92 = (f32[6,64]{1,0:T(8,128)}, f32[6,64]{1,0:T(8,128)S(1)}, u32[]{:S(2)}) copy-start(f32[6,64]{1,0:T(8,128)S(1)} %get-tuple-element.1066) | copy-start | bytes 4612
  19.5 153.3 %copy-start.53 = (pred[4096]{0:T(1024)(128)(4,1)}, pred[4096]{0:T(1024)(128)(4,1)S(1)}, u32[]{:S(2)}) copy-start(pred[4096]{0:T(1024)(128)(4,1)S(1)} %get-tuple-element.1095) | copy-start | bytes 12292
  19.5 153.3 %copy-start.55 = (pred[4096]{0:T(1024)(128)(4,1)}, pred[4096]{0:T(1024)(128)(4,1)S(1)}, u32[]{:S(2)}) copy-start(pred[4096]{0:T(1024)(128)(4,1)S(1)} %get-tuple-element.1096) | copy-start | bytes 12292
  19.7 153.1 %copy-start.57 = (pred[4096]{0:T(1024)(128)(4,1)}, pred[4096]{0:T(1024)(128)(4,1)S(1)}, u32[]{:S(2)}) copy-start(pred[4096]{0:T(1024)(128)(4,1)S(1)} %get-tuple-element.1093) | copy-start | bytes 12292
  19.8 153.1 %copy-start.59 = (pred[4096]{0:T(1024)(128)(4,1)}, pred[4096]{0:T(1024)(128)(4,1)S(1)}, u32[]{:S(2)}) copy-start(pred[4096]{0:T(1024)(128)(4,1)S(1)} %get-tuple-element.1094) | copy-start | bytes 12292
  20.0 152.9 %copy-start.61 = (pred[4096]{0:T(1024)(128)(4,1)}, pred[4096]{0:T(1024)(128)(4,1)S(1)}, u32[]{:S(2)}) copy-start(pred[4096]{0:T(1024)(128)(4,1)S(1)} %get-tuple-element.1097) | copy-start | bytes 12292
  20.0 152.9 %copy-start.63 = (pred[4096]{0:T(1024)(128)(4,1)}, pred[4096]{0:T(1024)(128)(4,1)S(1)}, u32[]{:S(2)}) copy-start(pred[4096]{0:T(1024)(128)(4,1)S(1)} %get-tuple-element.1098) | copy-start | bytes 12292
  20.2 152.7 %copy-start.65 = (pred[4096]{0:T(1024)(128)(4,1)}, pred[4096]{0:T(1024)(128)(4,1)S(1)}, u32[]{:S(2)}) copy-start(pred[4096]{0:T(1024)(128)(4,1)S(1)} %get-tuple-element.1100) | copy-start | bytes 12292
  21.0 152.0 %copy-start.96 = (f32[384]{0:T(512)}, f32[384]{0:T(512)S(1)}, u32[]{:S(2)}) copy-start(f32[384]{0:T(512)S(1)} %mul.978) | copy-start | bytes 4612
  21.0 151.9 %copy-start.98 = (f32[384]{0:T(512)}, f32[384]{0:T(512)S(1)}, u32[]{:S(2)}) copy-start(f32[384]{0:T(512)S(1)} %mul.996) | copy-start | bytes 4612
  21.1 151.8 %copy-start.100 = (f32[384]{0:T(512)}, f32[384]{0:T(512)S(1)}, u32[]{:S(2)}) copy-start(f32[384]{0:T(512)S(1)} %mul.993) | copy-start | bytes 4612
  21.2 151.8 %copy-start.102 = (f32[384]{0:T(512)}, f32[384]{0:T(512)S(1)}, u32[]{:S(2)}) copy-start(f32[384]{0:T(512)S(1)} %mul.990) | copy-start | bytes 4612
  21.3 151.7 %copy-start.104 = (f32[384]{0:T(512)}, f32[384]{0:T(512)S(1)}, u32[]{:S(2)}) copy-start(f32[384]{0:T(512)S(1)} %mul.987) | copy-start | bytes 4612
  21.4 151.6 %copy-start.106 = (f32[384]{0:T(512)}, f32[384]{0:T(512)S(1)}, u32[]{:S(2)}) copy-start(f32[384]{0:T(512)S(1)} %mul.984) | copy-start | bytes 4612
  21.4 151.6 %copy-start.108 = (f32[384]{0:T(512)}, f32[384]{0:T(512)S(1)}, u32[]{:S(2)}) copy-start(f32[384]{0:T(512)S(1)} %mul.981) | copy-start | bytes 4612
  853.9 147.0 %copy-start.46 = (f32[16,6,256]{2,0,1:T(8,128)}, f32[16,6,256]{2,0,1:T(8,128)S(1)}, u32[]{:S(2)}) copy-start(f32[16,6,256]{2,0,1:T(8,128)S(1)} %copy_bitcast_fusion.4) | copy-start | bytes 294916
  1218.4 378.3 %all-reduce.54.cloned.1.call-start = ((), (), s32[]{:S(2)}) async-start(), calls=%async_computation.8 | async-start | bytes 1572864 | tf_op jit(solution)/shard_map/psum | solution.py:251
  1304.6 296.1 %reduce-scatter.6.cloned.1.call-start = ((), (), s32[]{:S(2)}) async-start(), calls=%async_computation.6 | async-start | bytes 15728640 | tf_op jit(solution)/shard_map/reduce_scatter | solution.py:232
  1317.0 328.1 %reduce-scatter.4.cloned.1.call-start = ((), (), s32[]{:S(2)}) async-start(), calls=%async_computation.4 | async-start | bytes 15728640 | tf_op jit(solution)/shard_map/reduce_scatter | solution.py:193
  (145 other events, 2384.6 us)
Sparse Core Ops, SparseCore 0:
  10.8 54.0 all-gather.8
  67.0 46.5 all-gather.4
  115.2 46.3 all-gather.6
  1218.5 46.0 reduce-scatter.7
  1304.7 134.0 all-reduce.53
  1441.2 99.2 reduce-scatter.5
  1543.1 99.9 reduce-scatter.3
where the time goes:
time: 1680 us; the launch traced here: 1660 us
  matrix products  457 us (27%)
  local copies, waits for them, and re-layouts  456 us (27%)
  other arithmetic  428 us (25%)
  blocking collectives  210 us (12%)
  waiting for transfers between devices  85.2 us (5%)
  between operations  18.4 us (1%)
    dot_general x6, matrix products, within_blocks(): jnp.einsum('bhij,bjhp->bihp', weights, values_blk, precision=PRECISE)  219 us
    psum x1, blocking collectives, local(): block_total, params_total = lax.psum((block_grad, params_grad), 'dp')  152 us
    dynamic_slice x192, local copies, waits for them, and re-layouts, state_mix(): lax.scan(carry_state, initial, (local_state, log_decay[:, :, -1], keep_fl...  105 us
    dynamic_update_slice x64, other arithmetic, state_mix(): lax.scan(carry_state, initial, (local_state, log_decay[:, :, -1], keep_fl...  65.3 us
    dot_general x6, matrix products, within_blocks(): jnp.einsum('bjn,bhj,bjhp->bhnp', b_blk, tail_decay, values_blk, precision...  61.1 us
    reduce_sum x32, other arithmetic, carry_state(): new_state = entering * jnp.exp(total_decay)[:, None, None] + local_state  54.8 us
    unnamed x347, local copies, waits for them, and re-layouts  52.1 us
    dot_general x8, matrix products, within_blocks(): scores = jnp.einsum('bin,bjn->bij', c_blk, b_blk, precision=PRECISE)  47.9 us
  transfers between devices with their start and end apart: 7, of which 2 were waited for; matrix products, arithmetic and copies ran while one was open for 40% of the time, Pallas kernels for 0%

commit v1 on v0

v1 whole, which is shorter than its diff:
```python
import jax
import jax.numpy as jnp
from jax import lax
from jax.experimental import pallas as pl
from jax.experimental.pallas import tpu as pltpu
from jax.sharding import PartitionSpec as P

D = 768
H = 24
PS = 64
NS = 64
K = 7
STEP = 3
CH = H * PS
BL = 128
GH = 8
NG = H // GH
WV = 80
PAD = 128
HALO = 8
NORM_EPS = 1e-05
BETA_ONE = 0.5
BETA_TWO = 0.5
ADAM_EPS = 1e-08
WEIGHT_DECAY = 0.1
MATRIX_RATE = 0.04
SMALL_RATE = 0.2
AVERAGE_KEEP = 0.75

f32 = jnp.float32
bf16 = jnp.bfloat16
LQ, RQ, KF, KR, WF, WR, EF, ER, XF, XR, RF, RR = range(12)
KINDS = 12


def params(mb=56):
    return pltpu.CompilerParams(
        dimension_semantics=("arbitrary",), vmem_limit_bytes=mb * 1024 * 1024
    )


def cost(micros):
    return pl.CostEstimate(flops=0, transcendentals=0, bytes_accessed=micros * 1_000_000)


def nt(a, b, precision=None):
    return lax.dot_general(
        a, b, (((1,), (1,)), ((), ())), preferred_element_type=f32, precision=precision
    )


def nn(a, b, precision=None):
    return lax.dot_general(
        a, b, (((1,), (0,)), ((), ())), preferred_element_type=f32, precision=precision
    )


def tn(a, b):
    return lax.dot_general(a, b, (((0,), (0,)), ((), ())), preferred_element_type=f32)


def sigmoid(v):
    return 1.0 / (1.0 + jnp.exp(-v))


def lane_first(shape):
    return lax.broadcasted_iota(jnp.int32, shape, len(shape) - 1) < NS


def conv_taps(signal, taps, sign):
    ext = signal.shape[1]
    total = None
    for k in range(K):
        shift = (sign * (k - K // 2)) % ext
        moved = signal if shift == 0 else pltpu.roll(signal, shift, axis=1)
        term = moved * taps[:, k : k + 1]
        total = term if total is None else total + term
    return total


def causal_masks():
    row = lax.broadcasted_iota(jnp.int32, (BL, BL), 0)
    col = lax.broadcasted_iota(jnp.int32, (BL, BL), 1)
    return row < col, row > col


def stacked_keys(a, b):
    zero = jnp.zeros_like(a)
    return jnp.concatenate(
        [jnp.concatenate([a, zero], axis=1), jnp.concatenate([zero, b], axis=1)], axis=0
    )


def key_kernel(nx_ref, w_ref, taps_ref, p_ref, u_ref, k_ref, st_ref):
    tokens = u_ref.shape[1]
    proj = nt(w_ref[...], nx_ref[...])
    pre = conv_taps(proj, taps_ref[...], -1)
    key = pre * sigmoid(pre)
    ext = key.shape[1]
    b_f = key[:NS, :tokens].astype(bf16)
    c_f = pltpu.roll(key[NS : 2 * NS], 1, axis=1)[:, :tokens].astype(bf16)
    b_r = key[2 * NS : 3 * NS, :tokens].astype(bf16)
    c_r = pltpu.roll(key[3 * NS :], ext - 1, axis=1)[:, :tokens].astype(bf16)
    p_ref[...] = proj
    u_ref[...] = pre[:, :tokens]
    k_ref[...] = jnp.concatenate([b_f, c_f, b_r, c_r], axis=0)
    lower, upper = causal_masks()
    for blk in range(tokens // BL):
        part = slice(blk * BL, (blk + 1) * BL)
        s_f = tn(b_f[:, part], c_f[:, part])
        s_r = tn(b_r[:, part], c_r[:, part])
        st_ref[blk] = jnp.where(lower, s_f, jnp.where(upper, s_r, 0.0))


def key_stage(nx, key_low, taps, tokens):
    ext = nx.shape[0]
    blocks = tokens // BL
    return pl.pallas_call(
        key_kernel,
        out_shape=(
            jax.ShapeDtypeStruct((4 * NS, ext), f32),
            jax.ShapeDtypeStruct((4 * NS, tokens), f32),
            jax.ShapeDtypeStruct((4 * NS, tokens), bf16),
            jax.ShapeDtypeStruct((blocks, BL, BL), f32),
        ),
        compiler_params=pltpu.CompilerParams(vmem_limit_bytes=56 * 1024 * 1024),
        cost_estimate=cost(6),
        name="key_stage",
    )(nx, key_low, taps)


def value_kernel(
    nx_ref, wv_ref, taps_ref, bias_ref, k4_ref, tri_ref,
    v_ref, u_ref, s_ref, rows_ref, tot_ref, sblk_ref, sdev_ref, tdev_ref,
    p_scr, lhs_scr,
):
    tokens = v_ref.shape[1]
    blocks = tokens // BL
    p_scr[...] = nt(wv_ref[...].reshape(GH * WV, D), nx_ref[...])
    for h in range(GH):
        for c in range(PS // 16):
            src = h * WV + c * 16
            dst = h * PS + c * 16
            signal = p_scr[src : src + 16, :]
            pre = conv_taps(signal, taps_ref[dst : dst + 16, :], -1)[:, :tokens]
            s_ref[dst : dst + 16, :] = signal.astype(bf16)
            u_ref[dst : dst + 16, :] = pre.astype(bf16)
            v_ref[dst : dst + 16, :] = (pre * sigmoid(pre)).astype(bf16)
    x_f = jnp.concatenate(
        [p_scr[h * WV + PS : h * WV + PS + 1, :tokens] for h in range(GH)], axis=0
    )
    x_r = jnp.concatenate(
        [p_scr[h * WV + PS + 1 : h * WV + PS + 2, :tokens] for h in range(GH)], axis=0
    )
    x_f = x_f + bias_ref[:, 0:1]
    x_r = x_r + bias_ref[:, 1:2]
    rate_f = jnp.maximum(x_f, 0.0) + jnp.log1p(jnp.exp(-jnp.abs(x_f)))
    rate_r = jnp.maximum(x_r, 0.0) + jnp.log1p(jnp.exp(-jnp.abs(x_r)))
    rows_ref[XF] = x_f
    rows_ref[XR] = x_r
    rows_ref[RF] = rate_f
    rows_ref[RR] = rate_r
    cuts = [slice(b * BL, (b + 1) * BL) for b in range(blocks)]
    stack = jnp.concatenate([rate_f[:, c] for c in cuts] + [rate_r[:, c] for c in cuts], axis=0)
    sums = -nn(stack, tri_ref[...], lax.Precision.HIGHEST)
    first = lane_first((GH, BL))
    cum_r = jnp.zeros((GH, BL), f32)
    cum_f = jnp.zeros((GH, BL), f32)
    state = jnp.zeros((GH * PS, BL), f32)
    for b in range(blocks):
        l_f = sums[b * GH : (b + 1) * GH]
        l_r = sums[(blocks + b) * GH : (blocks + b + 1) * GH]
        r_f = rate_f[:, cuts[b]]
        r_r = rate_r[:, cuts[b]]
        end_f = jnp.broadcast_to(l_f[:, BL - 1 : BL], (GH, BL))
        end_r = jnp.broadcast_to(l_r[:, BL - 1 : BL], (GH, BL))
        w_f = jnp.exp(end_f - l_f) * r_f
        w_r = jnp.exp(l_r + r_r) * r_r
        rows_ref[LQ, :, cuts[b]] = l_f + r_f
        rows_ref[RQ, :, cuts[b]] = -l_r
        rows_ref[KF, :, cuts[b]] = l_f - jnp.log(r_f)
        rows_ref[KR, :, cuts[b]] = -(l_r + r_r + jnp.log(r_r))
        rows_ref[WF, :, cuts[b]] = w_f
        rows_ref[WR, :, cuts[b]] = w_r
        rows_ref[EF, :, cuts[b]] = jnp.exp(l_f + r_f)
        rows_ref[ER, :, cuts[b]] = jnp.exp(end_r - l_r)
        tot_ref[b] = jnp.where(first, end_f, end_r)
        for h in range(GH):
            span = slice(h * PS, (h + 1) * PS)
            vals = v_ref[span, cuts[b]].astype(f32)
            lhs_scr[span, :BL] = (vals * w_f[h : h + 1]).astype(bf16)
            lhs_scr[span, BL:] = (vals * w_r[h : h + 1]).astype(bf16)
        keys = stacked_keys(k4_ref[:NS, cuts[b]], k4_ref[2 * NS : 3 * NS, cuts[b]])
        local_state = nt(lhs_scr[...], keys)
        sblk_ref[b] = local_state
        keep = jnp.where(first, jnp.exp(end_f), 1.0)
        gain = jnp.where(first, 1.0, jnp.exp(cum_r))
        state = jnp.concatenate(
            [
                state[h * PS : (h + 1) * PS] * keep[h : h + 1]
                + local_state[h * PS : (h + 1) * PS] * gain[h : h + 1]
                for h in range(GH)
            ],
            axis=0,
        )
        cum_f = cum_f + end_f
        cum_r = cum_r + end_r
    sdev_ref[...] = state.astype(bf16)
    tdev_ref[...] = jnp.where(first, cum_f, cum_r)


def value_stage(nx, wv, taps, bias, k4, tri, tokens):
    ext = nx.shape[0]
    blocks = tokens // BL
    rows = GH * PS
    return pl.pallas_call(
        value_kernel,
        grid=(NG,),
        in_specs=[
            pl.BlockSpec((ext, D), lambda g: (0, 0), pipeline_mode=pl.Buffered(1)),
            pl.BlockSpec((GH, WV, D), lambda g: (g, 0, 0)),
            pl.BlockSpec((rows, 8), lambda g: (g, 0)),
            pl.BlockSpec((GH, 2), lambda g: (g, 0)),
            pl.BlockSpec((4 * NS, tokens), lambda g: (0, 0)),
            pl.BlockSpec((BL, BL), lambda g: (0, 0)),
        ],
        out_specs=[
            pl.BlockSpec((rows, tokens), lambda g: (g, 0)),
            pl.BlockSpec((rows, tokens), lambda g: (g, 0)),
            pl.BlockSpec((rows, ext), lambda g: (g, 0)),
            pl.BlockSpec((KINDS, GH, tokens), lambda g: (0, g, 0)),
            pl.BlockSpec((blocks, GH, BL), lambda g: (0, g, 0)),
            pl.BlockSpec((blocks, rows, BL), lambda g: (0, g, 0)),
            pl.BlockSpec((rows, BL), lambda g: (g, 0)),
            pl.BlockSpec((GH, BL), lambda g: (g, 0)),
        ],
        out_shape=(
            jax.ShapeDtypeStruct((CH, tokens), bf16),
            jax.ShapeDtypeStruct((CH, tokens), bf16),
            jax.ShapeDtypeStruct((CH, ext), bf16),
            jax.ShapeDtypeStruct((KINDS, H, tokens), f32),
            jax.ShapeDtypeStruct((blocks, H, BL), f32),
            jax.ShapeDtypeStruct((blocks, CH, BL), f32),
            jax.ShapeDtypeStruct((CH, BL), bf16),
            jax.ShapeDtypeStruct((H, BL), f32),
        ),
        scratch_shapes=[pltpu.VMEM((GH * WV, ext), f32), pltpu.VMEM((rows, 2 * BL), bf16)],
        compiler_params=params(),
        cost_estimate=cost(27),
        name="value_stage",
    )(nx, wv, taps, bias, k4, tri)


def chain_kernel(flip, copies, tokens, twist, meta_ref, sblk_ref, tot_ref, far_ref, *refs):
    states = refs[:copies]
    if flip:
        other_ref, out_ref, dot_ref = refs[copies:]
    else:
        (out_ref,) = refs[copies:]
    blocks = sblk_ref.shape[0]
    per = sblk_ref.shape[1] // PS
    step = pl.program_id(0)
    first = lane_first((1, BL))
    wide = lane_first((PS, BL))
    up_lanes = jnp.logical_not(wide) if flip else wide
    here = meta_ref[0]
    length = meta_ref[1]
    sequence = here * tokens // length
    places = [meta_ref[2 + k] for k in range(copies)]
    same = [(place * tokens // length) == sequence for place in places]
    for i in range(per):
        span = slice(i * PS, (i + 1) * PS)
        head = step * per + i
        totals = []
        for k in range(copies):
            place = twist(k, step) * per + i
            parts = [far_ref[k, pl.ds(part * H + place, 1), :] for part in range(3)]
            totals.append(parts[0] + parts[1] + parts[2])
        entering = jnp.zeros((PS, BL), f32)
        for k in range(copies):
            left = jnp.zeros((1, BL), f32)
            right = jnp.zeros((1, BL), f32)
            for q in range(copies):
                if q != k:
                    between = (places[q] > places[k]) & (places[q] < here)
                    left = left + totals[q] * between.astype(f32)
                    between = (places[q] < places[k]) & (places[q] > here)
                    right = right + totals[q] * between.astype(f32)
            from_left = jnp.exp(left) * (same[k] & (places[k] < here)).astype(f32)
            from_right = jnp.exp(right) * (same[k] & (places[k] > here)).astype(f32)
            if flip:
                weight = jnp.where(first, from_right, from_left)
            else:
                weight = jnp.where(first, from_left, from_right)
            entering = entering + weight * states[k][span, :].astype(f32)
        decay = [jnp.exp(tot_ref[b, pl.ds(head, 1), :]) for b in range(blocks)]
        up = [entering]
        for b in range(blocks):
            up.append(up[-1] * decay[b] + sblk_ref[b, span, :])
        down = entering
        for b in range(blocks, -1, -1):
            if b < blocks:
                down = down * decay[b] + sblk_ref[b, span, :]
            both = jnp.where(up_lanes, up[b], down)
            out_ref[b, span, :] = both.astype(bf16)
            if flip:
                dot_ref[b, pl.ds(head, 1), :] = jnp.sum(
                    both * other_ref[b, span, :].astype(f32), axis=0, keepdims=True
                )


def chain_stage(meta, sblk, tot, far_tot, states, twist, tokens, other=None):
    blocks = sblk.shape[0]
    copies = len(states)
    rows = CH // copies
    flip = other is not None
    in_specs = [
        pl.BlockSpec((blocks, rows, BL), lambda q, meta: (0, q, 0)),
        pl.BlockSpec((blocks, H, BL), lambda q, meta: (0, 0, 0)),
        pl.BlockSpec((copies, 3 * H, BL), lambda q, meta: (0, 0, 0)),
    ]
    for k in range(copies):
        in_specs.append(pl.BlockSpec((rows, BL), lambda q, meta, k=k: (twist(k, q), 0)))
    out_specs = [pl.BlockSpec((blocks + 1, rows, BL), lambda q, meta: (0, q, 0))]
    out_shape = [jax.ShapeDtypeStruct((blocks + 1, CH, BL), bf16)]
    args = [meta, sblk, tot, far_tot, *states]
    if flip:
        in_specs.append(pl.BlockSpec((blocks + 1, rows, BL), lambda q, meta: (0, q, 0)))
        out_specs.append(pl.BlockSpec((blocks + 1, H, BL), lambda q, meta: (0, 0, 0)))
        out_shape.append(jax.ShapeDtypeStruct((blocks + 1, H, BL), f32))
        args.append(other)

    def body(*refs):
        chain_kernel(flip, copies, tokens, twist, *refs)

    return pl.pallas_call(
        body,
        grid_spec=pltpu.PrefetchScalarGridSpec(
            num_scalar_prefetch=1, grid=(copies,), in_specs=in_specs, out_specs=out_specs
        ),
        out_shape=out_shape,
        compiler_params=params(),
        cost_estimate=cost(7),
        name="chain_back" if flip else "chain_stage",
    )(*args)


def pair_blocks(value):
    zero = jnp.zeros((PS, BL), value.dtype)
    return jnp.concatenate(
        [
            jnp.concatenate([value[:PS], zero], axis=1),
            jnp.concatenate([zero, value[PS:]], axis=1),
        ],
        axis=0,
    )


def intra_kernel(v_ref, rows_ref, st_ref, o_ref):
    lower, _ = causal_masks()
    kf_cols = jnp.transpose(rows_ref[KF])
    kr_cols = jnp.transpose(rows_ref[KR])
    for pair in range(H // 2):
        mats = []
        for h in (2 * pair, 2 * pair + 1):
            gap = jnp.where(
                lower,
                rows_ref[LQ, h : h + 1, :] - kf_cols[:, h : h + 1],
                rows_ref[RQ, h : h + 1, :] - kr_cols[:, h : h + 1],
            )
            decay = jnp.exp(jnp.minimum(gap, 80.0))
            mats.append((decay * st_ref[0]).astype(bf16))
        span = slice(pair * 2 * PS, (pair + 1) * 2 * PS)
        out = nn(pair_blocks(v_ref[span, :]), jnp.concatenate(mats, axis=0))
        o_ref[span, :] = out.astype(o_ref.dtype)


def intra_stage(v, rows, scores):
    tokens = v.shape[1]
    return pl.pallas_call(
        intra_kernel,
        grid=(tokens // BL,),
        in_specs=[
            pl.BlockSpec((CH, BL), lambda b: (0, b)),
            pl.BlockSpec((KINDS, H, BL), lambda b: (0, 0, b)),
            pl.BlockSpec((1, BL, BL), lambda b: (b, 0, 0)),
        ],
        out_specs=pl.BlockSpec((CH, BL), lambda b: (0, b)),
        out_shape=jax.ShapeDtypeStruct((CH, tokens), bf16),
        compiler_params=params(),
        cost_estimate=cost(12),
        name="intra_stage",
    )(v, rows, scores)


def token_kernel(
    oi_ref, v_ref, sa_ref, sb_ref, k4_ref, rows_ref, tot_ref, wg_ref, wo_ref,
    nx_ref, hid_ref, go_ref, cols_ref,
    ho_ref, r_ref, dg_ref, do_ref, dsblk_ref, dsdev_ref, rc_ref, small_ref,
    cf_scr, cr_scr, g_scr, dres_scr, mix_scr, gated_scr, lhs_scr, gain_scr, diag_scr,
    dev_scr, cum_scr,
):
    step = pl.program_id(0)
    last = pl.num_programs(0) - 1

    @pl.when(step == 0)
    def _():
        gain_scr[...] = jnp.zeros_like(gain_scr)
        diag_scr[...] = jnp.zeros_like(diag_scr)
        dev_scr[...] = jnp.zeros_like(dev_scr)
        cum_scr[...] = jnp.zeros_like(cum_scr)

    c_f = k4_ref[NS : 2 * NS, :]
    c_r = k4_ref[3 * NS :, :]
    zero = jnp.zeros_like(c_f)
    cf_scr[...] = nn(sa_ref[0], jnp.concatenate([c_f, zero], axis=0))
    cr_scr[...] = nn(sb_ref[0], jnp.concatenate([zero, c_r], axis=0))
    g_scr[...] = nt(wg_ref[...], nx_ref[...])
    dres_scr[...] = nt(wo_ref[...], go_ref[...])
    squares = jnp.zeros((8, BL), f32)
    for h in range(H):
        span = slice(h * PS, (h + 1) * PS)
        part_f = cf_scr[span, :] * rows_ref[EF, h : h + 1, :]
        part_r = cr_scr[span, :] * rows_ref[ER, h : h + 1, :]
        cf_scr[span, :] = part_f
        cr_scr[span, :] = part_r
        mix = (
            oi_ref[span, :].astype(f32)
            + part_f
            + part_r
            + cols_ref[span, 1:2] * v_ref[span, :].astype(f32)
        )
        gate = g_scr[span, :]
        gated = mix * (gate * sigmoid(gate))
        mix_scr[span, :] = mix
        gated_scr[span, :] = gated
        squares = squares + jnp.sum((gated * gated).reshape(PS // 8, 8, BL), axis=0)
    scale = lax.rsqrt(jnp.sum(squares, axis=0, keepdims=True) / CH + NORM_EPS)
    cross = jnp.zeros((8, BL), f32)
    for h in range(H):
        span = slice(h * PS, (h + 1) * PS)
        gated = gated_scr[span, :]
        gain = cols_ref[span, 0:1]
        normal = gated * scale
        r_ref[span, :] = (normal * gain).astype(bf16)
        dres = dres_scr[span, :]
        gain_scr[span, :] += dres * normal
        cross = cross + jnp.sum((dres * gain * gated).reshape(PS // 8, 8, BL), axis=0)
    out = tn(r_ref[...], wo_ref[...])
    ho_ref[...] = (hid_ref[...].astype(f32) + out).astype(bf16)
    pull = scale * scale * scale * (jnp.sum(cross, axis=0, keepdims=True) / CH)
    for h in range(H):
        span = slice(h * PS, (h + 1) * PS)
        dgated = scale * (dres_scr[span, :] * cols_ref[span, 0:1]) - gated_scr[span, :] * pull
        gate = g_scr[span, :]
        soft = sigmoid(gate)
        grad_mix = dgated * (gate * soft)
        dg_ref[span, :] = (dgated * mix_scr[span, :] * (soft * (1.0 + gate * (1.0 - soft)))).astype(
            bf16
        )
        diag_scr[span, :] += grad_mix * v_ref[span, :].astype(f32)
        do_ref[span, :] = grad_mix.astype(bf16)
        rc_ref[0, h : h + 1, :] = jnp.sum(grad_mix * cf_scr[span, :], axis=0, keepdims=True)
        rc_ref[1, h : h + 1, :] = jnp.sum(grad_mix * cr_scr[span, :], axis=0, keepdims=True)
        lhs_scr[span, :BL] = (grad_mix * rows_ref[EF, h : h + 1, :]).astype(bf16)
        lhs_scr[span, BL:] = (grad_mix * rows_ref[ER, h : h + 1, :]).astype(bf16)
    dstate = nt(lhs_scr[...], stacked_keys(c_f, c_r))
    dsblk_ref[0] = dstate
    first = lane_first((H, BL))
    total = tot_ref[0]
    keep = jnp.where(first, 1.0, jnp.exp(total))
    grow = jnp.where(first, jnp.exp(cum_scr[...]), 1.0)
    for h in range(H):
        span = slice(h * PS, (h + 1) * PS)
        dev_scr[span, :] = (
            dev_scr[span, :] * keep[h : h + 1] + dstate[span, :] * grow[h : h + 1]
        )
    cum_scr[...] += total

    @pl.when(step == last)
    def _():
        dsdev_ref[...] = dev_scr[...].astype(bf16)
        ones = jnp.ones((8, BL), f32)
        small_ref[0] = nt(ones, gain_scr[...], lax.Precision.HIGHEST)
        small_ref[1] = nt(ones, diag_scr[...], lax.Precision.HIGHEST)


def token_stage(oi, v, s9, k4, rows, tot, wg, wo, nx, hid, go, cols):
    tokens = v.shape[1]
    blocks = tokens // BL
    whole = dict(pipeline_mode=pl.Buffered(1))
    chan = pl.BlockSpec((CH, BL), lambda b: (0, b))
    toks = pl.BlockSpec((BL, D), lambda b: (b, 0))
    big = pltpu.VMEM((CH, BL), f32)
    return pl.pallas_call(
        token_kernel,
        grid=(blocks,),
        in_specs=[
            chan,
            chan,
            pl.BlockSpec((1, CH, BL), lambda b: (b, 0, 0)),
            pl.BlockSpec((1, CH, BL), lambda b: (b + 1, 0, 0)),
            pl.BlockSpec((4 * NS, BL), lambda b: (0, b)),
            pl.BlockSpec((KINDS, H, BL), lambda b: (0, 0, b)),
            pl.BlockSpec((1, H, BL), lambda b: (b, 0, 0)),
            pl.BlockSpec((CH, D), lambda b: (0, 0), **whole),
            pl.BlockSpec((CH, D), lambda b: (0, 0), **whole),
            toks,
            toks,
            toks,
            pl.BlockSpec((CH, 8), lambda b: (0, 0), **whole),
        ],
        out_specs=[
            toks,
            chan,
            chan,
            chan,
            pl.BlockSpec((1, CH, BL), lambda b: (b, 0, 0)),
            pl.BlockSpec((CH, BL), lambda b: (0, 0)),
            pl.BlockSpec((2, H, BL), lambda b: (0, 0, b)),
            pl.BlockSpec((2, 8, CH), lambda b: (0, 0, 0)),
        ],
        out_shape=(
            jax.ShapeDtypeStruct((tokens, D), bf16),
            jax.ShapeDtypeStruct((CH, tokens), bf16),
            jax.ShapeDtypeStruct((CH, tokens), bf16),
            jax.ShapeDtypeStruct((CH, tokens), bf16),
            jax.ShapeDtypeStruct((blocks, CH, BL), f32),
            jax.ShapeDtypeStruct((CH, BL), bf16),
            jax.ShapeDtypeStruct((2, H, tokens), f32),
            jax.ShapeDtypeStruct((2, 8, CH), f32),
        ),
        scratch_shapes=[big] * 6
        + [pltpu.VMEM((CH, 2 * BL), bf16)]
        + [big] * 3
        + [pltpu.VMEM((H, BL), f32)],
        compiler_params=params(),
        cost_estimate=cost(35),
        name="token_stage",
    )(oi, v, s9, s9, k4, rows, tot, wg, wo, nx, hid, go, cols)


def early_grad_kernel(dg_ref, r_ref, nx_ref, go_ref, wg_ref, out_ref, dn_ref):
    gate = nn(dg_ref[...], nx_ref[...]).astype(bf16)
    outp = nn(r_ref[...], go_ref[...]).astype(bf16)
    out_ref[:, :PS, :] = gate.reshape(GH, PS, D)
    out_ref[:, PS:, :] = outp.reshape(GH, PS, D)
    part = tn(dg_ref[...], wg_ref[...])
    step = pl.program_id(0)

    @pl.when(step == 0)
    def _():
        dn_ref[...] = part

    @pl.when(step > 0)
    def _():
        dn_ref[...] += part


def early_grad_stage(dgate, result, nx, go, wg):
    tokens = dgate.shape[1]
    rows = GH * PS
    return pl.pallas_call(
        early_grad_kernel,
        grid=(NG,),
        in_specs=[
            pl.BlockSpec((rows, tokens), lambda g: (g, 0)),
            pl.BlockSpec((rows, tokens), lambda g: (g, 0)),
            pl.BlockSpec((tokens, D), lambda g: (0, 0)),
            pl.BlockSpec((tokens, D), lambda g: (0, 0)),
            pl.BlockSpec((rows, D), lambda g: (g, 0)),
        ],
        out_specs=[
            pl.BlockSpec((GH, 2 * PS, D), lambda g: (g, 0, 0)),
            pl.BlockSpec((tokens, D), lambda g: (0, 0)),
        ],
        out_shape=(
            jax.ShapeDtypeStruct((H, 2 * PS, D), bf16),
            jax.ShapeDtypeStruct((tokens, D), f32),
        ),
        compiler_params=params(),
        cost_estimate=cost(12),
        name="early_grad",
    )(dgate, result, nx, go, wg)


def intra_back_kernel(
    v_ref, do_ref, rows_ref, st_ref, sa_ref, sb_ref, k4_ref, dv_ref, rc_ref, dk_ref, dos_scr
):
    lower, upper = causal_masks()
    kf_cols = jnp.transpose(rows_ref[KF])
    kr_cols = jnp.transpose(rows_ref[KR])
    score_grad = jnp.zeros((BL, BL), f32)
    for pair in range(H // 2):
        span = slice(pair * 2 * PS, (pair + 1) * 2 * PS)
        grads = pair_blocks(do_ref[span, :])
        mat_grads = tn(v_ref[span, :], grads)
        down = []
        over = []
        for i, h in enumerate((2 * pair, 2 * pair + 1)):
            gap = jnp.where(
                lower,
                rows_ref[LQ, h : h + 1, :] - kf_cols[:, h : h + 1],
                rows_ref[RQ, h : h + 1, :] - kr_cols[:, h : h + 1],
            )
            decay = jnp.exp(jnp.minimum(gap, 80.0))
            mat = decay * st_ref[0]
            term = decay * mat_grads[:, i * BL : (i + 1) * BL]
            score_grad = score_grad + term
            flow = term * st_ref[0]
            flow_f = jnp.where(lower, flow, 0.0)
            row_f = jnp.sum(flow_f, axis=0, keepdims=True)
            row_all = jnp.sum(flow, axis=0, keepdims=True)
            rc_ref[0, h : h + 1, :] = row_f
            rc_ref[1, h : h + 1, :] = row_all - row_f
            down.append(jnp.where(lower, mat, 0.0).astype(bf16))
            over.append(jnp.where(lower, 0.0, mat).astype(bf16))
        dv_f = nt(grads, jnp.concatenate(down, axis=1))
        dv_r = nt(grads, jnp.concatenate(over, axis=1))
        vals = v_ref[span, :].astype(f32)
        for i, h in enumerate((2 * pair, 2 * pair + 1)):
            half = slice(i * PS, (i + 1) * PS)
            rc_ref[2, h : h + 1, :] = jnp.sum(vals[half] * dv_f[half], axis=0, keepdims=True)
            rc_ref[3, h : h + 1, :] = jnp.sum(vals[half] * dv_r[half], axis=0, keepdims=True)
        dv_ref[span, :] = (dv_f + dv_r).astype(dv_ref.dtype)
    grad_f = jnp.where(lower, score_grad, 0.0).astype(bf16)
    grad_r = jnp.where(upper, score_grad, 0.0).astype(bf16)
    b_f = k4_ref[:NS, :]
    c_f = k4_ref[NS : 2 * NS, :]
    b_r = k4_ref[2 * NS : 3 * NS, :]
    c_r = k4_ref[3 * NS :, :]
    for h in range(H):
        span = slice(h * PS, (h + 1) * PS)
        grad = do_ref[span, :].astype(f32)
        dos_scr[span, :BL] = (grad * rows_ref[EF, h : h + 1, :]).astype(bf16)
        dos_scr[span, BL:] = (grad * rows_ref[ER, h : h + 1, :]).astype(bf16)
    cross_f = tn(sa_ref[0], dos_scr[:, :BL])
    cross_r = tn(sb_ref[0], dos_scr[:, BL:])
    dk_ref[:NS, :] = nt(c_f, grad_f)
    dk_ref[NS : 2 * NS, :] = nn(b_f, grad_f) + cross_f[:NS]
    dk_ref[2 * NS : 3 * NS, :] = nt(c_r, grad_r)
    dk_ref[3 * NS :, :] = nn(b_r, grad_r) + cross_r[NS:]


def intra_back_stage(v, do, rows, scores, s9, k4):
    tokens = v.shape[1]
    chan = pl.BlockSpec((CH, BL), lambda b: (0, b))
    return pl.pallas_call(
        intra_back_kernel,
        grid=(tokens // BL,),
        in_specs=[
            chan,
            chan,
            pl.BlockSpec((KINDS, H, BL), lambda b: (0, 0, b)),
            pl.BlockSpec((1, BL, BL), lambda b: (b, 0, 0)),
            pl.BlockSpec((1, CH, BL), lambda b: (b, 0, 0)),
            pl.BlockSpec((1, CH, BL), lambda b: (b + 1, 0, 0)),
            pl.BlockSpec((4 * NS, BL), lambda b: (0, b)),
        ],
        out_specs=[
            chan,
            pl.BlockSpec((4, H, BL), lambda b: (0, 0, b)),
            pl.BlockSpec((4 * NS, BL), lambda b: (0, b)),
        ],
        out_shape=(
            jax.ShapeDtypeStruct((CH, tokens), bf16),
            jax.ShapeDtypeStruct((4, H, tokens), f32),
            jax.ShapeDtypeStruct((4 * NS, tokens), f32),
        ),
        scratch_shapes=[pltpu.VMEM((CH, 2 * BL), bf16)],
        compiler_params=params(),
        cost_estimate=cost(18),
        name="intra_back",
    )(v, do, rows, scores, s9, s9, k4)


def cross_back_kernel(
    dvi_ref, v_ref, do_ref, u_ref, dsa_ref, dsb_ref, k4_ref, rows_ref, rci_ref, rcc_ref,
    xa_ref, xb_ref, dki_ref, cols_ref, after_ref,
    dpre_ref, dx_ref, dk_ref,
    f_scr, r_scr, lhs_scr, c_scr,
):
    b_f = k4_ref[:NS, :]
    b_r = k4_ref[2 * NS : 3 * NS, :]
    zero = jnp.zeros_like(b_f)
    f_scr[...] = nn(dsb_ref[0], jnp.concatenate([b_f, zero], axis=0))
    r_scr[...] = nn(dsa_ref[0], jnp.concatenate([zero, b_r], axis=0))
    for h in range(H):
        span = slice(h * PS, (h + 1) * PS)
        vals = v_ref[span, :].astype(f32)
        w_f = rows_ref[WF, h : h + 1, :]
        w_r = rows_ref[WR, h : h + 1, :]
        dv_f = f_scr[span, :] * w_f
        dv_r = r_scr[span, :] * w_r
        c_scr[0, h : h + 1, :] = jnp.sum(vals * dv_f, axis=0, keepdims=True)
        c_scr[1, h : h + 1, :] = jnp.sum(vals * dv_r, axis=0, keepdims=True)
        lhs_scr[span, :BL] = (vals * w_f).astype(bf16)
        lhs_scr[span, BL:] = (vals * w_r).astype(bf16)
        grad = (
            dvi_ref[span, :].astype(f32)
            + dv_f
            + dv_r
            + cols_ref[span, 1:2] * do_ref[span, :].astype(f32)
        )
        pre = u_ref[span, :].astype(f32)
        soft = sigmoid(pre)
        dpre_ref[span, :] = (grad * (soft * (1.0 + pre * (1.0 - soft)))).astype(dpre_ref.dtype)
    db_f = tn(dsb_ref[0], lhs_scr[:, :BL])
    db_r = tn(dsa_ref[0], lhs_scr[:, BL:])
    dk_ref[...] = dki_ref[...]
    dk_ref[:NS, :] += db_f[:NS]
    dk_ref[2 * NS : 3 * NS, :] += db_r[NS:]
    first = lane_first((H, BL))
    through_f = jnp.sum(jnp.where(first, xb_ref[0], 0.0), axis=1, keepdims=True)
    through_r = jnp.sum(jnp.where(first, 0.0, xa_ref[0]), axis=1, keepdims=True)
    row_f = rci_ref[0] + rcc_ref[0]
    row_r = rci_ref[1] + rcc_ref[1]
    col_f = rci_ref[2] + c_scr[0]
    col_r = rci_ref[3] + c_scr[1]
    after = after_ref[...]
    strict = lax.Precision.HIGHEST
    sum_f = nn(row_f, after, strict) - nn(col_f, after, strict) - col_f + through_f
    sum_r = nt(row_r, after, strict) - nt(col_r, after, strict) - col_r + through_r
    for kind, (total, col, x_kind, r_kind) in enumerate(
        ((sum_f, col_f, XF, RF), (sum_r, col_r, XR, RR))
    ):
        soft = sigmoid(rows_ref[x_kind])
        rate = rows_ref[r_kind]
        live = rate > 0.0
        ratio = jnp.where(live, soft / jnp.where(live, rate, 1.0), 1.0)
        dx_ref[kind] = col * ratio - total * soft


def cross_back_stage(dvi, v, do, u, ds9, k4, rows, rci, rcc, x9, dki, cols, after):
    tokens = v.shape[1]
    chan = pl.BlockSpec((CH, BL), lambda b: (0, b))
    keys = pl.BlockSpec((4 * NS, BL), lambda b: (0, b))
    return pl.pallas_call(
        cross_back_kernel,
        grid=(tokens // BL,),
        in_specs=[
            chan,
            chan,
            chan,
            chan,
            pl.BlockSpec((1, CH, BL), lambda b: (b, 0, 0)),
            pl.BlockSpec((1, CH, BL), lambda b: (b + 1, 0, 0)),
            keys,
            pl.BlockSpec((KINDS, H, BL), lambda b: (0, 0, b)),
            pl.BlockSpec((4, H, BL), lambda b: (0, 0, b)),
            pl.BlockSpec((2, H, BL), lambda b: (0, 0, b)),
            pl.BlockSpec((1, H, BL), lambda b: (b, 0, 0)),
            pl.BlockSpec((1, H, BL), lambda b: (b + 1, 0, 0)),
            keys,
            pl.BlockSpec((CH, 8), lambda b: (0, 0)),
            pl.BlockSpec((BL, BL), lambda b: (0, 0)),
        ],
        out_specs=[chan, pl.BlockSpec((2, H, BL), lambda b: (0, 0, b)), keys],
        out_shape=(
            jax.ShapeDtypeStruct((CH, tokens), bf16),
            jax.ShapeDtypeStruct((2, H, tokens), f32),
            jax.ShapeDtypeStruct((4 * NS, tokens), f32),
        ),
        scratch_shapes=[
            pltpu.VMEM((CH, BL), f32),
            pltpu.VMEM((CH, BL), f32),
            pltpu.VMEM((CH, 2 * BL), bf16),
            pltpu.VMEM((2, H, BL), f32),
        ],
        compiler_params=params(),
        cost_estimate=cost(16),
        name="cross_back",
    )(dvi, v, do, u, ds9, ds9, k4, rows, rci, rcc, x9, x9, dki, cols, after)


def key_pre_kernel(dk_ref, u_ref, edge_ref, out_ref):
    tokens = u_ref.shape[1]
    lane = lax.broadcasted_iota(jnp.int32, (NS, tokens), 1)
    d_cf = pltpu.roll(dk_ref[NS : 2 * NS, :], tokens - 1, axis=1)
    d_cf = jnp.where(lane == tokens - 1, edge_ref[:, 0:1], d_cf)
    d_cr = pltpu.roll(dk_ref[3 * NS :, :], 1, axis=1)
    d_cr = jnp.where(lane == 0, edge_ref[:, 1:2], d_cr)
    grad = jnp.concatenate([dk_ref[:NS, :], d_cf, dk_ref[2 * NS : 3 * NS, :], d_cr], axis=0)
    pre = u_ref[...]
    soft = sigmoid(pre)
    out_ref[...] = grad * (soft * (1.0 + pre * (1.0 - soft)))


def key_pre_stage(dk, u, edge):
    return pl.pallas_call(
        key_pre_kernel,
        out_shape=jax.ShapeDtypeStruct(u.shape, f32),
        compiler_params=pltpu.CompilerParams(vmem_limit_bytes=56 * 1024 * 1024),
        cost_estimate=cost(3),
        name="key_pre",
    )(dk, u, edge)


def conv_back_rows(dpre, taps, signal):
    rows, tokens = dpre.shape
    ext = signal.shape[1]
    wide = jnp.concatenate([dpre, jnp.zeros((rows, ext - tokens), f32)], axis=1)
    total = None
    sums = []
    for k in range(K):
        shift = (k - K // 2) % ext
        moved = wide if shift == 0 else pltpu.roll(wide, shift, axis=1)
        term = moved * taps[:, k : k + 1]
        total = term if total is None else total + term
        prod = moved * signal
        part = prod[:, :BL]
        for b in range(1, ext // BL):
            part = part + prod[:, b * BL : (b + 1) * BL]
        sums.append(part)
    return total, sums


def key_back_kernel(
    meta_ref, dpre_ref, taps_ref, p_ref, nx_ref, w_ref, g_ref, dn_ref, t_ref, low_scr, g_scr
):
    for c in range(4 * NS // 16):
        span = slice(c * 16, (c + 1) * 16)
        total, sums = conv_back_rows(dpre_ref[span, :], taps_ref[span, :], p_ref[span, :])
        low_scr[span, :] = total.astype(bf16)
        for k in range(K):
            t_ref[k, span, :] = sums[k]
    g_scr[...] = nn(low_scr[...], nx_ref[...])
    count, rows, _ = g_ref.shape
    for q in range(count):
        start = pl.multiple_of(meta_ref[2 + q] * rows, 8)
        g_ref[q] = g_scr[pl.ds(start, rows), :].astype(g_ref.dtype)
    dn_ref[...] = tn(low_scr[...], w_ref[...])


def key_back_stage(meta, dpre, taps, proj, nx, key_low):
    ext = nx.shape[0]
    count = meta.shape[0] - 2
    args = (dpre, taps, proj, nx, key_low)
    outs = (
        jax.ShapeDtypeStruct((count, 4 * NS // count, D), bf16),
        jax.ShapeDtypeStruct((ext, D), f32),
        jax.ShapeDtypeStruct((K, 4 * NS, BL), f32),
    )

    def whole(shape):
        return pl.BlockSpec(shape, lambda i, meta: (0,) * len(shape))

    return pl.pallas_call(
        key_back_kernel,
        grid_spec=pltpu.PrefetchScalarGridSpec(
            num_scalar_prefetch=1,
            grid=(1,),
            in_specs=[whole(x.shape) for x in args],
            out_specs=[whole(x.shape) for x in outs],
            scratch_shapes=[pltpu.VMEM((4 * NS, ext), bf16), pltpu.VMEM((4 * NS, D), f32)],
        ),
        out_shape=outs,
        compiler_params=params(),
        cost_estimate=cost(8),
        name="key_back",
    )(meta, *args)


def value_back_kernel(
    dpre_ref, taps_ref, s_ref, dx_ref, nx_ref, wv_ref, g_ref, dn_ref, t_ref, low_scr, tap_scr
):
    tokens = dpre_ref.shape[1]
    ext = s_ref.shape[1]
    step = pl.program_id(0)
    for h in range(GH):
        for c in range(PS // 16):
            src = h * PS + c * 16
            span = slice(src, src + 16)
            total, sums = conv_back_rows(
                dpre_ref[span, :].astype(f32), taps_ref[span, :], s_ref[span, :].astype(f32)
            )
            low_scr[h * WV + c * 16 : h * WV + (c + 1) * 16, :] = total.astype(bf16)
            for k in range(K):
                tap_scr[k, span, :] = sums[k]
        tail = jnp.concatenate(
            [
                dx_ref[0, h : h + 1, :],
                dx_ref[1, h : h + 1, :],
                jnp.zeros((14, tokens), f32),
            ],
            axis=0,
        )
        low_scr[h * WV + PS : (h + 1) * WV, :tokens] = tail.astype(bf16)
        low_scr[h * WV + PS : (h + 1) * WV, tokens:] = jnp.zeros((16, ext - tokens), bf16)
    ones = jnp.ones((8, BL), f32)
    for k in range(K):
        t_ref[0, k : k + 1, :] = nt(ones, tap_scr[k], lax.Precision.HIGHEST)[:1]
    t_ref[0, K : K + 1, :] = jnp.zeros((1, GH * PS), f32)
    g_ref[...] = nn(low_scr[...], nx_ref[...]).reshape(GH, WV, D).astype(g_ref.dtype)
    part = tn(low_scr[...], wv_ref[...].reshape(GH * WV, D))

    @pl.when(step == 0)
    def _():
        dn_ref[...] = part

    @pl.when(step > 0)
    def _():
        dn_ref[...] += part


def value_back_stage(dpre, taps, s, dx, nx, wv):
    tokens = dpre.shape[1]
    ext = nx.shape[0]
    rows = GH * PS
    return pl.pallas_call(
        value_back_kernel,
        grid=(NG,),
        in_specs=[
            pl.BlockSpec((rows, tokens), lambda g: (g, 0)),
            pl.BlockSpec((rows, 8), lambda g: (g, 0)),
            pl.BlockSpec((rows, ext), lambda g: (g, 0)),
            pl.BlockSpec((2, GH, tokens), lambda g: (0, g, 0)),
            pl.BlockSpec((ext, D), lambda g: (0, 0), pipeline_mode=pl.Buffered(1)),
            pl.BlockSpec((GH, WV, D), lambda g: (g, 0, 0)),
        ],
        out_specs=[
            pl.BlockSpec((GH, WV, D), lambda g: (g, 0, 0)),
            pl.BlockSpec((ext, D), lambda g: (0, 0)),
            pl.BlockSpec((1, 8, rows), lambda g: (g, 0, 0)),
        ],
        out_shape=(
            jax.ShapeDtypeStruct((H, WV, D), bf16),
            jax.ShapeDtypeStruct((ext, D), f32),
            jax.ShapeDtypeStruct((NG, 8, rows), f32),
        ),
        scratch_shapes=[
            pltpu.VMEM((GH * WV, ext), bf16),
            pltpu.VMEM((K, rows, BL), f32),
        ],
        compiler_params=params(),
        cost_estimate=cost(27),
        name="value_back",
    )(dpre, taps, s, dx, nx, wv)


def pick(sources, index):
    count = index.shape[0]
    rows, width = sources[0].shape[1:]

    def body(index_ref, *refs):
        out_ref = refs[-1]
        for i in range(count):
            first = 0
            for ref in refs[:-1]:
                n = ref.shape[0]
                local = index_ref[i] - first

                @pl.when((local >= 0) & (local < n))
                def _(ref=ref, local=local, i=i):
                    out_ref[i] = ref[local]

                first += n

    return pl.pallas_call(
        body,
        grid_spec=pltpu.PrefetchScalarGridSpec(
            num_scalar_prefetch=1,
            grid=(1,),
            in_specs=[pl.BlockSpec(x.shape, lambda i, index: (0, 0, 0)) for x in sources],
            out_specs=pl.BlockSpec((count, rows, width), lambda i, index: (0, 0, 0)),
        ),
        out_shape=jax.ShapeDtypeStruct((count, rows, width), sources[0].dtype),
        compiler_params=params(),
        cost_estimate=cost(3),
        name="pick",
    )(index, *sources)


def pick_two_kernel(index_ref, slots_ref, gate_ref, out_ref):
    for h in range(H):
        gate_ref[h] = slots_ref[index_ref[h], :PS, :]
        out_ref[h] = slots_ref[index_ref[h], PS:, :]


def pick_two(slots, index):
    half = jax.ShapeDtypeStruct((H, PS, D), slots.dtype)
    return pl.pallas_call(
        pick_two_kernel,
        grid_spec=pltpu.PrefetchScalarGridSpec(
            num_scalar_prefetch=1,
            grid=(1,),
            in_specs=[pl.BlockSpec(slots.shape, lambda i, index: (0, 0, 0))],
            out_specs=[pl.BlockSpec((H, PS, D), lambda i, index: (0, 0, 0))] * 2,
        ),
        out_shape=(half, half),
        compiler_params=params(),
        cost_estimate=cost(6),
        name="pick_two",
    )(index, slots)


def deal(source, index, live, target=None, extra=None, single=None, joined=0):
    count = index.shape[0]
    rows, width = source.shape[1:]
    more = 0 if extra is None else extra.shape[0] // count
    plan = [index, live] if extra is None else [index, live, target]
    args = [source] if extra is None else [source, extra, single]

    def body(*refs):
        index_ref, live_ref = refs[:2]
        source_ref = refs[len(plan)]
        outs = refs[len(plan) + len(args) :]
        for k in range(count):
            value = source_ref[index_ref[k]]
            value = jnp.where(live_ref[k] > 0, value, jnp.zeros_like(value))
            if joined:
                outs[k // joined][k % joined] = value
            elif more:
                start = pl.multiple_of(refs[2][k] * more, 8)
                last = refs[len(plan) + 1][pl.ds(start, more), :]
                one = refs[len(plan) + 2][pl.ds(refs[2][k], 1), :]
                space = jnp.zeros((16 - more - 1, width), f32)
                last = jnp.concatenate([space, one, last], axis=0)
                outs[k][: rows - 16] = value[: rows - 16]
                outs[k][rows - 16 :] = (value[rows - 16 :].astype(f32) + last).astype(bf16)
            else:
                outs[k][...] = value

    def whole(shape):
        return pl.BlockSpec(shape, lambda i, *plan: (0,) * len(shape))

    if joined:
        shapes = [jax.ShapeDtypeStruct((joined, rows, width), source.dtype)] * (count // joined)
    else:
        shapes = [jax.ShapeDtypeStruct((rows, width), source.dtype)] * count
    return pl.pallas_call(
        body,
        grid_spec=pltpu.PrefetchScalarGridSpec(
            num_scalar_prefetch=len(plan),
            grid=(1,),
            in_specs=[whole(x.shape) for x in args],
            out_specs=[whole(x.shape) for x in shapes],
        ),
        out_shape=shapes,
        compiler_params=params(),
        cost_estimate=cost(3),
        name="deal",
    )(*plan, *args)


def adamw_update(weight, gradient, first_moment, second, average, step_rate):
    first_new = BETA_ONE * first_moment + (1.0 - BETA_ONE) * gradient
    second_new = BETA_TWO * second + (1.0 - BETA_TWO) * gradient * gradient
    correct_one = 1.0 - BETA_ONE**STEP
    correct_two = 1.0 - BETA_TWO**STEP
    normalized = first_new / correct_one / (jnp.sqrt(second_new / correct_two) + ADAM_EPS)
    weight_new = weight - step_rate * (normalized + WEIGHT_DECAY * weight)
    average_new = AVERAGE_KEEP * average + (1.0 - AVERAGE_KEEP) * weight_new
    return (weight_new, first_new, second_new, average_new)


def finish_kernel(
    code_ref, share_ref, w_ref, m_ref, v_ref, a_ref,
    w_out, m_out, v_out, a_out, small_ref, gain_ref, scr,
):
    count, rows, _ = share_ref.shape
    keys = 4 * NS // count
    total = jnp.zeros((1, D), f32)
    for i in range(count):
        share = share_ref[code_ref[i]].astype(f32)
        scr[i * keys : (i + 1) * keys, :] = share[rows - keys :]
        small_ref[i : i + 1, :] = share[rows - keys - 1 : rows - keys]
        total = total + share[:1]
    gain_ref[...] = jnp.broadcast_to(total, (8, D))
    new = adamw_update(
        w_ref[...], jnp.transpose(scr[...]), m_ref[...], v_ref[...], a_ref[...], MATRIX_RATE
    )
    for out, value in zip((w_out, m_out, v_out, a_out), new):
        out[...] = value


def finish_stage(code, shares, weight, first, second, ema):
    count = shares.shape[0]
    args = (shares, weight, first, second, ema)
    outs = [jax.ShapeDtypeStruct(weight.shape, f32)] * 4 + [
        jax.ShapeDtypeStruct((count, D), f32),
        jax.ShapeDtypeStruct((8, D), f32),
    ]

    def whole(shape):
        return pl.BlockSpec(shape, lambda i, code: (0,) * len(shape))

    return pl.pallas_call(
        finish_kernel,
        grid_spec=pltpu.PrefetchScalarGridSpec(
            num_scalar_prefetch=1,
            grid=(1,),
            in_specs=[whole(x.shape) for x in args],
            out_specs=[whole(x.shape) for x in outs],
            scratch_shapes=[pltpu.VMEM((4 * NS, D), f32)],
        ),
        out_shape=outs,
        compiler_params=params(),
        cost_estimate=cost(5),
        name="finish_stage",
    )(code, *args)


def make_local(n_dp, n_mp):
    per = H // n_mp
    direct = n_mp == 4 and n_dp == 8

    def swap(x, axis, size, bit):
        return lax.ppermute(x, axis, [(i, i ^ bit) for i in range(size)])

    def head_rows(mp_index):
        rows = jnp.arange(n_mp, dtype=jnp.int32)
        return jnp.bitwise_xor(rows, mp_index) if direct else rows

    def over_mp(x):
        if direct:
            far = swap(x, "mp", n_mp, 2)
            return [x, swap(x, "mp", n_mp, 1), far, swap(far, "mp", n_mp, 1)]
        copies = lax.all_gather(x, "mp", axis=0)
        return [copies[k] for k in range(n_mp)]

    def gather_dp(part):
        return [part[None]] + [swap(part, "dp", n_dp, k)[None] for k in range(1, n_dp)]

    def pick_own(pieces, owners, dp_index):
        return pick(pieces, jnp.bitwise_xor(owners, dp_index))

    def scatter_mp(grads):
        got = swap(jnp.stack([grads[1], grads[3]]), "mp", n_mp, 1)
        away = (grads[2].astype(f32) + got[1].astype(f32)).astype(bf16)
        mine = grads[0].astype(f32) + got[0].astype(f32)
        return mine + swap(away, "mp", n_mp, 2).astype(f32)

    def deal_targets(owners, targets):
        match = targets[:, None] == owners[None, :]
        return jnp.argmax(match, axis=1).astype(jnp.int32), jnp.any(match, axis=1).astype(jnp.int32)

    def gather_all(x, mp_index, dp_index):
        both = x[None]
        for axis, size, bit in (
            ("dp", n_dp, 2), ("dp", n_dp, 4), ("dp", n_dp, 1), ("mp", n_mp, 2), ("mp", n_mp, 1)
        ):
            both = jnp.concatenate([both, swap(both, axis, size, bit)], axis=0)
        far = jnp.bitwise_xor(jnp.arange(n_mp, dtype=jnp.int32), mp_index)[:, None]
        off = jnp.bitwise_xor(jnp.arange(n_dp, dtype=jnp.int32), dp_index)[None, :]
        code = ((off >> 1) & 3) + 4 * (off & 1) + 8 * (far >> 1) + 16 * (far & 1)
        return both, code.reshape(-1)

    def local(
        hidden_in, out_grad, seq_len, owner_list,
        block_master, block_first, block_second, block_ema,
        head_small, head_first, head_second, head_ema,
        bc_weight, bc_first, bc_second, bc_ema,
        shared_small, shared_first, shared_second, shared_ema,
    ):
        tokens = hidden_in.shape[0]
        mp_index = lax.axis_index("mp")
        dp_index = lax.axis_index("dp")
        owners = lax.dynamic_slice_in_dim(owner_list, mp_index * per, per)
        order = head_rows(mp_index)
        bounds = (mp_index + jnp.arange(2, dtype=jnp.int32)) * tokens % seq_len == 0
        starts = bounds[:1].reshape(1, 1)
        ends = bounds[1:].reshape(1, 1)
        meta = jnp.concatenate([mp_index.reshape(1), seq_len, order]).astype(jnp.int32)
        nexts = [(i, i + 1) for i in range(n_mp - 1)]
        prevs = [(i + 1, i) for i in range(n_mp - 1)]

        slot_t = jnp.transpose(block_master[0, 0]).astype(bf16)
        part_v = jnp.concatenate(
            [slot_t[PS : 2 * PS + 2], jnp.zeros((WV - PS - 2, D), bf16)], axis=0
        )
        part_go = jnp.concatenate([slot_t[:PS], slot_t[2 * PS + 2 :]], axis=0)
        if direct:
            pieces_v = gather_dp(part_v)
            mine_v = pick_own(pieces_v, owners, dp_index)
            far_v = swap(mine_v, "mp", n_mp, 2)
            near_v = swap(mine_v, "mp", n_mp, 1)
            slots = lax.all_gather(part_go, ("mp", "dp"), axis=0)
            rows_of = jnp.repeat(order, per)
            heads_of = rows_of * per + jnp.arange(H, dtype=jnp.int32) % per
            wg, wo = pick_two(slots, rows_of * n_dp + jnp.take(owner_list, heads_of))
        else:
            mine_v = pick([lax.all_gather(part_v, "dp", axis=0)], owners)
            wv = jnp.concatenate(over_mp(mine_v), axis=0)
            mine_go = pick([lax.all_gather(part_go, "dp", axis=0)], owners)
            all_go = over_mp(mine_go)
            wg = jnp.concatenate([x[:, :PS] for x in all_go], axis=0)
            wo = jnp.concatenate([x[:, PS:] for x in all_go], axis=0)
        wg = wg.reshape(CH, D)
        wo = wo.reshape(CH, D)

        hidden = hidden_in.astype(f32)
        gain_in = shared_small[K:].reshape(D)
        scale_in = lax.rsqrt(jnp.mean(hidden * hidden, axis=1, keepdims=True) + NORM_EPS)
        normed = (hidden * scale_in * gain_in).astype(bf16)
        from_left = lax.ppermute(normed[-HALO:], "mp", nexts)
        from_right = lax.ppermute(normed[:HALO], "mp", prevs)
        from_left = jnp.where(starts, jnp.zeros_like(from_left), from_left)
        from_right = jnp.where(ends, jnp.zeros_like(from_right), from_right)
        nx = jnp.concatenate(
            [normed, from_right, jnp.zeros((PAD - 2 * HALO, D), bf16), from_left], axis=0
        )

        heads = jnp.concatenate(over_mp(head_small), axis=0)
        taps_v = jnp.transpose(heads[:, 1 : 1 + K, :], (0, 2, 1)).reshape(CH, K)
        taps_v = jnp.pad(taps_v, ((0, 0), (0, 1)))
        cols = jnp.stack([heads[:, 0].reshape(CH), heads[:, K + 1].reshape(CH)], axis=1)
        cols = jnp.pad(cols, ((0, 0), (0, 6)))
        bias = heads[:, K + 2, :2]
        key_low = jnp.transpose(bc_weight).astype(bf16)
        taps_k = jnp.pad(jnp.transpose(shared_small[:K]), ((0, 0), (0, 1)))
        ids = jnp.arange(BL)
        tri = (ids[:, None] <= ids[None, :]).astype(f32)
        after = (ids[:, None] > ids[None, :]).astype(f32)

        key_proj, key_u, k4, scores = key_stage(nx, key_low, taps_k, tokens)
        if direct:
            far_v, k4 = lax.optimization_barrier((far_v, k4))
            wv = jnp.concatenate([mine_v, near_v, far_v, swap(far_v, "mp", n_mp, 1)], axis=0)
        v, u, s, rows, tot, sblk, sdev, tdev = value_stage(
            nx, wv, taps_v, bias, k4, tri, tokens
        )
        tot_hi = lax.reduce_precision(tdev, 8, 7)
        tot_mid = lax.reduce_precision(tdev - tot_hi, 8, 7)
        tot_low = tdev - tot_hi - tot_mid
        message = jnp.concatenate(
            [sdev, tot_hi.astype(bf16), tot_mid.astype(bf16), tot_low.astype(bf16)], axis=0
        )
        def twist(k, q):
            return q ^ k if direct else q

        o_intra = intra_stage(v, rows, scores)
        if direct:
            far = swap(message, "mp", n_mp, 2)
            near = swap(message, "mp", n_mp, 1)
            far, o_intra = lax.optimization_barrier((far, o_intra))
            messages = [message, near, far, swap(far, "mp", n_mp, 1)]
        else:
            messages = over_mp(message)
        far_tot = jnp.stack([x[CH:] for x in messages]).astype(f32)

        (s9,) = chain_stage(meta, sblk, tot, far_tot, messages, twist, tokens)
        hidden_out, result_t, dgate_t, do_t, dsblk, dsdev, rcc, small_mid = token_stage(
            o_intra, v, s9, k4, rows, tot, wg, wo, nx, hidden_in, out_grad, cols
        )
        if direct:
            far_d = swap(dsdev, "mp", n_mp, 2)
            near_d = swap(dsdev, "mp", n_mp, 1)
        grad_go, dn_gate = early_grad_stage(dgate_t, result_t, nx, out_grad, wg)
        grad_go = grad_go.reshape(n_mp, per * 2 * PS, D)
        if direct:
            got = swap(jnp.stack([grad_go[1], grad_go[3]]), "mp", n_mp, 1)
            away = (grad_go[2].astype(f32) + got[1].astype(f32)).astype(bf16)
            far_go = swap(away, "mp", n_mp, 2)
            do_back, away, far_d = lax.optimization_barrier((do_t, away, far_d))
        else:
            do_back = do_t
        dvi, rci, dki = intra_back_stage(v, do_back, rows, scores, s9, k4)
        to_prev = lax.ppermute(dki[NS : 2 * NS, :1].reshape(1, NS), "mp", prevs)
        to_next = lax.ppermute(dki[3 * NS :, tokens - 1 :].reshape(1, NS), "mp", nexts)
        if direct:
            messages = [dsdev, near_d, far_d, swap(far_d, "mp", n_mp, 1)]
        else:
            messages = over_mp(dsdev)
        natural = jnp.arange(n_dp, dtype=jnp.int32)
        if direct:
            far_go, dvi = lax.optimization_barrier((far_go, dvi))
            mine_go = grad_go[0].astype(f32) + got[0].astype(f32) + far_go.astype(f32)
            mine_go = mine_go.astype(bf16)
        else:
            mine_go = lax.psum_scatter(grad_go, "mp", scatter_dimension=0, tiled=True)[0]
        if direct:
            bits = jnp.arange(n_dp, dtype=jnp.int32)
            bits = (bits >> 2) + 4 * ((bits >> 1) & 1) + 2 * (bits & 1)
            keep_go, send_go = deal(
                mine_go.reshape(per, 2 * PS, D),
                *deal_targets(owners, jnp.bitwise_xor(bits, dp_index)),
                joined=n_dp // 2,
            )
            keep_go, dvi = lax.optimization_barrier((keep_go, dvi))
            keep_go = keep_go.astype(f32) + swap(send_go, "dp", n_dp, 1).astype(f32)
        else:
            (dealt,) = deal(
                mine_go.reshape(per, 2 * PS, D), *deal_targets(owners, natural), joined=n_dp
            )
            own_go = lax.psum_scatter(dealt, "dp", scatter_dimension=0, tiled=True)[0]
        ds9, x9 = chain_stage(meta, dsblk, tot, far_tot, messages, twist, tokens, s9)
        dpre, dx, dk = cross_back_stage(
            dvi, v, do_t, u, ds9, k4, rows, rci, rcc, x9, dki, cols, after
        )
        if direct:
            keep_go, dpre, dk = lax.optimization_barrier((keep_go, dpre, dk))
            far_go = swap(keep_go[2:].astype(bf16), "dp", n_dp, 4)
        d_last, d_first = to_prev, to_next
        d_last = jnp.where(ends, 0.0, d_last)
        d_first = jnp.where(starts, 0.0, d_first)
        edge = jnp.transpose(jnp.concatenate([d_last, d_first, jnp.zeros((6, NS), f32)], axis=0))
        dpre_k = key_pre_stage(dk, key_u, edge)
        grad_v, dn_value, tap_v = value_back_stage(dpre, taps_v, s, dx, nx, wv)
        if direct:
            far_go, dpre_k, dn_value = lax.optimization_barrier((far_go, dpre_k, dn_value))
            keep_go = keep_go[:2] + far_go.astype(f32)
            own_go = keep_go[0] + swap(keep_go[1].astype(bf16), "dp", n_dp, 2).astype(f32)
        grad_key, dn_key, tap_key = key_back_stage(meta, dpre_k, taps_k, key_proj, nx, key_low)
        head_grad = jnp.concatenate(
            [
                small_mid[0, 0].reshape(H, 1, PS),
                jnp.transpose(
                    tap_v.reshape(NG, 8, GH, PS)[:, :K], (0, 2, 1, 3)
                ).reshape(H, K, PS),
                small_mid[1, 0].reshape(H, 1, PS),
                jnp.pad(jnp.transpose(jnp.sum(dx, axis=2)), ((0, 0), (0, PS - 2))).reshape(
                    H, 1, PS
                ),
            ],
            axis=1,
        )
        if direct:
            head_grad = jnp.take(head_grad.reshape(n_mp, per, 10, PS), order, axis=0)
        small_grad = jnp.concatenate(
            [head_grad.reshape(-1), jnp.sum(tap_key, axis=2).reshape(-1)]
        )
        count = small_grad.shape[0]

        if direct:
            rows_key = (4 * NS) // (n_mp * n_dp)
            small_rows = jnp.pad(small_grad, (0, n_mp * n_dp * D - count)).reshape(n_mp, n_dp, D)
            small_rows = jnp.take(small_rows, order, axis=0).astype(bf16)
            both = jnp.concatenate([grad_v.reshape(n_mp, per * WV, D), grad_key, small_rows], axis=1)
            mine_v = scatter_mp(both)
            mine_v, own_go = lax.optimization_barrier((mine_v, own_go))
            targets = jnp.bitwise_xor(natural, dp_index)
            dealt = deal(
                mine_v[: per * WV].astype(bf16).reshape(per, WV, D),
                *deal_targets(owners, targets),
                targets,
                mine_v[per * WV : per * WV + n_dp * rows_key],
                mine_v[per * WV + n_dp * rows_key :],
            )
            own_v = dealt[0].astype(f32)
            for k in range(1, n_dp):
                own_v = own_v + swap(dealt[k], "dp", n_dp, k).astype(f32)
        else:
            mine_v = lax.psum_scatter(
                grad_v.reshape(n_mp, per * WV, D), "mp", scatter_dimension=0, tiled=True
            )[0]
            (dealt,) = deal(
                mine_v.reshape(per, WV, D), *deal_targets(owners, natural), joined=n_dp
            )
            own_v = lax.psum_scatter(dealt, "dp", scatter_dimension=0, tiled=True)[0].astype(f32)

        dn_ext = dn_key + dn_value
        halo_l = lax.ppermute(dn_ext[tokens : tokens + HALO], "mp", nexts)
        halo_r = lax.ppermute(dn_ext[-HALO:], "mp", prevs)
        halo_l = jnp.where(starts, 0.0, halo_l)
        halo_r = jnp.where(ends, 0.0, halo_r)
        edges = jnp.concatenate([halo_l, jnp.zeros((tokens - 2 * HALO, D), f32), halo_r], axis=0)
        dnormed = dn_gate + dn_ext[:tokens] + edges
        scaled = dnormed * gain_in
        gain_grad = jnp.sum(dnormed * hidden * scale_in, axis=0)
        cross_in = jnp.sum(scaled * hidden, axis=1, keepdims=True)
        hidden_grad = (
            out_grad.astype(f32) + scale_in * scaled - hidden * scale_in**3 * cross_in / D
        )

        if direct:
            share = jnp.concatenate(
                [jnp.broadcast_to(gain_grad, (15 - rows_key, D)), own_v[WV - rows_key - 1 :]],
                axis=0,
            ).astype(bf16)
            shares, code = gather_all(share, mp_index, dp_index)
            *key_new, small_total, gain_total = finish_stage(
                code, shares, bc_weight, bc_first, bc_second, bc_ema
            )
            small_total = small_total.reshape(-1)[:count]
            gain_total = gain_total[0]
        else:
            key_total, small_total, gain_total = lax.psum(
                (grad_key.reshape(4 * NS, D).astype(f32), small_grad, gain_grad), ("dp", "mp")
            )
            key_new = adamw_update(
                bc_weight, jnp.transpose(key_total), bc_first, bc_second, bc_ema, MATRIX_RATE
            )
        own_go = own_go.astype(f32)
        own_grad = jnp.transpose(
            jnp.concatenate([own_go[:PS], own_v[: PS + 2], own_go[PS:]], axis=0)
        )
        own_grad = lax.optimization_barrier(own_grad)
        is_owner = jnp.any(owners == dp_index)
        previous = (block_master[0, 0], block_first[0, 0], block_second[0, 0], block_ema[0, 0])
        slot_new = adamw_update(
            previous[0], own_grad, previous[1], previous[2], previous[3], MATRIX_RATE
        )
        slot_outs = [
            jnp.where(is_owner, renewed, before)[None, None]
            for renewed, before in zip(slot_new, previous)
        ]
        head_total = lax.dynamic_slice_in_dim(
            small_total[: H * 10 * PS].reshape(H, 10, PS), mp_index * per, per
        )
        head_new = adamw_update(
            head_small, head_total, head_first, head_second, head_ema, SMALL_RATE
        )
        shared_total = jnp.concatenate(
            [
                small_total[H * 10 * PS :].reshape(K, 4 * NS),
                gain_total.reshape(-1, 4 * NS),
            ],
            axis=0,
        )
        shared_new = adamw_update(
            shared_small, shared_total, shared_first, shared_second, shared_ema, SMALL_RATE
        )
        return (hidden_out, hidden_grad, *slot_outs, *head_new, *key_new, *shared_new)

    return local


def solution(mesh):
    rows = P(("dp", "mp"), None)
    slot = P("mp", "dp", None, None)
    head = P("mp", None, None)
    return jax.shard_map(
        make_local(mesh.shape["dp"], mesh.shape["mp"]),
        mesh=mesh,
        in_specs=(rows, rows, P("dp"), P()) + (slot,) * 4 + (head,) * 4 + (P(),) * 8,
        out_specs=(rows, rows) + (slot,) * 4 + (head,) * 4 + (P(),) * 8,
        check_vma=False,
    )
```

time: 1680 us -> 460 us (0.27)
  matrix products: 457 us -> 0 us
  local copies, waits for them, and re-layouts: 456 us -> 33.3 us
  other arithmetic: 428 us -> 45.5 us
  blocking collectives: 210 us -> 0 us
  Pallas kernels: 0 us -> 203 us
  starting transfers between devices: 0.29 us -> 64.5 us
    dot_general x34 -> x0, matrix products: 444 us -> none  [the longest x6 219 us: within_blocks(): jnp.einsum('bhij,bjhp->bihp', weights, values_blk, precision=PRECISE)]
    psum x4 -> x0, blocking collectives: 210 us -> none  [the longest x1 152 us: local(): block_total, params_total = lax.psum((block_grad, params_grad), 'dp')]
    pallas_call x0 -> x17, Pallas kernels: none -> 203 us  [the longest x1 34.6 us: token_stage(): pl.pallas_call(token_kernel, grid=(blocks,), in_specs=[chan, chan, pl.Blo...]
    rev x10 -> x0, local copies, waits for them, and re-layouts: 137 us -> none  [the longest x2 40.3 us: local_mix(): shift_down(state_mix(values[::-1], reverse_b[::-1], reverse_c[::-1], step...]
    reduce_sum x43 -> x3, other arithmetic: 127 us -> 6.07 us  [the longest x1 4.49 us: local(): gain_grad = jnp.sum(dnormed * hidden * scale_in, axis=0)]
    dynamic_slice x192 -> x1, local copies, waits for them, and re-layouts: 105 us -> 0.01 us  [local(): lax.dynamic_slice_in_dim(small_total[:H * 10 * PS].reshape(H, 10, PS), mp...]
    ppermute x0 -> x44, waiting for transfers between devices: none -> 90.6 us  [the longest x38 71.7 us: swap(): return lax.ppermute(x, axis, [(i, i ^ bit) for i in range(size)])]
    all_gather x3 -> x1, waiting for transfers between devices: 84.3 us -> 0.01 us  [local(): slots = lax.all_gather(part_go, ('mp', 'dp'), axis=0)]
  transfers between devices with their start and end apart: 7 -> 45, of which waited for: 2 -> 14; matrix products, arithmetic and copies ran while one was open for 40% -> 12% of each run, Pallas kernels for 0% -> 28%
where the time goes in v1:
time: 460 us; the launch traced here: 453 us
  Pallas kernels  203 us (44%)
  waiting for transfers between devices  90.6 us (20%)
  starting transfers between devices  64.5 us (14%)
  other arithmetic  45.5 us (10%)
  local copies, waits for them, and re-layouts  33.3 us (7%)
  between operations  16.4 us (4%)
    ppermute x38, waiting for transfers between devices, swap(): return lax.ppermute(x, axis, [(i, i ^ bit) for i in range(size)])  71.7 us
    ppermute x38, starting transfers between devices, swap(): return lax.ppermute(x, axis, [(i, i ^ bit) for i in range(size)])  47.9 us
    pallas_call x1, Pallas kernels, token_stage(): pl.pallas_call(token_kernel, grid=(blocks,), in_specs=[chan, chan, pl.Blo...  34.6 us
    pallas_call x1, Pallas kernels, value_back_stage(): pl.pallas_call(value_back_kernel, grid=(NG,), in_specs=[pl.BlockSpec((row...  27.7 us
    pallas_call x1, Pallas kernels, value_stage(): pl.pallas_call(value_kernel, grid=(NG,), in_specs=[pl.BlockSpec((ext, D),...  26.6 us
    pallas_call x1, Pallas kernels, intra_back_stage(): pl.pallas_call(intra_back_kernel, grid=(tokens // BL,), in_specs=[chan, c...  18.4 us
    ppermute x1, waiting for transfers between devices, local(): halo_r = lax.ppermute(dn_ext[-HALO:], 'mp', prevs)  16.4 us
    pallas_call x1, Pallas kernels, cross_back_stage(): pl.pallas_call(cross_back_kernel, grid=(tokens // BL,), in_specs=[chan, c...  15.8 us
  transfers between devices with their start and end apart: 45, of which 14 were waited for; matrix products, arithmetic and copies ran while one was open for 12% of the time, Pallas kernels for 28%

profile of v1, /device:TPU:1, one launch (start us, length us, event | category | flops | bytes accessed | tf_op | source)
XLA Modules:
  0.0 452.8 jit_solution(18018369041636384025)
XLA Ops:
  9.9 4.1 collective-permute-start.6
  20.7 3.7 collective-permute-start
  34.0 3.9 collective-permute-start.1
  43.7 3.2 pick.1
  50.2 6.2 %key_stage.1 = (f32[256,1152]{1,0:T(8,128)}, f32[256,1024]{1,0:T(8,128)}, bf16[256,1024]{1,0:T(8,128)(2,1)}, f32[8,128,128]{2,1,0:T(8,128)}) custom-call(bf16[1152,768]{1,0:T(8,128)(2,1)} %pad_maximum_fusion.3.nx_ref, bf16[256,768]{1,0:T(8,128)(2,1)} %bitcast.152, f32[256,8]{1,0:T(8,128)} %pad.21.taps_ref), custom_call_target="tpu_custom_call" | custom-call | bytes 6000000 | tf_op jit(solution)/shard_map/key_stage/pallas_call | solution.py:118
  57.4 8.6 %collective-permute-done.10 = bf16[6,80,768]{2,1,0:T(8,128)(2,1)S(1)} collective-permute-done((bf16[6,80,768]{2,1,0:T(8,128)(2,1)}, bf16[6,80,768]{2,1,0:T(8,128)(2,1)S(1)}, u32[]{:S(2)}, u32[]{:S(2)}) %collective-permute-start.10) | collective-permute-done | bytes 737312 | tf_op jit(solution)/shard_map/ppermute | solution.py:1109
  66.0 3.1 collective-permute-start.11
  72.9 3.3 pad_maximum_fusion.1.wv_ref
  76.2 26.6 %value_stage.1 = (bf16[1536,1024]{1,0:T(8,128)(2,1)}, bf16[1536,1024]{1,0:T(8,128)(2,1)}, bf16[1536,1152]{1,0:T(8,128)(2,1)}, f32[12,24,1024]{2,1,0:T(8,128)}, f...) custom-call(bf16[1152,768]{1,0:T(8,128)(2,1)} %pad_maximum_fusion.3.nx_ref, ...), custom_call_target="tpu_custom_call" | custom-call | bytes 27000000 | tf_op jit(solution)/shard_map/value_stage/pallas_call | solution.py:216
  109.0 11.9 %intra_stage.1.oi_ref = bf16[1536,1024]{1,0:T(8,128)(2,1)} custom-call(bf16[1536,1024]{1,0:T(8,128)(2,1)} %get-tuple-element.97.v_ref, f32[12,24,1024]{2,1,0:T(8,128)} %get-tuple-element.98.rows_ref, f32[8,128,128]{2,1,0:T(8,128)} %get-tuple-element.99.st_ref), custom_call_target="tpu_custom_call" | custom-call | bytes 12000000 | tf_op jit(solution)/shard_map/intra_stage/pallas_call | solution.py:380
  123.5 7.0 %chain_stage.1.sa_ref.sb_ref.refs_8_ = bf16[9,1536,128]{2,1,0:T(8,128)(2,1)} custom-call(s32[6]{0:T(128)} %pad_add_fusion.refs_0_.meta_ref, f32[8,1536,128]{2,1,0:T(8,128)} %get-tuple-element.101.refs_1_, f32[8,24,128]{2,1,0:T(8,128)} %get-tuple-element.102.refs_2_.tot_ref, f32[4,72,128]{2,1,0:T(8,128)} %maximum_convert_fusion.refs_3_, ...), custom_call_target="tpu_custom_call" | custom-call | bytes 7000000 | tf_op jit(solution)/shard_map/chain_stage/pallas_call | solution.py:336
  130.5 5.9 %pick_two.1 = (bf16[24,64,768]{2,1,0:T(8,128)(2,1)}, bf16[24,64,768]{2,1,0:T(8,128)(2,1)}) custom-call(s32[24]{0:T(128)} %fusion.39.index_ref, bf16[32,128,768]{2,1,0:T(8,128)(2,1)} %bitcast.148), custom_call_target="tpu_custom_call" | custom-call | bytes 6000000 | tf_op jit(solution)/shard_map/pick_two/pallas_call | solution.py:982
  136.5 34.6 %token_stage.1 = (bf16[1024,768]{1,0:T(8,128)(2,1)}, bf16[1536,1024]{1,0:T(8,128)(2,1)}, bf16[1536,1024]{1,0:T(8,128)(2,1)}, bf16[1536,1024]{1,0:T(8,128)(2,1)},...) custom-call(bf16[1536,1024]{1,0:T(8,128)(2,1)} %intra_stage.1.oi_ref, ...), custom_call_target="tpu_custom_call" | custom-call | bytes 35000000 | tf_op jit(solution)/shard_map/token_stage/pallas_call | solution.py:495
  171.0 13.9 %early_grad.1 = (bf16[24,128,768]{2,1,0:T(8,128)(2,1)}, f32[1024,768]{1,0:T(8,128)}) custom-call(bf16[1536,1024]{1,0:T(8,128)(2,1)} %get-tuple-element.107.dg_ref, bf16[1536,1024]{1,0:T(8,128)(2,1)} %get-tuple-element.108.r_ref, bf16[1152,768]{1,0:T(8,128)(2,1)} %pad_maximum_fusion.3.nx_ref, bf16[1024,768]{1,0:T(8,128)(2,1)} %go_ref.3, ...), custom_call_target="tpu_custom_call" | custom-call | bytes 12000000 | tf_op jit(solution)/shard_map/early_grad/pallas_call | solution.py:563
  188.1 4.4 collective-permute-done.18
  196.7 32.1 %collective-permute-done.20.refs_6_ = bf16[1536,128]{1,0:T(8,128)(2,1)S(1)} collective-permute-done((bf16[1536,128]{1,0:T(8,128)(2,1)S(1)}, bf16[1536,128]{1,0:T(8,128)(2,1)S(1)}, u32[]{:S(2)}, u32[]{:S(2)}) %collective-permute-start.20) | collective-permute-done | bytes 393248 | tf_op jit(solution)/shard_map/ppermute | solution.py:1109
  228.8 18.4 %intra_back.1 = (bf16[1536,1024]{1,0:T(8,128)(2,1)}, f32[4,24,1024]{2,1,0:T(8,128)}, f32[256,1024]{1,0:T(8,128)}) custom-call(bf16[1536,1024]{1,0:T(8,128)(2,1)} %get-tuple-element.97.v_ref, bf16[1536,1024]{1,0:T(8,128)(2,1)} %get-tuple-element.114.do_ref, f32[12,24,1024]{2,1,0:T(8,128)} %get-tuple-element.98.rows_ref, ...), custom_call_target="tpu_custom_call" | custom-call | bytes 18000000 | tf_op jit(solution)/shard_map/intra_back/pallas_call | solution.py:648
  248.8 3.2 deal.2
  265.5 8.6 %chain_back.1 = (bf16[9,1536,128]{2,1,0:T(8,128)(2,1)}, f32[9,24,128]{2,1,0:T(8,128)}) custom-call(s32[6]{0:T(128)} %pad_add_fusion.refs_0_.meta_ref, f32[8,1536,128]{2,1,0:T(8,128)} %get-tuple-element.123.refs_1_, f32[8,24,128]{2,1,0:T(8,128)} %get-tuple-element.102.refs_2_.tot_ref, f32[4,72,128]{2,1,0:T(8,128)} %maximum_convert_fusion.refs_3_, ...), custom_call_target="tpu_custom_call" | custom-call | bytes 7000000 | tf_op jit(solution)/shard_map/chain_back/pallas_call | solution.py:336
  274.1 15.8 %cross_back.1 = (bf16[1536,1024]{1,0:T(8,128)(2,1)}, f32[2,24,1024]{2,1,0:T(8,128)}, f32[256,1024]{1,0:T(8,128)}) custom-call(bf16[1536,1024]{1,0:T(8,128)(2,1)} %get-tuple-element.121.dvi_ref, bf16[1536,1024]{1,0:T(8,128)(2,1)} %get-tuple-element.97.v_ref, bf16[1536,1024]{1,0:T(8,128)(2,1)} %get-tuple-element.114.do_ref, ...), custom_call_target="tpu_custom_call" | custom-call | bytes 16000000 | tf_op jit(solution)/shard_map/cross_back/pallas_call | solution.py:738
  292.4 27.7 %value_back.1 = (bf16[24,80,768]{2,1,0:T(8,128)(2,1)}, f32[1152,768]{1,0:T(8,128)}, f32[3,8,512]{2,1,0:T(8,128)}) custom-call(bf16[1536,1024]{1,0:T(8,128)(2,1)} %get-tuple-element.135.dpre_ref, f32[1536,8]{1,0:T(8,128)} %pad.22.taps_ref, bf16[1536,1152]{1,0:T(8,128)(2,1)} %get-tuple-element.136.s_ref, f32[2,24,1024]{2,1,0:T(8,128)} %get-tuple-element.137.dx_ref, ...), custom_call_target="tpu_custom_call" | custom-call | bytes 27000000 | tf_op jit(solution)/shard_map/value_back/pallas_call | solution.py:910
  321.9 3.0 key_pre.1.dpre_ref
  324.9 8.3 %key_back.1 = (bf16[4,64,768]{2,1,0:T(8,128)(2,1)}, f32[1152,768]{1,0:T(8,128)}, f32[7,256,128]{2,1,0:T(8,128)}) custom-call(s32[6]{0:T(128)} %pad_add_fusion.refs_0_.meta_ref, f32[256,1024]{1,0:T(8,128)} %key_pre.1.dpre_ref, f32[256,8]{1,0:T(8,128)} %pad.21.taps_ref, f32[256,1152]{1,0:T(8,128)} %get-tuple-element.140.p_ref, ...), custom_call_target="tpu_custom_call" | custom-call | bytes 8000000 | tf_op jit(solution)/shard_map/key_back/pallas_call | solution.py:848
  341.0 3.7 add.298
  348.9 3.1 collective-permute-start.28
  352.7 16.4 %collective-permute-done.28 = f32[8,768]{1,0:T(8,128)S(1)} collective-permute-done((f32[8,768]{1,0:T(8,128)S(1)}, f32[8,768]{1,0:T(8,128)S(1)}, u32[]{:S(2)}, u32[]{:S(2)}) %collective-permute-start.28) | collective-permute-done | bytes 24608 | tf_op jit(solution)/shard_map/ppermute | solution.py:1354
  377.6 4.5 fusion.8
  393.0 10.4 %collective-permute-done.36 = bf16[80,768]{1,0:T(8,128)(2,1)S(1)} collective-permute-done((bf16[80,768]{1,0:T(8,128)(2,1)S(1)}, bf16[80,768]{1,0:T(8,128)(2,1)S(1)}, u32[]{:S(2)}, u32[]{:S(2)}) %collective-permute-start.36) | collective-permute-done | bytes 122912 | tf_op jit(solution)/shard_map/ppermute | solution.py:1109
  403.6 5.6 %collective-permute-start.39 = (bf16[1,16,768]{2,1,0:T(8,128)(2,1)S(1)}, bf16[1,16,768]{2,1,0:T(8,128)(2,1)S(1)}, u32[]{:S(2)}, u32[]{:S(2)}) collective-permute-start(bf16[1,16,768]{2,1,0:T(8,128)(2,1)S(1)} %get-tuple-element.323), channel_id=1, source_target_pairs={{0,8},{4,12},{8,0},{12,4},{16,24},{20,28},{24,16},{28,20},{1,9},{5... | collective-permute-start | bytes 73736 | tf_op jit(solution)/shard_map/ppermute | solution.py:1109
  418.0 4.5 collective-permute-done.42
  422.5 4.9 %collective-permute-start.43 = (bf16[16,16,768]{2,1,0:T(8,128)(2,1)S(1)}, bf16[16,16,768]{2,1,0:T(8,128)(2,1)S(1)}, u32[]{:S(2)}, u32[]{:S(2)}) collective-permute-start(bf16[16,16,768]{2,1,0:T(8,128)(2,1)S(1)} %get-tuple-element.311), channel_id=1, source_target_pairs={{0,1},{1,0},{2,3},{3,2},{4,5},{5,4},{6,7},{7,6},{8,9},{9,8},{10,11... | collective-permute-start | bytes 1179656 | tf_op jit(solution)/shard_map/ppermute | solution.py:1109
  436.2 5.2 %finish_stage.1 = (f32[768,256]{1,0:T(8,128)}, f32[768,256]{1,0:T(8,128)}, f32[768,256]{1,0:T(8,128)}, f32[768,256]{1,0:T(8,128)}, f32[32,768]{1,0:T(8,128)}, /*index=5*/f32[8,768]{1,0:T(8,128)}) custom-call(s32[32]{0:T(128)} %add.329.code_ref, bf16[32,16,768]{2,1,0:T(8,128)(2,1)} %copy-done.10, f32[768,256]{1,0:T(8,128)} %w_ref.1, f32[768,256]{1,0:T(8,128)} %m_ref.1, ...), custom_call_target="tpu_custom_call" | custom-call | bytes 5000000 | tf_op jit(solution)/shard_map/finish_stage/pallas_call | solution.py:1088
  (332 shorter events, 120.6 us)
Async XLA Ops:
  7.2 123.3 %all-gather.3.cloned.1.call-start = ((), (), s32[]{:S(2)}) async-start(), calls=%async_computation | async-start | bytes 6488064 | tf_op jit(solution)/shard_map/all_gather | solution.py:1178
  9.9 21.8 %collective-permute-start.6 = (bf16[80,768]{1,0:T(8,128)(2,1)}, bf16[80,768]{1,0:T(8,128)(2,1)S(1)}, u32[]{:S(2)}, u32[]{:S(2)}) collective-permute-start(bf16[80,768]{1,0:T(8,128)(2,1)} %get-tuple-element.315), channel_id=1, source_target_pairs={{0,20},{4,16},{8,28},{12,24},{16,4},{20,0},{24,12},{28,8},{1,21},{... | collective-permute-start | bytes 368648 | tf_op jit(solution)/shard_map/ppermute | solution.py:1109
  14.0 19.1 %collective-permute-start.7 = (bf16[80,768]{1,0:T(8,128)(2,1)}, bf16[80,768]{1,0:T(8,128)(2,1)S(1)}, u32[]{:S(2)}, u32[]{:S(2)}) collective-permute-start(bf16[80,768]{1,0:T(8,128)(2,1)} %get-tuple-element.315), channel_id=1, source_target_pairs={{0,24},{4,28},{8,16},{12,20},{16,8},{20,12},{24,0},{28,4},{1,25},{... | collective-permute-start | bytes 368648 | tf_op jit(solution)/shard_map/ppermute | solution.py:1109
  15.1 18.9 %collective-permute-start.8 = (bf16[80,768]{1,0:T(8,128)(2,1)}, bf16[80,768]{1,0:T(8,128)(2,1)}, u32[]{:S(2)}, u32[]{:S(2)}) collective-permute-start(bf16[80,768]{1,0:T(8,128)(2,1)} %get-tuple-element.315), channel_id=1, source_target_pairs={{0,28},{4,24},{8,20},{12,16},{16,12},{20,8},{24,4},{28,0},{1,29},{... | collective-permute-start | bytes 368648 | tf_op jit(solution)/shard_map/ppermute | solution.py:1109
  17.3 21.4 %collective-permute-start.2 = (bf16[80,768]{1,0:T(8,128)(2,1)}, bf16[80,768]{1,0:T(8,128)(2,1)}, u32[]{:S(2)}, u32[]{:S(2)}) collective-permute-start(bf16[80,768]{1,0:T(8,128)(2,1)} %get-tuple-element.315), channel_id=1, source_target_pairs={{0,4},{4,0},{8,12},{12,8},{16,20},{20,16},{24,28},{28,24},{1,5},{5... | collective-permute-start | bytes 368648 | tf_op jit(solution)/shard_map/ppermute | solution.py:1109
  20.7 11.1 %collective-permute-start = (bf16[8,768]{1,0:T(8,128)(2,1)S(1)}, bf16[8,768]{1,0:T(8,128)(2,1)S(1)}, u32[]{:S(2)}, u32[]{:S(2)}) collective-permute-start(bf16[8,768]{1,0:T(8,128)(2,1)S(1)} %get-tuple-element.303), channel_id=1, source_target_pairs={{1,0},{2,1},{3,2},{5,4},{6,5},{7,6},{9,8},{10,9},{11,10},{13,12},{... | collective-permute-start | bytes 36872 | tf_op jit(solution)/shard_map/ppermute | solution.py:1197
  31.8 8.7 %collective-permute-start.3 = (bf16[80,768]{1,0:T(8,128)(2,1)}, bf16[80,768]{1,0:T(8,128)(2,1)S(1)}, u32[]{:S(2)}, u32[]{:S(2)}) collective-permute-start(bf16[80,768]{1,0:T(8,128)(2,1)} %get-tuple-element.315), channel_id=1, source_target_pairs={{0,8},{4,12},{8,0},{12,4},{16,24},{20,28},{24,16},{28,20},{1,9},{5... | collective-permute-start | bytes 368648 | tf_op jit(solution)/shard_map/ppermute | solution.py:1109
  31.8 11.2 %collective-permute-start.4 = (bf16[80,768]{1,0:T(8,128)(2,1)}, bf16[80,768]{1,0:T(8,128)(2,1)S(1)}, u32[]{:S(2)}, u32[]{:S(2)}) collective-permute-start(bf16[80,768]{1,0:T(8,128)(2,1)} %get-tuple-element.315), channel_id=1, source_target_pairs={{0,12},{4,8},{8,4},{12,0},{16,28},{20,24},{24,20},{28,16},{1,13},{... | collective-permute-start | bytes 368648 | tf_op jit(solution)/shard_map/ppermute | solution.py:1109
  33.2 9.8 %collective-permute-start.5 = (bf16[80,768]{1,0:T(8,128)(2,1)}, bf16[80,768]{1,0:T(8,128)(2,1)S(1)}, u32[]{:S(2)}, u32[]{:S(2)}) collective-permute-start(bf16[80,768]{1,0:T(8,128)(2,1)} %get-tuple-element.315), channel_id=1, source_target_pairs={{0,16},{4,20},{8,24},{12,28},{16,0},{20,4},{24,8},{28,12},{1,17},{... | collective-permute-start | bytes 368648 | tf_op jit(solution)/shard_map/ppermute | solution.py:1109
  34.0 13.9 %collective-permute-start.1 = (bf16[8,768]{1,0:T(8,128)(2,1)S(1)}, bf16[8,768]{1,0:T(8,128)(2,1)S(1)}, u32[]{:S(2)}, u32[]{:S(2)}) collective-permute-start(bf16[8,768]{1,0:T(8,128)(2,1)S(1)} %get-tuple-element.304), channel_id=1, source_target_pairs={{0,1},{1,2},{2,3},{4,5},{5,6},{6,7},{8,9},{9,10},{10,11},{12,13},{... | collective-permute-start | bytes 36872 | tf_op jit(solution)/shard_map/ppermute | solution.py:1196
  38.6 31.1 %collective-permute-start.13 = (f32[6,10,64]{2,0,1:T(8,128)S(1)}, f32[6,10,64]{2,0,1:T(8,128)S(1)}, u32[]{:S(2)}, u32[]{:S(2)}) collective-permute-start(f32[6,10,64]{2,0,1:T(8,128)S(1)} %copy-done.13), channel_id=1, source_target_pairs={{0,2},{1,3},{2,0},{3,1},{4,6},{5,7},{6,4},{7,5},{8,10},{9,11},{10,... | collective-permute-start | bytes 46088 | tf_op jit(solution)/shard_map/ppermute | solution.py:1109
  40.5 29.9 %collective-permute-start.12 = (f32[6,10,64]{2,0,1:T(8,128)S(1)}, f32[6,10,64]{2,0,1:T(8,128)S(1)}, u32[]{:S(2)}, u32[]{:S(2)}) collective-permute-start(f32[6,10,64]{2,0,1:T(8,128)S(1)} %copy-done.13), channel_id=1, source_target_pairs={{0,1},{1,0},{2,3},{3,2},{4,5},{5,4},{6,7},{7,6},{8,9},{9,8},{10,11... | collective-permute-start | bytes 46088 | tf_op jit(solution)/shard_map/ppermute | solution.py:1109
  46.9 19.1 %collective-permute-start.10 = (bf16[6,80,768]{2,1,0:T(8,128)(2,1)}, bf16[6,80,768]{2,1,0:T(8,128)(2,1)S(1)}, u32[]{:S(2)}, u32[]{:S(2)}) collective-permute-start(bf16[6,80,768]{2,1,0:T(8,128)(2,1)} %pick.1), channel_id=1, source_target_pairs={{0,2},{1,3},{2,0},{3,1},{4,6},{5,7},{6,4},{7,5},{8,10},{9,11},{10,... | collective-permute-start | bytes 2211848 | tf_op jit(solution)/shard_map/ppermute | solution.py:1109
  56.4 16.5 %collective-permute-start.9 = (bf16[6,80,768]{2,1,0:T(8,128)(2,1)S(1)}, bf16[6,80,768]{2,1,0:T(8,128)(2,1)S(1)}, u32[]{:S(2)}, u32[]{:S(2)}) collective-permute-start(bf16[6,80,768]{2,1,0:T(8,128)(2,1)S(1)} %copy-done.8), channel_id=1, source_target_pairs={{0,1},{1,0},{2,3},{3,2},{4,5},{5,4},{6,7},{7,6},{8,9},{9,8},{10,11... | collective-permute-start | bytes 2211848 | tf_op jit(solution)/shard_map/ppermute | solution.py:1109
  104.6 16.3 %collective-permute-start.15 = (bf16[1608,128]{1,0:T(8,128)(2,1)S(1)}, bf16[1608,128]{1,0:T(8,128)(2,1)S(1)}, u32[]{:S(2)}, u32[]{:S(2)}) collective-permute-start(bf16[1608,128]{1,0:T(8,128)(2,1)S(1)} %pad_maximum_fusion.5.refs_4_), channel_id=1, source_target_pairs={{0,2},{1,3},{2,0},{3,1},{4,6},{5,7},{6,4},{7,5},{8,10},{9,11},{10,... | collective-permute-start | bytes 1234952 | tf_op jit(solution)/shard_map/ppermute | solution.py:1109
  107.1 13.9 %collective-permute-start.16 = (bf16[1608,128]{1,0:T(8,128)(2,1)S(1)}, bf16[1608,128]{1,0:T(8,128)(2,1)S(1)}, u32[]{:S(2)}, u32[]{:S(2)}) collective-permute-start(bf16[1608,128]{1,0:T(8,128)(2,1)S(1)} %pad_maximum_fusion.5.refs_4_), channel_id=1, source_target_pairs={{0,1},{1,0},{2,3},{3,2},{4,5},{5,4},{6,7},{7,6},{8,9},{9,8},{10,11... | collective-permute-start | bytes 1234952 | tf_op jit(solution)/shard_map/ppermute | solution.py:1109
  192.9 54.4 %collective-permute-start.19 = (bf16[768,768]{1,0:T(8,128)(2,1)S(1)}, bf16[768,768]{1,0:T(8,128)(2,1)S(1)}, u32[]{:S(2)}, u32[]{:S(2)}) collective-permute-start(bf16[768,768]{1,0:T(8,128)(2,1)S(1)} %fusion.10), channel_id=1, source_target_pairs={{0,2},{1,3},{2,0},{3,1},{4,6},{5,7},{6,4},{7,5},{8,10},{9,11},{10,... | collective-permute-start | bytes 3538952 | tf_op jit(solution)/shard_map/ppermute | solution.py:1109
  193.2 35.6 %collective-permute-start.20 = (bf16[1536,128]{1,0:T(8,128)(2,1)S(1)}, bf16[1536,128]{1,0:T(8,128)(2,1)S(1)}, u32[]{:S(2)}, u32[]{:S(2)}) collective-permute-start(bf16[1536,128]{1,0:T(8,128)(2,1)S(1)} %copy-done.20), channel_id=1, source_target_pairs={{0,2},{1,3},{2,0},{3,1},{4,6},{5,7},{6,4},{7,5},{8,10},{9,11},{10,... | collective-permute-start | bytes 1179656 | tf_op jit(solution)/shard_map/ppermute | solution.py:1109
  252.0 38.0 %collective-permute-start.21 = (bf16[4,128,768]{2,1,0:T(8,128)(2,1)}, bf16[4,128,768]{2,1,0:T(8,128)(2,1)S(1)}, u32[]{:S(2)}, u32[]{:S(2)}) collective-permute-start(bf16[4,128,768]{2,1,0:T(8,128)(2,1)} %get-tuple-element.120), channel_id=1, source_target_pairs={{0,4},{4,0},{8,12},{12,8},{16,20},{20,16},{24,28},{28,24},{1,5},{5... | collective-permute-start | bytes 2359304 | tf_op jit(solution)/shard_map/ppermute | solution.py:1109
  253.1 11.5 %collective-permute-start.22 = (bf16[1536,128]{1,0:T(8,128)(2,1)S(1)}, bf16[1536,128]{1,0:T(8,128)(2,1)S(1)}, u32[]{:S(2)}, u32[]{:S(2)}) collective-permute-start(bf16[1536,128]{1,0:T(8,128)(2,1)S(1)} %copy-done.20), channel_id=1, source_target_pairs={{0,1},{1,0},{2,3},{3,2},{4,5},{5,4},{6,7},{7,6},{8,9},{9,8},{10,11... | collective-permute-start | bytes 1179656 | tf_op jit(solution)/shard_map/ppermute | solution.py:1109
  291.3 33.5 %collective-permute-start.24 = (bf16[2,128,768]{2,1,0:T(8,128)(2,1)S(1)}, bf16[2,128,768]{2,1,0:T(8,128)(2,1)S(1)}, u32[]{:S(2)}, u32[]{:S(2)}) collective-permute-start(bf16[2,128,768]{2,1,0:T(8,128)(2,1)S(1)} %slice.292), channel_id=1, source_target_pairs={{0,16},{4,20},{8,24},{12,28},{16,0},{20,4},{24,8},{28,12},{1,17},{... | collective-permute-start | bytes 1179656 | tf_op jit(solution)/shard_map/ppermute | solution.py:1109
  348.1 21.7 %collective-permute-start.30 = (bf16[552,768]{1,0:T(8,128)(2,1)S(1)}, bf16[552,768]{1,0:T(8,128)(2,1)S(1)}, u32[]{:S(2)}, u32[]{:S(2)}) collective-permute-start(bf16[552,768]{1,0:T(8,128)(2,1)S(1)} %fusion.13), channel_id=1, source_target_pairs={{0,2},{1,3},{2,0},{3,1},{4,6},{5,7},{6,4},{7,5},{8,10},{9,11},{10,... | collective-permute-start | bytes 2543624 | tf_op jit(solution)/shard_map/ppermute | solution.py:1109
  348.2 21.5 %collective-permute-start.31 = (bf16[128,768]{1,0:T(8,128)(2,1)S(1)}, bf16[128,768]{1,0:T(8,128)(2,1)S(1)}, u32[]{:S(2)}, u32[]{:S(2)}) collective-permute-start(bf16[128,768]{1,0:T(8,128)(2,1)S(1)} %fusion.24), channel_id=1, source_target_pairs={{0,8},{4,12},{8,0},{12,4},{16,24},{20,28},{24,16},{28,20},{1,9},{5... | collective-permute-start | bytes 589832 | tf_op jit(solution)/shard_map/ppermute | solution.py:1109
  348.9 20.1 %collective-permute-start.28 = (f32[8,768]{1,0:T(8,128)S(1)}, f32[8,768]{1,0:T(8,128)S(1)}, u32[]{:S(2)}, u32[]{:S(2)}) collective-permute-start(f32[8,768]{1,0:T(8,128)S(1)} %get-tuple-element.300), channel_id=1, source_target_pairs={{1,0},{2,1},{3,2},{5,4},{6,5},{7,6},{9,8},{10,9},{11,10},{13,12},{... | collective-permute-start | bytes 73736 | tf_op jit(solution)/shard_map/ppermute | solution.py:1354
  376.6 9.9 %collective-permute-start.32 = (bf16[80,768]{1,0:T(8,128)(2,1)}, bf16[80,768]{1,0:T(8,128)(2,1)S(1)}, u32[]{:S(2)}, u32[]{:S(2)}) collective-permute-start(bf16[80,768]{1,0:T(8,128)(2,1)} %get-tuple-element.153), channel_id=1, source_target_pairs={{0,4},{4,0},{8,12},{12,8},{16,20},{20,16},{24,28},{28,24},{1,5},{5... | collective-permute-start | bytes 368648 | tf_op jit(solution)/shard_map/ppermute | solution.py:1109
  377.0 11.5 %collective-permute-start.33 = (bf16[80,768]{1,0:T(8,128)(2,1)}, bf16[80,768]{1,0:T(8,128)(2,1)S(1)}, u32[]{:S(2)}, u32[]{:S(2)}) collective-permute-start(bf16[80,768]{1,0:T(8,128)(2,1)} %get-tuple-element.154), channel_id=1, source_target_pairs={{0,8},{4,12},{8,0},{12,4},{16,24},{20,28},{24,16},{28,20},{1,9},{5... | collective-permute-start | bytes 368648 | tf_op jit(solution)/shard_map/ppermute | solution.py:1109
  382.2 10.8 %collective-permute-start.34 = (bf16[80,768]{1,0:T(8,128)(2,1)S(1)}, bf16[80,768]{1,0:T(8,128)(2,1)S(1)}, u32[]{:S(2)}, u32[]{:S(2)}) collective-permute-start(bf16[80,768]{1,0:T(8,128)(2,1)S(1)} %copy-done.51), channel_id=1, source_target_pairs={{0,12},{4,8},{8,4},{12,0},{16,28},{20,24},{24,20},{28,16},{1,13},{... | collective-permute-start | bytes 368648 | tf_op jit(solution)/shard_map/ppermute | solution.py:1109
  384.0 9.0 %collective-permute-start.35 = (bf16[80,768]{1,0:T(8,128)(2,1)S(1)}, bf16[80,768]{1,0:T(8,128)(2,1)S(1)}, u32[]{:S(2)}, u32[]{:S(2)}) collective-permute-start(bf16[80,768]{1,0:T(8,128)(2,1)S(1)} %copy-done.50), channel_id=1, source_target_pairs={{0,16},{4,20},{8,24},{12,28},{16,0},{20,4},{24,8},{28,12},{1,17},{... | collective-permute-start | bytes 368648 | tf_op jit(solution)/shard_map/ppermute | solution.py:1109
  386.4 17.0 %collective-permute-start.36 = (bf16[80,768]{1,0:T(8,128)(2,1)S(1)}, bf16[80,768]{1,0:T(8,128)(2,1)S(1)}, u32[]{:S(2)}, u32[]{:S(2)}) collective-permute-start(bf16[80,768]{1,0:T(8,128)(2,1)S(1)} %copy-done.49), channel_id=1, source_target_pairs={{0,20},{4,16},{8,28},{12,24},{16,4},{20,0},{24,12},{28,8},{1,21},{... | collective-permute-start | bytes 368648 | tf_op jit(solution)/shard_map/ppermute | solution.py:1109
  386.5 16.9 %collective-permute-start.37 = (bf16[80,768]{1,0:T(8,128)(2,1)S(1)}, bf16[80,768]{1,0:T(8,128)(2,1)S(1)}, u32[]{:S(2)}, u32[]{:S(2)}) collective-permute-start(bf16[80,768]{1,0:T(8,128)(2,1)S(1)} %copy-done.48), channel_id=1, source_target_pairs={{0,24},{4,28},{8,16},{12,20},{16,8},{20,12},{24,0},{28,4},{1,25},{... | collective-permute-start | bytes 368648 | tf_op jit(solution)/shard_map/ppermute | solution.py:1109
  388.6 14.8 %collective-permute-start.38 = (bf16[80,768]{1,0:T(8,128)(2,1)S(1)}, bf16[80,768]{1,0:T(8,128)(2,1)S(1)}, u32[]{:S(2)}, u32[]{:S(2)}) collective-permute-start(bf16[80,768]{1,0:T(8,128)(2,1)S(1)} %copy-done.47), channel_id=1, source_target_pairs={{0,28},{4,24},{8,20},{12,16},{16,12},{20,8},{24,4},{28,0},{1,29},{... | collective-permute-start | bytes 368648 | tf_op jit(solution)/shard_map/ppermute | solution.py:1109
  422.5 12.7 %collective-permute-start.43 = (bf16[16,16,768]{2,1,0:T(8,128)(2,1)S(1)}, bf16[16,16,768]{2,1,0:T(8,128)(2,1)S(1)}, u32[]{:S(2)}, u32[]{:S(2)}) collective-permute-start(bf16[16,16,768]{2,1,0:T(8,128)(2,1)S(1)} %get-tuple-element.311), channel_id=1, source_target_pairs={{0,1},{1,0},{2,3},{3,2},{4,5},{5,4},{6,7},{7,6},{8,9},{9,8},{10,11... | collective-permute-start | bytes 1179656 | tf_op jit(solution)/shard_map/ppermute | solution.py:1109
  (66 other events, 946.9 us)
Sparse Core Ops, SparseCore 0:
  11.5 76.0 all-gather.2

commit v2 on v1

--- a/solution.py
+++ b/solution.py
@@ -59,6 +59,13 @@
     return lax.dot_general(a, b, (((0,), (0,)), ((), ())), preferred_element_type=f32)
 
 
+def lane_sums(x):
+    ones = jnp.ones((8, x.shape[1]), bf16)
+    high = x.astype(bf16)
+    rest = (x - high.astype(f32)).astype(bf16)
+    return nt(ones, high) + nt(ones, rest)
+
+
 def sigmoid(v):
     return 1.0 / (1.0 + jnp.exp(-v))
 
@@ -73,7 +80,7 @@
     for k in range(K):
         shift = (sign * (k - K // 2)) % ext
         moved = signal if shift == 0 else pltpu.roll(signal, shift, axis=1)
-        term = moved * taps[:, k : k + 1]
+        term = moved.astype(f32) * taps[:, k : k + 1]
         total = term if total is None else total + term
     return total
 
@@ -141,9 +148,9 @@
         for c in range(PS // 16):
             src = h * WV + c * 16
             dst = h * PS + c * 16
-            signal = p_scr[src : src + 16, :]
+            signal = p_scr[src : src + 16, :].astype(bf16)
             pre = conv_taps(signal, taps_ref[dst : dst + 16, :], -1)[:, :tokens]
-            s_ref[dst : dst + 16, :] = signal.astype(bf16)
+            s_ref[dst : dst + 16, :] = signal
             u_ref[dst : dst + 16, :] = pre.astype(bf16)
             v_ref[dst : dst + 16, :] = (pre * sigmoid(pre)).astype(bf16)
     x_f = jnp.concatenate(
@@ -192,7 +199,7 @@
             lhs_scr[span, BL:] = (vals * w_r[h : h + 1]).astype(bf16)
         keys = stacked_keys(k4_ref[:NS, cuts[b]], k4_ref[2 * NS : 3 * NS, cuts[b]])
         local_state = nt(lhs_scr[...], keys)
-        sblk_ref[b] = local_state
+        sblk_ref[b] = local_state.astype(bf16)
         keep = jnp.where(first, jnp.exp(end_f), 1.0)
         gain = jnp.where(first, 1.0, jnp.exp(cum_r))
         state = jnp.concatenate(
@@ -240,7 +247,7 @@
             jax.ShapeDtypeStruct((CH, ext), bf16),
             jax.ShapeDtypeStruct((KINDS, H, tokens), f32),
             jax.ShapeDtypeStruct((blocks, H, BL), f32),
-            jax.ShapeDtypeStruct((blocks, CH, BL), f32),
+            jax.ShapeDtypeStruct((blocks, CH, BL), bf16),
             jax.ShapeDtypeStruct((CH, BL), bf16),
             jax.ShapeDtypeStruct((H, BL), f32),
         ),
@@ -294,19 +301,24 @@
                 weight = jnp.where(first, from_left, from_right)
             entering = entering + weight * states[k][span, :].astype(f32)
         decay = [jnp.exp(tot_ref[b, pl.ds(head, 1), :]) for b in range(blocks)]
+        locals_ = [sblk_ref[b, span, :].astype(f32) for b in range(blocks)]
         up = [entering]
+        down = [entering]
         for b in range(blocks):
-            up.append(up[-1] * decay[b] + sblk_ref[b, span, :])
-        down = entering
-        for b in range(blocks, -1, -1):
-            if b < blocks:
-                down = down * decay[b] + sblk_ref[b, span, :]
-            both = jnp.where(up_lanes, up[b], down)
+            up.append(up[-1] * decay[b] + locals_[b])
+            rev = blocks - 1 - b
+            down.append(down[-1] * decay[rev] + locals_[rev])
+        down = down[::-1]
+        for b in range(blocks):
+            both = jnp.where(up_lanes, up[b], down[b + 1])
             out_ref[b, span, :] = both.astype(bf16)
             if flip:
-                dot_ref[b, pl.ds(head, 1), :] = jnp.sum(
-                    both * other_ref[b, span, :].astype(f32), axis=0, keepdims=True
-                )
+                before = other_ref[b - 1 if b > 0 else blocks, span, :]
+                beyond = other_ref[b + 1, span, :]
+                far = jnp.where(wide, beyond.astype(f32), before.astype(f32))
+                dot_ref[b, pl.ds(head, 1), :] = jnp.sum(both * far, axis=0, keepdims=True)
+        if not flip:
+            out_ref[blocks, span, :] = jnp.where(up_lanes, up[blocks], down[0]).astype(bf16)
 
 
 def chain_stage(meta, sblk, tot, far_tot, states, twist, tokens, other=None):
@@ -321,13 +333,14 @@
     ]
     for k in range(copies):
         in_specs.append(pl.BlockSpec((rows, BL), lambda q, meta, k=k: (twist(k, q), 0)))
-    out_specs = [pl.BlockSpec((blocks + 1, rows, BL), lambda q, meta: (0, q, 0))]
-    out_shape = [jax.ShapeDtypeStruct((blocks + 1, CH, BL), bf16)]
+    held = blocks if flip else blocks + 1
+    out_specs = [pl.BlockSpec((held, rows, BL), lambda q, meta: (0, q, 0))]
+    out_shape = [jax.ShapeDtypeStruct((held, CH, BL), bf16)]
     args = [meta, sblk, tot, far_tot, *states]
     if flip:
         in_specs.append(pl.BlockSpec((blocks + 1, rows, BL), lambda q, meta: (0, q, 0)))
-        out_specs.append(pl.BlockSpec((blocks + 1, H, BL), lambda q, meta: (0, 0, 0)))
-        out_shape.append(jax.ShapeDtypeStruct((blocks + 1, H, BL), f32))
+        out_specs.append(pl.BlockSpec((blocks, H, BL), lambda q, meta: (0, 0, 0)))
+        out_shape.append(jax.ShapeDtypeStruct((blocks, H, BL), f32))
         args.append(other)
 
     def body(*refs):
@@ -394,11 +407,11 @@
 
 
 def token_kernel(
-    oi_ref, v_ref, sa_ref, sb_ref, k4_ref, rows_ref, tot_ref, wg_ref, wo_ref,
+    oi_ref, v_ref, s_ref, k4_ref, rows_ref, tot_ref, wg_ref, wo_ref,
     nx_ref, hid_ref, go_ref, cols_ref,
-    ho_ref, r_ref, dg_ref, do_ref, dsblk_ref, dsdev_ref, rc_ref, small_ref,
-    cf_scr, cr_scr, g_scr, dres_scr, mix_scr, gated_scr, lhs_scr, gain_scr, diag_scr,
-    dev_scr, cum_scr,
+    ho_ref, r_ref, dg_ref, do_ref, dsblk_ref, dsdev_ref, rc_ref, dk_ref, small_ref,
+    cross_scr, g_scr, dres_scr, mix_scr, gated_scr, lhs_scr, gain_scr, diag_scr,
+    dev_scr, cum_scr, wide_scr,
 ):
     step = pl.program_id(0)
     last = pl.num_programs(0) - 1
@@ -409,26 +422,25 @@
         diag_scr[...] = jnp.zeros_like(diag_scr)
         dev_scr[...] = jnp.zeros_like(dev_scr)
         cum_scr[...] = jnp.zeros_like(cum_scr)
+        wide_scr[0] = jnp.broadcast_to(cols_ref[:, 0:1], (CH, BL))
+        wide_scr[1] = jnp.broadcast_to(cols_ref[:, 1:2], (CH, BL))
 
     c_f = k4_ref[NS : 2 * NS, :]
     c_r = k4_ref[3 * NS :, :]
-    zero = jnp.zeros_like(c_f)
-    cf_scr[...] = nn(sa_ref[0], jnp.concatenate([c_f, zero], axis=0))
-    cr_scr[...] = nn(sb_ref[0], jnp.concatenate([zero, c_r], axis=0))
+    both_keys = stacked_keys(c_f, c_r)
+    cross_scr[...] = nn(s_ref[0], both_keys)
     g_scr[...] = nt(wg_ref[...], nx_ref[...])
     dres_scr[...] = nt(wo_ref[...], go_ref[...])
     squares = jnp.zeros((8, BL), f32)
     for h in range(H):
         span = slice(h * PS, (h + 1) * PS)
-        part_f = cf_scr[span, :] * rows_ref[EF, h : h + 1, :]
-        part_r = cr_scr[span, :] * rows_ref[ER, h : h + 1, :]
-        cf_scr[span, :] = part_f
-        cr_scr[span, :] = part_r
+        part_f = cross_scr[span, :BL] * rows_ref[EF, h : h + 1, :]
+        part_r = cross_scr[span, BL:] * rows_ref[ER, h : h + 1, :]
         mix = (
             oi_ref[span, :].astype(f32)
             + part_f
             + part_r
-            + cols_ref[span, 1:2] * v_ref[span, :].astype(f32)
+            + wide_scr[1, span, :] * v_ref[span, :].astype(f32)
         )
         gate = g_scr[span, :]
         gated = mix * (gate * sigmoid(gate))
@@ -440,7 +452,7 @@
     for h in range(H):
         span = slice(h * PS, (h + 1) * PS)
         gated = gated_scr[span, :]
-        gain = cols_ref[span, 0:1]
+        gain = wide_scr[0, span, :]
         normal = gated * scale
         r_ref[span, :] = (normal * gain).astype(bf16)
         dres = dres_scr[span, :]
@@ -451,7 +463,7 @@
     pull = scale * scale * scale * (jnp.sum(cross, axis=0, keepdims=True) / CH)
     for h in range(H):
         span = slice(h * PS, (h + 1) * PS)
-        dgated = scale * (dres_scr[span, :] * cols_ref[span, 0:1]) - gated_scr[span, :] * pull
+        dgated = scale * (dres_scr[span, :] * wide_scr[0, span, :]) - gated_scr[span, :] * pull
         gate = g_scr[span, :]
         soft = sigmoid(gate)
         grad_mix = dgated * (gate * soft)
@@ -460,12 +472,17 @@
         )
         diag_scr[span, :] += grad_mix * v_ref[span, :].astype(f32)
         do_ref[span, :] = grad_mix.astype(bf16)
-        rc_ref[0, h : h + 1, :] = jnp.sum(grad_mix * cf_scr[span, :], axis=0, keepdims=True)
-        rc_ref[1, h : h + 1, :] = jnp.sum(grad_mix * cr_scr[span, :], axis=0, keepdims=True)
-        lhs_scr[span, :BL] = (grad_mix * rows_ref[EF, h : h + 1, :]).astype(bf16)
-        lhs_scr[span, BL:] = (grad_mix * rows_ref[ER, h : h + 1, :]).astype(bf16)
-    dstate = nt(lhs_scr[...], stacked_keys(c_f, c_r))
-    dsblk_ref[0] = dstate
+        grad_f = grad_mix * rows_ref[EF, h : h + 1, :]
+        grad_r = grad_mix * rows_ref[ER, h : h + 1, :]
+        rc_ref[0, h : h + 1, :] = jnp.sum(grad_f * cross_scr[span, :BL], axis=0, keepdims=True)
+        rc_ref[1, h : h + 1, :] = jnp.sum(grad_r * cross_scr[span, BL:], axis=0, keepdims=True)
+        lhs_scr[span, :BL] = grad_f.astype(bf16)
+        lhs_scr[span, BL:] = grad_r.astype(bf16)
+    dstate = nt(lhs_scr[...], both_keys)
+    dkeys = tn(s_ref[0], lhs_scr[...])
+    dk_ref[:NS, :] = dkeys[:NS, :BL]
+    dk_ref[NS:, :] = dkeys[NS:, BL:]
+    dsblk_ref[0] = dstate.astype(bf16)
     first = lane_first((H, BL))
     total = tot_ref[0]
     keep = jnp.where(first, 1.0, jnp.exp(total))
@@ -480,9 +497,8 @@
     @pl.when(step == last)
     def _():
         dsdev_ref[...] = dev_scr[...].astype(bf16)
-        ones = jnp.ones((8, BL), f32)
-        small_ref[0] = nt(ones, gain_scr[...], lax.Precision.HIGHEST)
-        small_ref[1] = nt(ones, diag_scr[...], lax.Precision.HIGHEST)
+        small_ref[0] = lane_sums(gain_scr[...])
+        small_ref[1] = lane_sums(diag_scr[...])
 
 
 def token_stage(oi, v, s9, k4, rows, tot, wg, wo, nx, hid, go, cols):
@@ -499,7 +515,6 @@
             chan,
             chan,
             pl.BlockSpec((1, CH, BL), lambda b: (b, 0, 0)),
-            pl.BlockSpec((1, CH, BL), lambda b: (b + 1, 0, 0)),
             pl.BlockSpec((4 * NS, BL), lambda b: (0, b)),
             pl.BlockSpec((KINDS, H, BL), lambda b: (0, 0, b)),
             pl.BlockSpec((1, H, BL), lambda b: (b, 0, 0)),
@@ -518,6 +533,7 @@
             pl.BlockSpec((1, CH, BL), lambda b: (b, 0, 0)),
             pl.BlockSpec((CH, BL), lambda b: (0, 0)),
             pl.BlockSpec((2, H, BL), lambda b: (0, 0, b)),
+            pl.BlockSpec((2 * NS, BL), lambda b: (0, b)),
             pl.BlockSpec((2, 8, CH), lambda b: (0, 0, 0)),
         ],
         out_shape=(
@@ -525,19 +541,21 @@
             jax.ShapeDtypeStruct((CH, tokens), bf16),
             jax.ShapeDtypeStruct((CH, tokens), bf16),
             jax.ShapeDtypeStruct((CH, tokens), bf16),
-            jax.ShapeDtypeStruct((blocks, CH, BL), f32),
+            jax.ShapeDtypeStruct((blocks, CH, BL), bf16),
             jax.ShapeDtypeStruct((CH, BL), bf16),
             jax.ShapeDtypeStruct((2, H, tokens), f32),
+            jax.ShapeDtypeStruct((2 * NS, tokens), f32),
             jax.ShapeDtypeStruct((2, 8, CH), f32),
         ),
-        scratch_shapes=[big] * 6
+        scratch_shapes=[pltpu.VMEM((CH, 2 * BL), f32)]
+        + [big] * 4
         + [pltpu.VMEM((CH, 2 * BL), bf16)]
         + [big] * 3
-        + [pltpu.VMEM((H, BL), f32)],
+        + [pltpu.VMEM((H, BL), f32), pltpu.VMEM((2, CH, BL), f32)],
         compiler_params=params(),
         cost_estimate=cost(35),
         name="token_stage",
-    )(oi, v, s9, s9, k4, rows, tot, wg, wo, nx, hid, go, cols)
+    )(oi, v, s9, k4, rows, tot, wg, wo, nx, hid, go, cols)
 
 
 def early_grad_kernel(dg_ref, r_ref, nx_ref, go_ref, wg_ref, out_ref, dn_ref):
@@ -585,7 +603,7 @@
 
 
 def intra_back_kernel(
-    v_ref, do_ref, rows_ref, st_ref, sa_ref, sb_ref, k4_ref, dv_ref, rc_ref, dk_ref, dos_scr
+    v_ref, do_ref, rows_ref, st_ref, k4_ref, dkc_ref, dv_ref, rc_ref, dk_ref
 ):
     lower, upper = causal_masks()
     kf_cols = jnp.transpose(rows_ref[KF])
@@ -629,20 +647,13 @@
     c_f = k4_ref[NS : 2 * NS, :]
     b_r = k4_ref[2 * NS : 3 * NS, :]
     c_r = k4_ref[3 * NS :, :]
-    for h in range(H):
-        span = slice(h * PS, (h + 1) * PS)
-        grad = do_ref[span, :].astype(f32)
-        dos_scr[span, :BL] = (grad * rows_ref[EF, h : h + 1, :]).astype(bf16)
-        dos_scr[span, BL:] = (grad * rows_ref[ER, h : h + 1, :]).astype(bf16)
-    cross_f = tn(sa_ref[0], dos_scr[:, :BL])
-    cross_r = tn(sb_ref[0], dos_scr[:, BL:])
     dk_ref[:NS, :] = nt(c_f, grad_f)
-    dk_ref[NS : 2 * NS, :] = nn(b_f, grad_f) + cross_f[:NS]
+    dk_ref[NS : 2 * NS, :] = nn(b_f, grad_f) + dkc_ref[:NS, :]
     dk_ref[2 * NS : 3 * NS, :] = nt(c_r, grad_r)
-    dk_ref[3 * NS :, :] = nn(b_r, grad_r) + cross_r[NS:]
-
-
-def intra_back_stage(v, do, rows, scores, s9, k4):
+    dk_ref[3 * NS :, :] = nn(b_r, grad_r) + dkc_ref[NS:, :]
+
+
+def intra_back_stage(v, do, rows, scores, k4, dkc):
     tokens = v.shape[1]
     chan = pl.BlockSpec((CH, BL), lambda b: (0, b))
     return pl.pallas_call(
@@ -653,9 +664,8 @@
             chan,
             pl.BlockSpec((KINDS, H, BL), lambda b: (0, 0, b)),
             pl.BlockSpec((1, BL, BL), lambda b: (b, 0, 0)),
-            pl.BlockSpec((1, CH, BL), lambda b: (b, 0, 0)),
-            pl.BlockSpec((1, CH, BL), lambda b: (b + 1, 0, 0)),
             pl.BlockSpec((4 * NS, BL), lambda b: (0, b)),
+            pl.BlockSpec((2 * NS, BL), lambda b: (0, b)),
         ],
         out_specs=[
             chan,
@@ -667,31 +677,33 @@
             jax.ShapeDtypeStruct((4, H, tokens), f32),
             jax.ShapeDtypeStruct((4 * NS, tokens), f32),
         ),
-        scratch_shapes=[pltpu.VMEM((CH, 2 * BL), bf16)],
         compiler_params=params(),
         cost_estimate=cost(18),
         name="intra_back",
-    )(v, do, rows, scores, s9, s9, k4)
+    )(v, do, rows, scores, k4, dkc)
 
 
 def cross_back_kernel(
-    dvi_ref, v_ref, do_ref, u_ref, dsa_ref, dsb_ref, k4_ref, rows_ref, rci_ref, rcc_ref,
-    xa_ref, xb_ref, dki_ref, cols_ref, after_ref,
+    dvi_ref, v_ref, do_ref, u_ref, ds_ref, k4_ref, rows_ref, rci_ref, rcc_ref,
+    x_ref, dki_ref, cols_ref, after_ref,
     dpre_ref, dx_ref, dk_ref,
-    f_scr, r_scr, lhs_scr, c_scr,
+    cross_scr, lhs_scr, c_scr, wide_scr,
 ):
     b_f = k4_ref[:NS, :]
     b_r = k4_ref[2 * NS : 3 * NS, :]
-    zero = jnp.zeros_like(b_f)
-    f_scr[...] = nn(dsb_ref[0], jnp.concatenate([b_f, zero], axis=0))
-    r_scr[...] = nn(dsa_ref[0], jnp.concatenate([zero, b_r], axis=0))
+
+    @pl.when(pl.program_id(0) == 0)
+    def _():
+        wide_scr[...] = jnp.broadcast_to(cols_ref[:, 1:2], (CH, BL))
+
+    cross_scr[...] = nn(ds_ref[0], stacked_keys(b_f, b_r))
     for h in range(H):
         span = slice(h * PS, (h + 1) * PS)
         vals = v_ref[span, :].astype(f32)
         w_f = rows_ref[WF, h : h + 1, :]
         w_r = rows_ref[WR, h : h + 1, :]
-        dv_f = f_scr[span, :] * w_f
-        dv_r = r_scr[span, :] * w_r
+        dv_f = cross_scr[span, :BL] * w_f
+        dv_r = cross_scr[span, BL:] * w_r
         c_scr[0, h : h + 1, :] = jnp.sum(vals * dv_f, axis=0, keepdims=True)
         c_scr[1, h : h + 1, :] = jnp.sum(vals * dv_r, axis=0, keepdims=True)
         lhs_scr[span, :BL] = (vals * w_f).astype(bf16)
@@ -700,19 +712,18 @@
             dvi_ref[span, :].astype(f32)
             + dv_f
             + dv_r
-            + cols_ref[span, 1:2] * do_ref[span, :].astype(f32)
+            + wide_scr[span, :] * do_ref[span, :].astype(f32)
         )
         pre = u_ref[span, :].astype(f32)
         soft = sigmoid(pre)
         dpre_ref[span, :] = (grad * (soft * (1.0 + pre * (1.0 - soft)))).astype(dpre_ref.dtype)
-    db_f = tn(dsb_ref[0], lhs_scr[:, :BL])
-    db_r = tn(dsa_ref[0], lhs_scr[:, BL:])
+    dkeys = tn(ds_ref[0], lhs_scr[...])
     dk_ref[...] = dki_ref[...]
-    dk_ref[:NS, :] += db_f[:NS]
-    dk_ref[2 * NS : 3 * NS, :] += db_r[NS:]
+    dk_ref[:NS, :] += dkeys[:NS, :BL]
+    dk_ref[2 * NS : 3 * NS, :] += dkeys[NS:, BL:]
     first = lane_first((H, BL))
-    through_f = jnp.sum(jnp.where(first, xb_ref[0], 0.0), axis=1, keepdims=True)
-    through_r = jnp.sum(jnp.where(first, 0.0, xa_ref[0]), axis=1, keepdims=True)
+    through_f = jnp.sum(jnp.where(first, x_ref[0], 0.0), axis=1, keepdims=True)
+    through_r = jnp.sum(jnp.where(first, 0.0, x_ref[0]), axis=1, keepdims=True)
     row_f = rci_ref[0] + rcc_ref[0]
     row_r = rci_ref[1] + rcc_ref[1]
     col_f = rci_ref[2] + c_scr[0]
@@ -744,13 +755,11 @@
             chan,
             chan,
             pl.BlockSpec((1, CH, BL), lambda b: (b, 0, 0)),
-            pl.BlockSpec((1, CH, BL), lambda b: (b + 1, 0, 0)),
             keys,
             pl.BlockSpec((KINDS, H, BL), lambda b: (0, 0, b)),
             pl.BlockSpec((4, H, BL), lambda b: (0, 0, b)),
             pl.BlockSpec((2, H, BL), lambda b: (0, 0, b)),
             pl.BlockSpec((1, H, BL), lambda b: (b, 0, 0)),
-            pl.BlockSpec((1, H, BL), lambda b: (b + 1, 0, 0)),
             keys,
             pl.BlockSpec((CH, 8), lambda b: (0, 0)),
             pl.BlockSpec((BL, BL), lambda b: (0, 0)),
@@ -762,15 +771,15 @@
             jax.ShapeDtypeStruct((4 * NS, tokens), f32),
         ),
         scratch_shapes=[
-            pltpu.VMEM((CH, BL), f32),
-            pltpu.VMEM((CH, BL), f32),
+            pltpu.VMEM((CH, 2 * BL), f32),
             pltpu.VMEM((CH, 2 * BL), bf16),
             pltpu.VMEM((2, H, BL), f32),
+            pltpu.VMEM((CH, BL), f32),
         ],
         compiler_params=params(),
         cost_estimate=cost(16),
         name="cross_back",
-    )(dvi, v, do, u, ds9, ds9, k4, rows, rci, rcc, x9, x9, dki, cols, after)
+    )(dvi, v, do, u, ds9, k4, rows, rci, rcc, x9, dki, cols, after)
 
 
 def key_pre_kernel(dk_ref, u_ref, edge_ref, out_ref):
@@ -799,12 +808,13 @@
 def conv_back_rows(dpre, taps, signal):
     rows, tokens = dpre.shape
     ext = signal.shape[1]
-    wide = jnp.concatenate([dpre, jnp.zeros((rows, ext - tokens), f32)], axis=1)
+    wide = jnp.concatenate([dpre, jnp.zeros((rows, ext - tokens), dpre.dtype)], axis=1)
     total = None
     sums = []
     for k in range(K):
         shift = (k - K // 2) % ext
         moved = wide if shift == 0 else pltpu.roll(wide, shift, axis=1)
+        moved = moved.astype(f32)
         term = moved * taps[:, k : k + 1]
         total = term if total is None else total + term
         prod = moved * signal
@@ -816,14 +826,17 @@
 
 
 def key_back_kernel(
-    meta_ref, dpre_ref, taps_ref, p_ref, nx_ref, w_ref, g_ref, dn_ref, t_ref, low_scr, g_scr
+    meta_ref, dpre_ref, taps_ref, p_ref, nx_ref, w_ref, g_ref, dn_ref, t_ref, low_scr, g_scr, t_scr
 ):
     for c in range(4 * NS // 16):
         span = slice(c * 16, (c + 1) * 16)
         total, sums = conv_back_rows(dpre_ref[span, :], taps_ref[span, :], p_ref[span, :])
         low_scr[span, :] = total.astype(bf16)
         for k in range(K):
-            t_ref[k, span, :] = sums[k]
+            t_scr[k, span, :] = sums[k]
+    for k in range(K):
+        t_ref[k : k + 1, :] = lane_sums(t_scr[k])[:1]
+    t_ref[K : K + 1, :] = jnp.zeros((1, 4 * NS), f32)
     g_scr[...] = nn(low_scr[...], nx_ref[...])
     count, rows, _ = g_ref.shape
     for q in range(count):
@@ -839,7 +852,7 @@
     outs = (
         jax.ShapeDtypeStruct((count, 4 * NS // count, D), bf16),
         jax.ShapeDtypeStruct((ext, D), f32),
-        jax.ShapeDtypeStruct((K, 4 * NS, BL), f32),
+        jax.ShapeDtypeStruct((8, 4 * NS), f32),
     )
 
     def whole(shape):
@@ -852,7 +865,11 @@
             grid=(1,),
             in_specs=[whole(x.shape) for x in args],
             out_specs=[whole(x.shape) for x in outs],
-            scratch_shapes=[pltpu.VMEM((4 * NS, ext), bf16), pltpu.VMEM((4 * NS, D), f32)],
+            scratch_shapes=[
+                pltpu.VMEM((4 * NS, ext), bf16),
+                pltpu.VMEM((4 * NS, D), f32),
+                pltpu.VMEM((K, 4 * NS, BL), f32),
+            ],
         ),
         out_shape=outs,
         compiler_params=params(),
@@ -872,7 +889,7 @@
             src = h * PS + c * 16
             span = slice(src, src + 16)
             total, sums = conv_back_rows(
-                dpre_ref[span, :].astype(f32), taps_ref[span, :], s_ref[span, :].astype(f32)
+                dpre_ref[span, :], taps_ref[span, :], s_ref[span, :].astype(f32)
             )
             low_scr[h * WV + c * 16 : h * WV + (c + 1) * 16, :] = total.astype(bf16)
             for k in range(K):
@@ -887,9 +904,8 @@
         )
         low_scr[h * WV + PS : (h + 1) * WV, :tokens] = tail.astype(bf16)
         low_scr[h * WV + PS : (h + 1) * WV, tokens:] = jnp.zeros((16, ext - tokens), bf16)
-    ones = jnp.ones((8, BL), f32)
     for k in range(K):
-        t_ref[0, k : k + 1, :] = nt(ones, tap_scr[k], lax.Precision.HIGHEST)[:1]
+        t_ref[0, k : k + 1, :] = lane_sums(tap_scr[k])[:1]
     t_ref[0, K : K + 1, :] = jnp.zeros((1, GH * PS), f32)
     g_ref[...] = nn(low_scr[...], nx_ref[...]).reshape(GH, WV, D).astype(g_ref.dtype)
     part = tn(low_scr[...], wv_ref[...].reshape(GH * WV, D))
@@ -1240,7 +1256,7 @@
         far_tot = jnp.stack([x[CH:] for x in messages]).astype(f32)
 
         (s9,) = chain_stage(meta, sblk, tot, far_tot, messages, twist, tokens)
-        hidden_out, result_t, dgate_t, do_t, dsblk, dsdev, rcc, small_mid = token_stage(
+        hidden_out, result_t, dgate_t, do_t, dsblk, dsdev, rcc, dkc, small_mid = token_stage(
             o_intra, v, s9, k4, rows, tot, wg, wo, nx, hidden_in, out_grad, cols
         )
         if direct:
@@ -1249,13 +1265,14 @@
         grad_go, dn_gate = early_grad_stage(dgate_t, result_t, nx, out_grad, wg)
         grad_go = grad_go.reshape(n_mp, per * 2 * PS, D)
         if direct:
+            far_d, grad_go = lax.optimization_barrier((far_d, grad_go))
             got = swap(jnp.stack([grad_go[1], grad_go[3]]), "mp", n_mp, 1)
             away = (grad_go[2].astype(f32) + got[1].astype(f32)).astype(bf16)
             far_go = swap(away, "mp", n_mp, 2)
-            do_back, away, far_d = lax.optimization_barrier((do_t, away, far_d))
+            do_back, away = lax.optimization_barrier((do_t, away))
         else:
             do_back = do_t
-        dvi, rci, dki = intra_back_stage(v, do_back, rows, scores, s9, k4)
+        dvi, rci, dki = intra_back_stage(v, do_back, rows, scores, k4, dkc)
         to_prev = lax.ppermute(dki[NS : 2 * NS, :1].reshape(1, NS), "mp", prevs)
         to_next = lax.ppermute(dki[3 * NS :, tokens - 1 :].reshape(1, NS), "mp", nexts)
         if direct:
@@ -1263,8 +1280,9 @@
         else:
             messages = over_mp(dsdev)
         natural = jnp.arange(n_dp, dtype=jnp.int32)
+        ds9, x9 = chain_stage(meta, dsblk, tot, far_tot, messages, twist, tokens, s9)
         if direct:
-            far_go, dvi = lax.optimization_barrier((far_go, dvi))
+            far_go, ds9, dvi = lax.optimization_barrier((far_go, ds9, dvi))
             mine_go = grad_go[0].astype(f32) + got[0].astype(f32) + far_go.astype(f32)
             mine_go = mine_go.astype(bf16)
         else:
@@ -1277,14 +1295,13 @@
                 *deal_targets(owners, jnp.bitwise_xor(bits, dp_index)),
                 joined=n_dp // 2,
             )
-            keep_go, dvi = lax.optimization_barrier((keep_go, dvi))
+            keep_go, ds9 = lax.optimization_barrier((keep_go, ds9))
             keep_go = keep_go.astype(f32) + swap(send_go, "dp", n_dp, 1).astype(f32)
         else:
             (dealt,) = deal(
                 mine_go.reshape(per, 2 * PS, D), *deal_targets(owners, natural), joined=n_dp
             )
             own_go = lax.psum_scatter(dealt, "dp", scatter_dimension=0, tiled=True)[0]
-        ds9, x9 = chain_stage(meta, dsblk, tot, far_tot, messages, twist, tokens, s9)
         dpre, dx, dk = cross_back_stage(
             dvi, v, do_t, u, ds9, k4, rows, rci, rcc, x9, dki, cols, after
         )
@@ -1298,10 +1315,21 @@
         dpre_k = key_pre_stage(dk, key_u, edge)
         grad_v, dn_value, tap_v = value_back_stage(dpre, taps_v, s, dx, nx, wv)
         if direct:
-            far_go, dpre_k, dn_value = lax.optimization_barrier((far_go, dpre_k, dn_value))
+            far_go, grad_v = lax.optimization_barrier((far_go, grad_v))
             keep_go = keep_go[:2] + far_go.astype(f32)
-            own_go = keep_go[0] + swap(keep_go[1].astype(bf16), "dp", n_dp, 2).astype(f32)
+            last_go = swap(keep_go[1].astype(bf16), "dp", n_dp, 2)
+            both = grad_v.reshape(n_mp, per * WV, D)
+            got_v = swap(jnp.stack([both[1], both[3]]), "mp", n_mp, 1)
+            away_v = (both[2].astype(f32) + got_v[1].astype(f32)).astype(bf16)
+            away_v, dpre_k = lax.optimization_barrier((away_v, dpre_k))
+            far_v = swap(away_v, "mp", n_mp, 2)
         grad_key, dn_key, tap_key = key_back_stage(meta, dpre_k, taps_k, key_proj, nx, key_low)
+        if direct:
+            far_v, last_go, grad_key, dn_key, tap_key = lax.optimization_barrier(
+                (far_v, last_go, grad_key, dn_key, tap_key)
+            )
+            own_go = keep_go[0] + last_go.astype(f32)
+
         head_grad = jnp.concatenate(
             [
                 small_mid[0, 0].reshape(H, 1, PS),
@@ -1318,7 +1346,7 @@
         if direct:
             head_grad = jnp.take(head_grad.reshape(n_mp, per, 10, PS), order, axis=0)
         small_grad = jnp.concatenate(
-            [head_grad.reshape(-1), jnp.sum(tap_key, axis=2).reshape(-1)]
+            [head_grad.reshape(-1), tap_key[:K].reshape(-1)]
         )
         count = small_grad.shape[0]
 
@@ -1326,16 +1354,15 @@
             rows_key = (4 * NS) // (n_mp * n_dp)
             small_rows = jnp.pad(small_grad, (0, n_mp * n_dp * D - count)).reshape(n_mp, n_dp, D)
             small_rows = jnp.take(small_rows, order, axis=0).astype(bf16)
-            both = jnp.concatenate([grad_v.reshape(n_mp, per * WV, D), grad_key, small_rows], axis=1)
-            mine_v = scatter_mp(both)
-            mine_v, own_go = lax.optimization_barrier((mine_v, own_go))
+            extra = scatter_mp(jnp.concatenate([grad_key, small_rows], axis=1))
+            mine_v = both[0].astype(f32) + got_v[0].astype(f32) + far_v.astype(f32)
             targets = jnp.bitwise_xor(natural, dp_index)
             dealt = deal(
-                mine_v[: per * WV].astype(bf16).reshape(per, WV, D),
+                mine_v.astype(bf16).reshape(per, WV, D),
                 *deal_targets(owners, targets),
                 targets,
-                mine_v[per * WV : per * WV + n_dp * rows_key],
-                mine_v[per * WV + n_dp * rows_key :],
+                extra[: n_dp * rows_key],
+                extra[n_dp * rows_key :],
             )
             own_v = dealt[0].astype(f32)
             for k in range(1, n_dp):
@@ -1349,13 +1376,13 @@
             )
             own_v = lax.psum_scatter(dealt, "dp", scatter_dimension=0, tiled=True)[0].astype(f32)
 
-        dn_ext = dn_key + dn_value
-        halo_l = lax.ppermute(dn_ext[tokens : tokens + HALO], "mp", nexts)
-        halo_r = lax.ppermute(dn_ext[-HALO:], "mp", prevs)
+        right_halo = slice(tokens, tokens + HALO)
+        halo_l = lax.ppermute(dn_key[right_halo] + dn_value[right_halo], "mp", nexts)
+        halo_r = lax.ppermute(dn_key[-HALO:] + dn_value[-HALO:], "mp", prevs)
         halo_l = jnp.where(starts, 0.0, halo_l)
         halo_r = jnp.where(ends, 0.0, halo_r)
         edges = jnp.concatenate([halo_l, jnp.zeros((tokens - 2 * HALO, D), f32), halo_r], axis=0)
-        dnormed = dn_gate + dn_ext[:tokens] + edges
+        dnormed = dn_gate + dn_key[:tokens] + dn_value[:tokens] + edges
         scaled = dnormed * gain_in
         gain_grad = jnp.sum(dnormed * hidden * scale_in, axis=0)
         cross_in = jnp.sum(scaled * hidden, axis=1, keepdims=True)
@@ -1363,12 +1390,29 @@
             out_grad.astype(f32) + scale_in * scaled - hidden * scale_in**3 * cross_in / D
         )
 
+        own_v = lax.optimization_barrier(own_v)
+        own_go = own_go.astype(f32)
+        own_grad = jnp.concatenate([own_go[:PS], own_v[: PS + 2], own_go[PS:]], axis=0)
+        own_grad = lax.optimization_barrier(own_grad.reshape(3 * PS + 2, 1, D))
+        previous = [
+            jnp.transpose(x[0], (2, 0, 1))
+            for x in (block_master, block_first, block_second, block_ema)
+        ]
+        slot_new = adamw_update(
+            previous[0], own_grad, previous[1], previous[2], previous[3], MATRIX_RATE
+        )
+        is_owner = jnp.any(owners == dp_index)
+        slot_outs = [
+            jnp.transpose(jnp.where(is_owner, renewed, before), (1, 2, 0))[None]
+            for renewed, before in zip(slot_new, previous)
+        ]
         if direct:
             share = jnp.concatenate(
                 [jnp.broadcast_to(gain_grad, (15 - rows_key, D)), own_v[WV - rows_key - 1 :]],
                 axis=0,
             ).astype(bf16)
             shares, code = gather_all(share, mp_index, dp_index)
+            shares, slot_outs = lax.optimization_barrier((shares, slot_outs))
             *key_new, small_total, gain_total = finish_stage(
                 code, shares, bc_weight, bc_first, bc_second, bc_ema
             )
@@ -1381,20 +1425,6 @@
             key_new = adamw_update(
                 bc_weight, jnp.transpose(key_total), bc_first, bc_second, bc_ema, MATRIX_RATE
             )
-        own_go = own_go.astype(f32)
-        own_grad = jnp.transpose(
-            jnp.concatenate([own_go[:PS], own_v[: PS + 2], own_go[PS:]], axis=0)
-        )
-        own_grad = lax.optimization_barrier(own_grad)
-        is_owner = jnp.any(owners == dp_index)
-        previous = (block_master[0, 0], block_first[0, 0], block_second[0, 0], block_ema[0, 0])
-        slot_new = adamw_update(
-            previous[0], own_grad, previous[1], previous[2], previous[3], MATRIX_RATE
-        )
-        slot_outs = [
-            jnp.where(is_owner, renewed, before)[None, None]
-            for renewed, before in zip(slot_new, previous)
-        ]
         head_total = lax.dynamic_slice_in_dim(
             small_total[: H * 10 * PS].reshape(H, 10, PS), mp_index * per, per
         )

time: 460 us -> 413 us (0.90)
  waiting for transfers between devices: 90.6 us -> 57.5 us
  Pallas kernels: 203 us -> 190 us
    ppermute x38 -> x40, waiting for transfers between devices: 71.7 us -> 55.2 us  [swap(): return lax.ppermute(x, axis, [(i, i ^ bit) for i in range(size)])]
    ppermute x2, waiting for transfers between devices: 16.4 us -> 0.01 us  [the longest x1 0.01 us: local(): halo_r = lax.ppermute(dn_key[-HALO:] + dn_value[-HALO:], 'mp', prevs)]
    pallas_call x1, Pallas kernels: 26.6 us -> 19.3 us  [value_stage(): pl.pallas_call(value_kernel, grid=(NG,), in_specs=[pl.BlockSpec((ext, D),...]
    convert_element_type x0 -> x2, other arithmetic: none -> 4.77 us  [the longest x1 2.62 us: local(): mine_v.astype(bf16).reshape(per, WV, D)]
    ppermute x38 -> x40, starting transfers between devices: 47.9 us -> 47 us  [swap(): return lax.ppermute(x, axis, [(i, i ^ bit) for i in range(size)])]
    unnamed x115 -> x111, local copies, waits for them, and re-layouts: 13 us -> 13.9 us
  transfers between devices with their start and end apart: 45 -> 47, of which waited for: 14 -> 15; matrix products, arithmetic and copies ran while one was open for 12% -> 12% of each run, Pallas kernels for 28% -> 35%
where the time goes in v2:
time: 413 us; the launch traced here: 406 us
  Pallas kernels  190 us (46%)
  starting transfers between devices  64.9 us (16%)
  waiting for transfers between devices  57.5 us (14%)
  other arithmetic  43.2 us (10%)
  local copies, waits for them, and re-layouts  34.3 us (8%)
  between operations  16.3 us (4%)
    ppermute x40, waiting for transfers between devices, swap(): return lax.ppermute(x, axis, [(i, i ^ bit) for i in range(size)])  55.2 us
    ppermute x40, starting transfers between devices, swap(): return lax.ppermute(x, axis, [(i, i ^ bit) for i in range(size)])  47 us
    pallas_call x1, Pallas kernels, token_stage(): pl.pallas_call(token_kernel, grid=(blocks,), in_specs=[chan, chan, pl.Blo...  34.9 us
    pallas_call x1, Pallas kernels, value_back_stage(): pl.pallas_call(value_back_kernel, grid=(NG,), in_specs=[pl.BlockSpec((row...  26.5 us
    pallas_call x1, Pallas kernels, value_stage(): pl.pallas_call(value_kernel, grid=(NG,), in_specs=[pl.BlockSpec((ext, D),...  19.3 us
    pallas_call x1, Pallas kernels, intra_back_stage(): pl.pallas_call(intra_back_kernel, grid=(tokens // BL,), in_specs=[chan, c...  15.6 us
    pallas_call x1, Pallas kernels, cross_back_stage(): pl.pallas_call(cross_back_kernel, grid=(tokens // BL,), in_specs=[chan, c...  15.4 us
    pallas_call x2, Pallas kernels, chain_stage(): pl.pallas_call(body, grid_spec=pltpu.PrefetchScalarGridSpec(num_scalar_pr...  14.4 us
  transfers between devices with their start and end apart: 47, of which 15 were waited for; matrix products, arithmetic and copies ran while one was open for 12% of the time, Pallas kernels for 35%

profile of v2, /device:TPU:1, one launch (start us, length us, event | category | flops | bytes accessed | tf_op | source)
XLA Modules:
  0.0 406.1 jit_solution(15295783118025241972)
XLA Ops:
  17.3 4.8 %collective-permute-start.1 = (bf16[8,768]{1,0:T(8,128)(2,1)S(1)}, bf16[8,768]{1,0:T(8,128)(2,1)S(1)}, u32[]{:S(2)}, u32[]{:S(2)}) collective-permute-start(bf16[8,768]{1,0:T(8,128)(2,1)S(1)} %get-tuple-element.328), channel_id=1, source_target_pairs={{0,1},{1,2},{2,3},{4,5},{5,6},{6,7},{8,9},{9,10},{10,11},{12,13},{... | collective-permute-start | bytes 36872 | tf_op jit(solution)/shard_map/ppermute | solution.py:1212
  30.4 3.3 collective-permute-start.7
  37.2 7.9 %collective-permute-done.6 = bf16[80,768]{1,0:T(8,128)(2,1)S(1)} collective-permute-done((bf16[80,768]{1,0:T(8,128)(2,1)}, bf16[80,768]{1,0:T(8,128)(2,1)S(1)}, u32[]{:S(2)}, u32[]{:S(2)}) %collective-permute-start.6) | collective-permute-done | bytes 122912 | tf_op jit(solution)/shard_map/ppermute | solution.py:1125
  45.9 3.2 pick.1
  52.0 6.2 %key_stage.1 = (f32[256,1152]{1,0:T(8,128)}, f32[256,1024]{1,0:T(8,128)}, bf16[256,1024]{1,0:T(8,128)(2,1)}, f32[8,128,128]{2,1,0:T(8,128)}) custom-call(bf16[1152,768]{1,0:T(8,128)(2,1)} %pad_maximum_fusion.2.nx_ref, bf16[256,768]{1,0:T(8,128)(2,1)} %bitcast.173, f32[256,8]{1,0:T(8,128)} %pad.21.taps_ref), custom_call_target="tpu_custom_call" | custom-call | bytes 6000000 | tf_op jit(solution)/shard_map/key_stage/pallas_call | solution.py:125
  58.4 11.1 %collective-permute-done.10 = bf16[6,80,768]{2,1,0:T(8,128)(2,1)S(1)} collective-permute-done((bf16[6,80,768]{2,1,0:T(8,128)(2,1)}, bf16[6,80,768]{2,1,0:T(8,128)(2,1)S(1)}, u32[]{:S(2)}, u32[]{:S(2)}) %collective-permute-start.10) | collective-permute-done | bytes 737312 | tf_op jit(solution)/shard_map/ppermute | solution.py:1125
  74.0 3.3 pad_maximum_fusion.wv_ref
  77.3 19.3 %value_stage.1 = (bf16[1536,1024]{1,0:T(8,128)(2,1)}, bf16[1536,1024]{1,0:T(8,128)(2,1)}, bf16[1536,1152]{1,0:T(8,128)(2,1)}, f32[12,24,1024]{2,1,0:T(8,128)}, f...) custom-call(bf16[1152,768]{1,0:T(8,128)(2,1)} %pad_maximum_fusion.2.nx_ref,, ...), custom_call_target="tpu_custom_call" | custom-call | bytes 27000000 | tf_op jit(solution)/shard_map/value_stage/pallas_call | solution.py:223
  100.4 11.9 %intra_stage.1.oi_ref = bf16[1536,1024]{1,0:T(8,128)(2,1)} custom-call(bf16[1536,1024]{1,0:T(8,128)(2,1)} %get-tuple-element.109.v_ref, f32[12,24,1024]{2,1,0:T(8,128)} %get-tuple-element.110.rows_ref, f32[8,128,128]{2,1,0:T(8,128)} %get-tuple-element.111.st_ref), custom_call_target="tpu_custom_call" | custom-call | bytes 12000000 | tf_op jit(solution)/shard_map/intra_stage/pallas_call | solution.py:393
  115.0 6.6 %chain_stage.1.s_ref.refs_8_ = bf16[9,1536,128]{2,1,0:T(8,128)(2,1)} custom-call(s32[6]{0:T(128)} %pad_add_fusion.refs_0_.meta_ref, bf16[8,1536,128]{2,1,0:T(8,128)(2,1)} %get-tuple-element.113.refs_1_, f32[8,24,128]{2,1,0:T(8,128)} %get-tuple-element.114.refs_2_.tot_ref, f32[4,72,128]{2,1,0:T(8,128)} %maximum_convert_fusion.refs_3_, ...), custom_call_target="tpu_custom_call" | custom-call | bytes 7000000 | tf_op jit(solution)/shard_map/chain_stage/pallas_call | solution.py:349
  121.6 5.9 %pick_two.1 = (bf16[24,64,768]{2,1,0:T(8,128)(2,1)}, bf16[24,64,768]{2,1,0:T(8,128)(2,1)}) custom-call(s32[24]{0:T(128)} %fusion.43.index_ref, bf16[32,128,768]{2,1,0:T(8,128)(2,1)} %bitcast.168), custom_call_target="tpu_custom_call" | custom-call | bytes 6000000 | tf_op jit(solution)/shard_map/pick_two/pallas_call | solution.py:998
  127.4 34.9 %token_stage.1 = (bf16[1024,768]{1,0:T(8,128)(2,1)}, bf16[1536,1024]{1,0:T(8,128)(2,1)}, bf16[1536,1024]{1,0:T(8,128)(2,1)}, bf16[1536,1024]{1,0:T(8,128)(2,1)},...) custom-call(bf16[1536,1024]{1,0:T(8,128)(2,1)} %intra_stage.1.oi_ref, ...), custom_call_target="tpu_custom_call" | custom-call | bytes 35000000 | tf_op jit(solution)/shard_map/token_stage/pallas_call | solution.py:511
  164.0 14.0 %early_grad.1 = (bf16[24,128,768]{2,1,0:T(8,128)(2,1)}, f32[1024,768]{1,0:T(8,128)}) custom-call(bf16[1536,1024]{1,0:T(8,128)(2,1)} %get-tuple-element.119.dg_ref, bf16[1536,1024]{1,0:T(8,128)(2,1)} %get-tuple-element.120.r_ref, bf16[1152,768]{1,0:T(8,128)(2,1)} %pad_maximum_fusion.2.nx_ref, bf16[1024,768]{1,0:T(8,128)(2,1)} %go_ref.3, ...), custom_call_target="tpu_custom_call" | custom-call | bytes 12000000 | tf_op jit(solution)/shard_map/early_grad/pallas_call | solution.py:581
  181.2 4.2 %collective-permute-done.19 = bf16[2,768,768]{2,1,0:T(8,128)(2,1)S(1)} collective-permute-done((bf16[2,768,768]{2,1,0:T(8,128)(2,1)S(1)}, bf16[2,768,768]{2,1,0:T(8,128)(2,1)S(1)}, u32[]{:S(2)}, u32[]{:S(2)}) %collective-permute-start.19) | collective-permute-done | bytes 2359328 | tf_op jit(solution)/shard_map/ppermute | solution.py:1125
  190.3 7.9 %chain_back.1 = (bf16[8,1536,128]{2,1,0:T(8,128)(2,1)}, f32[8,24,128]{2,1,0:T(8,128)}) custom-call(s32[6]{0:T(128)} %pad_add_fusion.refs_0_.meta_ref, bf16[8,1536,128]{2,1,0:T(8,128)(2,1)} %get-tuple-element.126.refs_1_, f32[8,24,128]{2,1,0:T(8,128)} %get-tuple-element.114.refs_2_.tot_ref, f32[4,72,128]{2,1,0:T(8,128)} %maximum_convert_fusion.refs_3_, ...), custom_call_target="tpu_custom_call" | custom-call | bytes 7000000 | tf_op jit(solution)/shard_map/chain_back/pallas_call | solution.py:349
  198.2 15.6 %intra_back.1 = (bf16[1536,1024]{1,0:T(8,128)(2,1)}, f32[4,24,1024]{2,1,0:T(8,128)}, f32[256,1024]{1,0:T(8,128)}) custom-call(bf16[1536,1024]{1,0:T(8,128)(2,1)} %get-tuple-element.109.v_ref, bf16[1536,1024]{1,0:T(8,128)(2,1)} %get-tuple-element.130.do_ref, f32[12,24,1024]{2,1,0:T(8,128)} %get-tuple-element.110.rows_ref, ...), custom_call_target="tpu_custom_call" | custom-call | bytes 18000000 | tf_op jit(solution)/shard_map/intra_back/pallas_call | solution.py:659
  216.6 3.2 deal.2
  221.9 15.4 %cross_back.1 = (bf16[1536,1024]{1,0:T(8,128)(2,1)}, f32[2,24,1024]{2,1,0:T(8,128)}, f32[256,1024]{1,0:T(8,128)}) custom-call(bf16[1536,1024]{1,0:T(8,128)(2,1)} %get-tuple-element.138.dvi_ref, bf16[1536,1024]{1,0:T(8,128)(2,1)} %get-tuple-element.109.v_ref, bf16[1536,1024]{1,0:T(8,128)(2,1)} %get-tuple-element.130.do_ref, ...), custom_call_target="tpu_custom_call" | custom-call | bytes 16000000 | tf_op jit(solution)/shard_map/cross_back/pallas_call | solution.py:749
  238.9 6.5 %collective-permute-start.24 = (bf16[2,128,768]{2,1,0:T(8,128)(2,1)S(1)}, bf16[2,128,768]{2,1,0:T(8,128)(2,1)S(1)}, u32[]{:S(2)}, u32[]{:S(2)}) collective-permute-start(bf16[2,128,768]{2,1,0:T(8,128)(2,1)S(1)} %slice.354), channel_id=1, source_target_pairs={{0,16},{4,20},{8,24},{12,28},{16,0},{20,4},{24,8},{28,12},{1,17},{... | collective-permute-start | bytes 1179656 | tf_op jit(solution)/shard_map/ppermute | solution.py:1125
  245.5 26.5 %value_back.1 = (bf16[24,80,768]{2,1,0:T(8,128)(2,1)}, f32[1152,768]{1,0:T(8,128)}, f32[3,8,512]{2,1,0:T(8,128)}) custom-call(bf16[1536,1024]{1,0:T(8,128)(2,1)} %get-tuple-element.148.dpre_ref, f32[1536,8]{1,0:T(8,128)} %pad.22.taps_ref, bf16[1536,1152]{1,0:T(8,128)(2,1)} %get-tuple-element.149.s_ref, f32[2,24,1024]{2,1,0:T(8,128)} %get-tuple-element.150.dx_ref, ...), custom_call_target="tpu_custom_call" | custom-call | bytes 27000000 | tf_op jit(solution)/shard_map/value_back/pallas_call | solution.py:926
  281.7 3.5 collective-permute-start.27
  292.6 3.1 key_pre.1.dpre_ref
  298.2 8.3 %key_back.1 = (bf16[4,64,768]{2,1,0:T(8,128)(2,1)}, f32[1152,768]{1,0:T(8,128)}, f32[8,256]{1,0:T(8,128)}) custom-call(s32[6]{0:T(128)} %pad_add_fusion.refs_0_.meta_ref, f32[256,1024]{1,0:T(8,128)} %key_pre.1.dpre_ref, f32[256,8]{1,0:T(8,128)} %pad.21.taps_ref, f32[256,1152]{1,0:T(8,128)} %get-tuple-element.158.p_ref, ...), custom_call_target="tpu_custom_call" | custom-call | bytes 8000000 | tf_op jit(solution)/shard_map/key_back/pallas_call | solution.py:861
  306.6 8.7 %collective-permute-done.28 = bf16[480,768]{1,0:T(8,128)(2,1)} collective-permute-done((bf16[480,768]{1,0:T(8,128)(2,1)}, bf16[480,768]{1,0:T(8,128)(2,1)}, u32[]{:S(2)}, u32[]{:S(2)}) %collective-permute-start.28) | collective-permute-done | bytes 737312 | tf_op jit(solution)/shard_map/ppermute | solution.py:1125
  318.0 3.9 collective-permute-start.30
  345.7 4.1 %fusion.8 = (bf16[768]{0:T(1024)(128)(2,1)S(1)}, f32[1024]{0:T(1024)S(1)}, f32[1024,768]{1,0:T(8,128)S(1)}) fusion(bf16[1024,768]{1,0:T(8,128)(2,1)S(1)} %copy-done.2, f32[1024]{0:T(1024)S(1)} %get-tuple-element.356, f32[768]{0:T(1024)S(1)} %mul.247, f32[8,768]{1,0:T(8,128)S(1)} %broadcast_select_fusion.1, f32[1024]{0:T(1024)S(1)} %pad.60.clone, ...), kind=kLoop, calls=%fused_computation.16 | loop fusion | flops 9435392 | bytes 14221824 | tf_op jit(solution)/shard_map/reduce_sum | solution.py:1387
  349.8 4.9 %collective-permute-done.38 = bf16[80,768]{1,0:T(8,128)(2,1)S(1)} collective-permute-done((bf16[80,768]{1,0:T(8,128)(2,1)}, bf16[80,768]{1,0:T(8,128)(2,1)S(1)}, u32[]{:S(2)}, u32[]{:S(2)}) %collective-permute-start.38) | collective-permute-done | bytes 122912 | tf_op jit(solution)/shard_map/ppermute | solution.py:1125
  354.7 3.2 collective-permute-done.37
  365.0 3.4 collective-permute-done.43
  369.9 3.1 collective-permute-done.44
  373.0 7.7 %collective-permute-start.45 = (bf16[16,16,768]{2,1,0:T(8,128)(2,1)S(1)}, bf16[16,16,768]{2,1,0:T(8,128)(2,1)S(1)}, u32[]{:S(2)}, u32[]{:S(2)}) collective-permute-start(bf16[16,16,768]{2,1,0:T(8,128)(2,1)S(1)} %get-tuple-element.337), channel_id=1, source_target_pairs={{0,1},{1,0},{2,3},{3,2},{4,5},{5,4},{6,7},{7,6},{8,9},{9,8},{10,11... | collective-permute-start | bytes 1179656 | tf_op jit(solution)/shard_map/ppermute | solution.py:1125
  383.6 5.2 %finish_stage.1 = (f32[768,256]{1,0:T(8,128)}, f32[768,256]{1,0:T(8,128)}, f32[768,256]{1,0:T(8,128)}, f32[768,256]{1,0:T(8,128)}, f32[32,768]{1,0:T(8,128)}, /*index=5*/f32[8,768]{1,0:T(8,128)}) custom-call(s32[32]{0:T(128)} %add.354.code_ref, bf16[32,16,768]{2,1,0:T(8,128)(2,1)} %copy-done.10, f32[768,256]{1,0:T(8,128)} %w_ref.1, f32[768,256]{1,0:T(8,128)} %m_ref.1, ...), custom_call_target="tpu_custom_call" | custom-call | bytes 5000000 | tf_op jit(solution)/shard_map/finish_stage/pallas_call | solution.py:1104
  (333 shorter events, 119.2 us)
Async XLA Ops:
  7.2 114.4 %all-gather.3.cloned.1.call-start = ((), (), s32[]{:S(2)}) async-start(), calls=%async_computation | async-start | bytes 6488064 | tf_op jit(solution)/shard_map/all_gather | solution.py:1194
  9.9 20.4 %collective-permute-start.2 = (bf16[80,768]{1,0:T(8,128)(2,1)}, bf16[80,768]{1,0:T(8,128)(2,1)S(1)}, u32[]{:S(2)}, u32[]{:S(2)}) collective-permute-start(bf16[80,768]{1,0:T(8,128)(2,1)} %get-tuple-element.341), channel_id=1, source_target_pairs={{0,4},{4,0},{8,12},{12,8},{16,20},{20,16},{24,28},{28,24},{1,5},{5... | collective-permute-start | bytes 368648 | tf_op jit(solution)/shard_map/ppermute | solution.py:1125
  12.0 21.7 %collective-permute-start.3 = (bf16[80,768]{1,0:T(8,128)(2,1)}, bf16[80,768]{1,0:T(8,128)(2,1)S(1)}, u32[]{:S(2)}, u32[]{:S(2)}) collective-permute-start(bf16[80,768]{1,0:T(8,128)(2,1)} %get-tuple-element.341), channel_id=1, source_target_pairs={{0,8},{4,12},{8,0},{12,4},{16,24},{20,28},{24,16},{28,20},{1,9},{5... | collective-permute-start | bytes 368648 | tf_op jit(solution)/shard_map/ppermute | solution.py:1125
  13.3 20.4 %collective-permute-start.4 = (bf16[80,768]{1,0:T(8,128)(2,1)}, bf16[80,768]{1,0:T(8,128)(2,1)}, u32[]{:S(2)}, u32[]{:S(2)}) collective-permute-start(bf16[80,768]{1,0:T(8,128)(2,1)} %get-tuple-element.341), channel_id=1, source_target_pairs={{0,12},{4,8},{8,4},{12,0},{16,28},{20,24},{24,20},{28,16},{1,13},{... | collective-permute-start | bytes 368648 | tf_op jit(solution)/shard_map/ppermute | solution.py:1125
  13.3 23.0 %collective-permute-start.5 = (bf16[80,768]{1,0:T(8,128)(2,1)}, bf16[80,768]{1,0:T(8,128)(2,1)}, u32[]{:S(2)}, u32[]{:S(2)}) collective-permute-start(bf16[80,768]{1,0:T(8,128)(2,1)} %get-tuple-element.341), channel_id=1, source_target_pairs={{0,16},{4,20},{8,24},{12,28},{16,0},{20,4},{24,8},{28,12},{1,17},{... | collective-permute-start | bytes 368648 | tf_op jit(solution)/shard_map/ppermute | solution.py:1125
  17.3 12.0 %collective-permute-start.1 = (bf16[8,768]{1,0:T(8,128)(2,1)S(1)}, bf16[8,768]{1,0:T(8,128)(2,1)S(1)}, u32[]{:S(2)}, u32[]{:S(2)}) collective-permute-start(bf16[8,768]{1,0:T(8,128)(2,1)S(1)} %get-tuple-element.328), channel_id=1, source_target_pairs={{0,1},{1,2},{2,3},{4,5},{5,6},{6,7},{8,9},{9,10},{10,11},{12,13},{... | collective-permute-start | bytes 36872 | tf_op jit(solution)/shard_map/ppermute | solution.py:1212
  29.4 15.8 %collective-permute-start.6 = (bf16[80,768]{1,0:T(8,128)(2,1)}, bf16[80,768]{1,0:T(8,128)(2,1)S(1)}, u32[]{:S(2)}, u32[]{:S(2)}) collective-permute-start(bf16[80,768]{1,0:T(8,128)(2,1)} %get-tuple-element.341), channel_id=1, source_target_pairs={{0,20},{4,16},{8,28},{12,24},{16,4},{20,0},{24,12},{28,8},{1,21},{... | collective-permute-start | bytes 368648 | tf_op jit(solution)/shard_map/ppermute | solution.py:1125
  30.4 14.8 %collective-permute-start.7 = (bf16[80,768]{1,0:T(8,128)(2,1)}, bf16[80,768]{1,0:T(8,128)(2,1)S(1)}, u32[]{:S(2)}, u32[]{:S(2)}) collective-permute-start(bf16[80,768]{1,0:T(8,128)(2,1)} %get-tuple-element.341), channel_id=1, source_target_pairs={{0,24},{4,28},{8,16},{12,20},{16,8},{20,12},{24,0},{28,4},{1,25},{... | collective-permute-start | bytes 368648 | tf_op jit(solution)/shard_map/ppermute | solution.py:1125
  33.7 11.5 %collective-permute-start.8 = (bf16[80,768]{1,0:T(8,128)(2,1)}, bf16[80,768]{1,0:T(8,128)(2,1)S(1)}, u32[]{:S(2)}, u32[]{:S(2)}) collective-permute-start(bf16[80,768]{1,0:T(8,128)(2,1)} %get-tuple-element.341), channel_id=1, source_target_pairs={{0,28},{4,24},{8,20},{12,16},{16,12},{20,8},{24,4},{28,0},{1,29},{... | collective-permute-start | bytes 368648 | tf_op jit(solution)/shard_map/ppermute | solution.py:1125
  33.7 16.0 %collective-permute-start = (bf16[8,768]{1,0:T(8,128)(2,1)S(1)}, bf16[8,768]{1,0:T(8,128)(2,1)S(1)}, u32[]{:S(2)}, u32[]{:S(2)}) collective-permute-start(bf16[8,768]{1,0:T(8,128)(2,1)S(1)} %get-tuple-element.327), channel_id=1, source_target_pairs={{1,0},{2,1},{3,2},{5,4},{6,5},{7,6},{9,8},{10,9},{11,10},{13,12},{... | collective-permute-start | bytes 36872 | tf_op jit(solution)/shard_map/ppermute | solution.py:1213
  36.3 34.5 %collective-permute-start.13 = (f32[6,10,64]{2,0,1:T(8,128)S(1)}, f32[6,10,64]{2,0,1:T(8,128)S(1)}, u32[]{:S(2)}, u32[]{:S(2)}) collective-permute-start(f32[6,10,64]{2,0,1:T(8,128)S(1)} %copy-done.13), channel_id=1, source_target_pairs={{0,2},{1,3},{2,0},{3,1},{4,6},{5,7},{6,4},{7,5},{8,10},{9,11},{10,... | collective-permute-start | bytes 46088 | tf_op jit(solution)/shard_map/ppermute | solution.py:1125
  45.1 26.3 %collective-permute-start.12 = (f32[6,10,64]{2,0,1:T(8,128)S(1)}, f32[6,10,64]{2,0,1:T(8,128)S(1)}, u32[]{:S(2)}, u32[]{:S(2)}) collective-permute-start(f32[6,10,64]{2,0,1:T(8,128)S(1)} %copy-done.13), channel_id=1, source_target_pairs={{0,1},{1,0},{2,3},{3,2},{4,5},{5,4},{6,7},{7,6},{8,9},{9,8},{10,11... | collective-permute-start | bytes 46088 | tf_op jit(solution)/shard_map/ppermute | solution.py:1125
  49.1 20.4 %collective-permute-start.10 = (bf16[6,80,768]{2,1,0:T(8,128)(2,1)}, bf16[6,80,768]{2,1,0:T(8,128)(2,1)S(1)}, u32[]{:S(2)}, u32[]{:S(2)}) collective-permute-start(bf16[6,80,768]{2,1,0:T(8,128)(2,1)} %pick.1), channel_id=1, source_target_pairs={{0,2},{1,3},{2,0},{3,1},{4,6},{5,7},{6,4},{7,5},{8,10},{9,11},{10,... | collective-permute-start | bytes 2211848 | tf_op jit(solution)/shard_map/ppermute | solution.py:1125
  58.2 15.8 %collective-permute-start.9 = (bf16[6,80,768]{2,1,0:T(8,128)(2,1)S(1)}, bf16[6,80,768]{2,1,0:T(8,128)(2,1)S(1)}, u32[]{:S(2)}, u32[]{:S(2)}) collective-permute-start(bf16[6,80,768]{2,1,0:T(8,128)(2,1)S(1)} %copy-done.8), channel_id=1, source_target_pairs={{0,1},{1,0},{2,3},{3,2},{4,5},{5,4},{6,7},{7,6},{8,9},{9,8},{10,11... | collective-permute-start | bytes 2211848 | tf_op jit(solution)/shard_map/ppermute | solution.py:1125
  98.3 14.0 %collective-permute-start.15 = (bf16[1608,128]{1,0:T(8,128)(2,1)S(1)}, bf16[1608,128]{1,0:T(8,128)(2,1)S(1)}, u32[]{:S(2)}, u32[]{:S(2)}) collective-permute-start(bf16[1608,128]{1,0:T(8,128)(2,1)S(1)} %pad_maximum_fusion.4.refs_4_), channel_id=1, source_target_pairs={{0,2},{1,3},{2,0},{3,1},{4,6},{5,7},{6,4},{7,5},{8,10},{9,11},{10,... | collective-permute-start | bytes 1234952 | tf_op jit(solution)/shard_map/ppermute | solution.py:1125
  98.7 13.8 %collective-permute-start.16 = (bf16[1608,128]{1,0:T(8,128)(2,1)S(1)}, bf16[1608,128]{1,0:T(8,128)(2,1)S(1)}, u32[]{:S(2)}, u32[]{:S(2)}) collective-permute-start(bf16[1608,128]{1,0:T(8,128)(2,1)S(1)} %pad_maximum_fusion.4.refs_4_), channel_id=1, source_target_pairs={{0,1},{1,0},{2,3},{3,2},{4,5},{5,4},{6,7},{7,6},{8,9},{9,8},{10,11... | collective-permute-start | bytes 1234952 | tf_op jit(solution)/shard_map/ppermute | solution.py:1125
  162.3 15.6 %collective-permute-start.18 = (bf16[1536,128]{1,0:T(8,128)(2,1)}, bf16[1536,128]{1,0:T(8,128)(2,1)S(1)}, u32[]{:S(2)}, u32[]{:S(2)}) collective-permute-start(bf16[1536,128]{1,0:T(8,128)(2,1)} %get-tuple-element.123.refs_4_), channel_id=1, source_target_pairs={{0,2},{1,3},{2,0},{3,1},{4,6},{5,7},{6,4},{7,5},{8,10},{9,11},{10,... | collective-permute-start | bytes 1179656 | tf_op jit(solution)/shard_map/ppermute | solution.py:1125
  185.7 28.2 %collective-permute-start.20 = (bf16[768,768]{1,0:T(8,128)(2,1)S(1)}, bf16[768,768]{1,0:T(8,128)(2,1)}, u32[]{:S(2)}, u32[]{:S(2)}) collective-permute-start(bf16[768,768]{1,0:T(8,128)(2,1)S(1)} %fusion.13), channel_id=1, source_target_pairs={{0,2},{1,3},{2,0},{3,1},{4,6},{5,7},{6,4},{7,5},{8,10},{9,11},{10,... | collective-permute-start | bytes 3538952 | tf_op jit(solution)/shard_map/ppermute | solution.py:1125
  219.8 18.9 %collective-permute-start.23 = (bf16[4,128,768]{2,1,0:T(8,128)(2,1)}, bf16[4,128,768]{2,1,0:T(8,128)(2,1)S(1)}, u32[]{:S(2)}, u32[]{:S(2)}) collective-permute-start(bf16[4,128,768]{2,1,0:T(8,128)(2,1)} %get-tuple-element.137), channel_id=1, source_target_pairs={{0,4},{4,0},{8,12},{12,8},{16,20},{20,16},{24,28},{28,24},{1,5},{5... | collective-permute-start | bytes 2359304 | tf_op jit(solution)/shard_map/ppermute | solution.py:1125
  238.9 33.1 %collective-permute-start.24 = (bf16[2,128,768]{2,1,0:T(8,128)(2,1)S(1)}, bf16[2,128,768]{2,1,0:T(8,128)(2,1)S(1)}, u32[]{:S(2)}, u32[]{:S(2)}) collective-permute-start(bf16[2,128,768]{2,1,0:T(8,128)(2,1)S(1)} %slice.354), channel_id=1, source_target_pairs={{0,16},{4,20},{8,24},{12,28},{16,0},{20,4},{24,8},{28,12},{1,17},{... | collective-permute-start | bytes 1179656 | tf_op jit(solution)/shard_map/ppermute | solution.py:1125
  276.0 19.7 %collective-permute-start.25 = (bf16[2,480,768]{2,1,0:T(8,128)(2,1)}, bf16[2,480,768]{2,1,0:T(8,128)(2,1)}, u32[]{:S(2)}, u32[]{:S(2)}) collective-permute-start(bf16[2,480,768]{2,1,0:T(8,128)(2,1)} %pad_maximum_fusion.3), channel_id=1, source_target_pairs={{0,1},{1,0},{2,3},{3,2},{4,5},{5,4},{6,7},{7,6},{8,9},{9,8},{10,11... | collective-permute-start | bytes 4423688 | tf_op jit(solution)/shard_map/ppermute | solution.py:1125
  297.8 17.4 %collective-permute-start.28 = (bf16[480,768]{1,0:T(8,128)(2,1)}, bf16[480,768]{1,0:T(8,128)(2,1)}, u32[]{:S(2)}, u32[]{:S(2)}) collective-permute-start(bf16[480,768]{1,0:T(8,128)(2,1)} %fusion.12), channel_id=1, source_target_pairs={{0,2},{1,3},{2,0},{3,1},{4,6},{5,7},{6,4},{7,5},{8,10},{9,11},{10,... | collective-permute-start | bytes 2211848 | tf_op jit(solution)/shard_map/ppermute | solution.py:1125
  297.9 8.6 %collective-permute-start.29 = (bf16[128,768]{1,0:T(8,128)(2,1)S(1)}, bf16[128,768]{1,0:T(8,128)(2,1)S(1)}, u32[]{:S(2)}, u32[]{:S(2)}) collective-permute-start(bf16[128,768]{1,0:T(8,128)(2,1)S(1)} %fusion.24), channel_id=1, source_target_pairs={{0,8},{4,12},{8,0},{12,4},{16,24},{20,28},{24,16},{28,20},{1,9},{5... | collective-permute-start | bytes 589832 | tf_op jit(solution)/shard_map/ppermute | solution.py:1125
  316.1 11.9 %collective-permute-start.31 = (f32[8,768]{1,0:T(8,128)S(1)}, f32[8,768]{1,0:T(8,128)S(1)}, u32[]{:S(2)}, u32[]{:S(2)}) collective-permute-start(f32[8,768]{1,0:T(8,128)S(1)} %get-tuple-element.320), channel_id=1, source_target_pairs={{1,0},{2,1},{3,2},{5,4},{6,5},{7,6},{9,8},{10,9},{11,10},{13,12},{... | collective-permute-start | bytes 73736 | tf_op jit(solution)/shard_map/ppermute | solution.py:1381
  318.0 22.3 %collective-permute-start.30 = (f32[8,768]{1,0:T(8,128)S(1)}, f32[8,768]{1,0:T(8,128)S(1)}, u32[]{:S(2)}, u32[]{:S(2)}) collective-permute-start(f32[8,768]{1,0:T(8,128)S(1)} %get-tuple-element.319), channel_id=1, source_target_pairs={{0,1},{1,2},{2,3},{4,5},{5,6},{6,7},{8,9},{9,10},{10,11},{12,13},{... | collective-permute-start | bytes 73736 | tf_op jit(solution)/shard_map/ppermute | solution.py:1380
  337.2 8.5 %collective-permute-start.39 = (bf16[80,768]{1,0:T(8,128)(2,1)}, bf16[80,768]{1,0:T(8,128)(2,1)S(1)}, u32[]{:S(2)}, u32[]{:S(2)}) collective-permute-start(bf16[80,768]{1,0:T(8,128)(2,1)} %get-tuple-element.176), channel_id=1, source_target_pairs={{0,24},{4,28},{8,16},{12,20},{16,8},{20,12},{24,0},{28,4},{1,25},{... | collective-permute-start | bytes 368648 | tf_op jit(solution)/shard_map/ppermute | solution.py:1125
  340.9 13.8 %collective-permute-start.38 = (bf16[80,768]{1,0:T(8,128)(2,1)}, bf16[80,768]{1,0:T(8,128)(2,1)S(1)}, u32[]{:S(2)}, u32[]{:S(2)}) collective-permute-start(bf16[80,768]{1,0:T(8,128)(2,1)} %get-tuple-element.175), channel_id=1, source_target_pairs={{0,20},{4,16},{8,28},{12,24},{16,4},{20,0},{24,12},{28,8},{1,21},{... | collective-permute-start | bytes 368648 | tf_op jit(solution)/shard_map/ppermute | solution.py:1125
  341.0 17.0 %collective-permute-start.37 = (bf16[80,768]{1,0:T(8,128)(2,1)}, bf16[80,768]{1,0:T(8,128)(2,1)S(1)}, u32[]{:S(2)}, u32[]{:S(2)}) collective-permute-start(bf16[80,768]{1,0:T(8,128)(2,1)} %get-tuple-element.174), channel_id=1, source_target_pairs={{0,16},{4,20},{8,24},{12,28},{16,0},{20,4},{24,8},{28,12},{1,17},{... | collective-permute-start | bytes 368648 | tf_op jit(solution)/shard_map/ppermute | solution.py:1125
  343.1 14.9 %collective-permute-start.36 = (bf16[80,768]{1,0:T(8,128)(2,1)}, bf16[80,768]{1,0:T(8,128)(2,1)S(1)}, u32[]{:S(2)}, u32[]{:S(2)}) collective-permute-start(bf16[80,768]{1,0:T(8,128)(2,1)} %get-tuple-element.173), channel_id=1, source_target_pairs={{0,12},{4,8},{8,4},{12,0},{16,28},{20,24},{24,20},{28,16},{1,13},{... | collective-permute-start | bytes 368648 | tf_op jit(solution)/shard_map/ppermute | solution.py:1125
  343.1 14.9 %collective-permute-start.35 = (bf16[80,768]{1,0:T(8,128)(2,1)}, bf16[80,768]{1,0:T(8,128)(2,1)S(1)}, u32[]{:S(2)}, u32[]{:S(2)}) collective-permute-start(bf16[80,768]{1,0:T(8,128)(2,1)} %get-tuple-element.172), channel_id=1, source_target_pairs={{0,8},{4,12},{8,0},{12,4},{16,24},{20,28},{24,16},{28,20},{1,9},{5... | collective-permute-start | bytes 368648 | tf_op jit(solution)/shard_map/ppermute | solution.py:1125
  345.7 12.2 %collective-permute-start.34 = (bf16[80,768]{1,0:T(8,128)(2,1)}, bf16[80,768]{1,0:T(8,128)(2,1)S(1)}, u32[]{:S(2)}, u32[]{:S(2)}) collective-permute-start(bf16[80,768]{1,0:T(8,128)(2,1)} %get-tuple-element.171), channel_id=1, source_target_pairs={{0,4},{4,0},{8,12},{12,8},{16,20},{20,16},{24,28},{28,24},{1,5},{5... | collective-permute-start | bytes 368648 | tf_op jit(solution)/shard_map/ppermute | solution.py:1125
  373.0 9.7 %collective-permute-start.45 = (bf16[16,16,768]{2,1,0:T(8,128)(2,1)S(1)}, bf16[16,16,768]{2,1,0:T(8,128)(2,1)S(1)}, u32[]{:S(2)}, u32[]{:S(2)}) collective-permute-start(bf16[16,16,768]{2,1,0:T(8,128)(2,1)S(1)} %get-tuple-element.337), channel_id=1, source_target_pairs={{0,1},{1,0},{2,3},{3,2},{4,5},{5,4},{6,7},{7,6},{8,9},{9,8},{10,11... | collective-permute-start | bytes 1179656 | tf_op jit(solution)/shard_map/ppermute | solution.py:1125
  (66 other events, 700.4 us)
Sparse Core Ops, SparseCore 0:
  11.5 81.8 all-gather.2

commit v3 on v2

--- a/solution.py
+++ b/solution.py
@@ -130,7 +130,7 @@
             jax.ShapeDtypeStruct((4 * NS, tokens), bf16),
             jax.ShapeDtypeStruct((blocks, BL, BL), f32),
         ),
-        compiler_params=pltpu.CompilerParams(vmem_limit_bytes=56 * 1024 * 1024),
+        compiler_params=pltpu.CompilerParams(vmem_limit_bytes=16 * 1024 * 1024),
         cost_estimate=cost(6),
         name="key_stage",
     )(nx, key_low, taps)
@@ -415,6 +415,7 @@
 ):
     step = pl.program_id(0)
     last = pl.num_programs(0) - 1
+    cuts = [slice(j * BL, (j + 1) * BL) for j in range(v_ref.shape[1] // BL)]
 
     @pl.when(step == 0)
     def _():
@@ -425,74 +426,89 @@
         wide_scr[0] = jnp.broadcast_to(cols_ref[:, 0:1], (CH, BL))
         wide_scr[1] = jnp.broadcast_to(cols_ref[:, 1:2], (CH, BL))
 
-    c_f = k4_ref[NS : 2 * NS, :]
-    c_r = k4_ref[3 * NS :, :]
-    both_keys = stacked_keys(c_f, c_r)
-    cross_scr[...] = nn(s_ref[0], both_keys)
+    keys = [stacked_keys(k4_ref[NS : 2 * NS, cut], k4_ref[3 * NS :, cut]) for cut in cuts]
+    for j, both_keys in enumerate(keys):
+        cross_scr[j] = nn(s_ref[j], both_keys)
     g_scr[...] = nt(wg_ref[...], nx_ref[...])
     dres_scr[...] = nt(wo_ref[...], go_ref[...])
-    squares = jnp.zeros((8, BL), f32)
+    squares = [jnp.zeros((8, BL), f32) for _ in cuts]
+    cross = [jnp.zeros((8, BL), f32) for _ in cuts]
     for h in range(H):
         span = slice(h * PS, (h + 1) * PS)
-        part_f = cross_scr[span, :BL] * rows_ref[EF, h : h + 1, :]
-        part_r = cross_scr[span, BL:] * rows_ref[ER, h : h + 1, :]
-        mix = (
-            oi_ref[span, :].astype(f32)
-            + part_f
-            + part_r
-            + wide_scr[1, span, :] * v_ref[span, :].astype(f32)
-        )
-        gate = g_scr[span, :]
-        gated = mix * (gate * sigmoid(gate))
-        mix_scr[span, :] = mix
-        gated_scr[span, :] = gated
-        squares = squares + jnp.sum((gated * gated).reshape(PS // 8, 8, BL), axis=0)
-    scale = lax.rsqrt(jnp.sum(squares, axis=0, keepdims=True) / CH + NORM_EPS)
-    cross = jnp.zeros((8, BL), f32)
+        gain = wide_scr[0, span, :]
+        for j, cut in enumerate(cuts):
+            part_f = cross_scr[j, span, :BL] * rows_ref[EF, h : h + 1, cut]
+            part_r = cross_scr[j, span, BL:] * rows_ref[ER, h : h + 1, cut]
+            mix = (
+                oi_ref[span, cut].astype(f32)
+                + part_f
+                + part_r
+                + wide_scr[1, span, :] * v_ref[span, cut].astype(f32)
+            )
+            gate = g_scr[span, cut]
+            gated = mix * (gate * sigmoid(gate))
+            mix_scr[span, cut] = mix
+            gated_scr[span, cut] = gated
+            squares[j] = squares[j] + jnp.sum((gated * gated).reshape(PS // 8, 8, BL), axis=0)
+            flow = dres_scr[span, cut] * gain * gated
+            cross[j] = cross[j] + jnp.sum(flow.reshape(PS // 8, 8, BL), axis=0)
+    scales = [
+        lax.rsqrt(jnp.sum(x, axis=0, keepdims=True) / CH + NORM_EPS) for x in squares
+    ]
+    pulls = [
+        scale * scale * scale * (jnp.sum(x, axis=0, keepdims=True) / CH)
+        for scale, x in zip(scales, cross)
+    ]
     for h in range(H):
         span = slice(h * PS, (h + 1) * PS)
-        gated = gated_scr[span, :]
         gain = wide_scr[0, span, :]
-        normal = gated * scale
-        r_ref[span, :] = (normal * gain).astype(bf16)
-        dres = dres_scr[span, :]
-        gain_scr[span, :] += dres * normal
-        cross = cross + jnp.sum((dres * gain * gated).reshape(PS // 8, 8, BL), axis=0)
+        diags = diag_scr[span, :]
+        gains = gain_scr[span, :]
+        for j, cut in enumerate(cuts):
+            gated = gated_scr[span, cut]
+            normal = gated * scales[j]
+            dres = dres_scr[span, cut]
+            r_ref[span, cut] = (normal * gain).astype(bf16)
+            gains = gains + dres * normal
+            dgated = scales[j] * (dres * gain) - gated * pulls[j]
+            gate = g_scr[span, cut]
+            soft = sigmoid(gate)
+            grad_mix = dgated * (gate * soft)
+            dg_ref[span, cut] = (
+                dgated * mix_scr[span, cut] * (soft * (1.0 + gate * (1.0 - soft)))
+            ).astype(bf16)
+            diags = diags + grad_mix * v_ref[span, cut].astype(f32)
+            do_ref[span, cut] = grad_mix.astype(bf16)
+            grad_f = grad_mix * rows_ref[EF, h : h + 1, cut]
+            grad_r = grad_mix * rows_ref[ER, h : h + 1, cut]
+            rc_ref[0, h : h + 1, cut] = jnp.sum(
+                grad_f * cross_scr[j, span, :BL], axis=0, keepdims=True
+            )
+            rc_ref[1, h : h + 1, cut] = jnp.sum(
+                grad_r * cross_scr[j, span, BL:], axis=0, keepdims=True
+            )
+            lhs_scr[j, span, :BL] = grad_f.astype(bf16)
+            lhs_scr[j, span, BL:] = grad_r.astype(bf16)
+        diag_scr[span, :] = diags
+        gain_scr[span, :] = gains
     out = tn(r_ref[...], wo_ref[...])
     ho_ref[...] = (hid_ref[...].astype(f32) + out).astype(bf16)
-    pull = scale * scale * scale * (jnp.sum(cross, axis=0, keepdims=True) / CH)
-    for h in range(H):
-        span = slice(h * PS, (h + 1) * PS)
-        dgated = scale * (dres_scr[span, :] * wide_scr[0, span, :]) - gated_scr[span, :] * pull
-        gate = g_scr[span, :]
-        soft = sigmoid(gate)
-        grad_mix = dgated * (gate * soft)
-        dg_ref[span, :] = (dgated * mix_scr[span, :] * (soft * (1.0 + gate * (1.0 - soft)))).astype(
-            bf16
-        )
-        diag_scr[span, :] += grad_mix * v_ref[span, :].astype(f32)
-        do_ref[span, :] = grad_mix.astype(bf16)
-        grad_f = grad_mix * rows_ref[EF, h : h + 1, :]
-        grad_r = grad_mix * rows_ref[ER, h : h + 1, :]
-        rc_ref[0, h : h + 1, :] = jnp.sum(grad_f * cross_scr[span, :BL], axis=0, keepdims=True)
-        rc_ref[1, h : h + 1, :] = jnp.sum(grad_r * cross_scr[span, BL:], axis=0, keepdims=True)
-        lhs_scr[span, :BL] = grad_f.astype(bf16)
-        lhs_scr[span, BL:] = grad_r.astype(bf16)
-    dstate = nt(lhs_scr[...], both_keys)
-    dkeys = tn(s_ref[0], lhs_scr[...])
-    dk_ref[:NS, :] = dkeys[:NS, :BL]
-    dk_ref[NS:, :] = dkeys[NS:, BL:]
-    dsblk_ref[0] = dstate.astype(bf16)
     first = lane_first((H, BL))
-    total = tot_ref[0]
-    keep = jnp.where(first, 1.0, jnp.exp(total))
-    grow = jnp.where(first, jnp.exp(cum_scr[...]), 1.0)
-    for h in range(H):
-        span = slice(h * PS, (h + 1) * PS)
-        dev_scr[span, :] = (
-            dev_scr[span, :] * keep[h : h + 1] + dstate[span, :] * grow[h : h + 1]
-        )
-    cum_scr[...] += total
+    for j, cut in enumerate(cuts):
+        dstate = nt(lhs_scr[j], keys[j])
+        dkeys = tn(s_ref[j], lhs_scr[j])
+        dk_ref[:NS, cut] = dkeys[:NS, :BL]
+        dk_ref[NS:, cut] = dkeys[NS:, BL:]
+        dsblk_ref[j] = dstate.astype(bf16)
+        total = tot_ref[j]
+        keep = jnp.where(first, 1.0, jnp.exp(total))
+        grow = jnp.where(first, jnp.exp(cum_scr[...]), 1.0)
+        for h in range(H):
+            span = slice(h * PS, (h + 1) * PS)
+            dev_scr[span, :] = (
+                dev_scr[span, :] * keep[h : h + 1] + dstate[span, :] * grow[h : h + 1]
+            )
+        cum_scr[...] += total
 
     @pl.when(step == last)
     def _():
@@ -504,20 +520,24 @@
 def token_stage(oi, v, s9, k4, rows, tot, wg, wo, nx, hid, go, cols):
     tokens = v.shape[1]
     blocks = tokens // BL
+    two = 2
+    wide = two * BL
     whole = dict(pipeline_mode=pl.Buffered(1))
-    chan = pl.BlockSpec((CH, BL), lambda b: (0, b))
-    toks = pl.BlockSpec((BL, D), lambda b: (b, 0))
+    chan = pl.BlockSpec((CH, wide), lambda b: (0, b))
+    toks = pl.BlockSpec((wide, D), lambda b: (b, 0))
+    state = pl.BlockSpec((two, CH, BL), lambda b: (b, 0, 0))
     big = pltpu.VMEM((CH, BL), f32)
+    large = pltpu.VMEM((CH, wide), f32)
     return pl.pallas_call(
         token_kernel,
-        grid=(blocks,),
+        grid=(blocks // two,),
         in_specs=[
             chan,
             chan,
-            pl.BlockSpec((1, CH, BL), lambda b: (b, 0, 0)),
-            pl.BlockSpec((4 * NS, BL), lambda b: (0, b)),
-            pl.BlockSpec((KINDS, H, BL), lambda b: (0, 0, b)),
-            pl.BlockSpec((1, H, BL), lambda b: (b, 0, 0)),
+            state,
+            pl.BlockSpec((4 * NS, wide), lambda b: (0, b)),
+            pl.BlockSpec((KINDS, H, wide), lambda b: (0, 0, b)),
+            pl.BlockSpec((two, H, BL), lambda b: (b, 0, 0)),
             pl.BlockSpec((CH, D), lambda b: (0, 0), **whole),
             pl.BlockSpec((CH, D), lambda b: (0, 0), **whole),
             toks,
@@ -530,10 +550,10 @@
             chan,
             chan,
             chan,
-            pl.BlockSpec((1, CH, BL), lambda b: (b, 0, 0)),
+            state,
             pl.BlockSpec((CH, BL), lambda b: (0, 0)),
-            pl.BlockSpec((2, H, BL), lambda b: (0, 0, b)),
-            pl.BlockSpec((2 * NS, BL), lambda b: (0, b)),
+            pl.BlockSpec((2, H, wide), lambda b: (0, 0, b)),
+            pl.BlockSpec((2 * NS, wide), lambda b: (0, b)),
             pl.BlockSpec((2, 8, CH), lambda b: (0, 0, 0)),
         ],
         out_shape=(
@@ -547,9 +567,9 @@
             jax.ShapeDtypeStruct((2 * NS, tokens), f32),
             jax.ShapeDtypeStruct((2, 8, CH), f32),
         ),
-        scratch_shapes=[pltpu.VMEM((CH, 2 * BL), f32)]
-        + [big] * 4
-        + [pltpu.VMEM((CH, 2 * BL), bf16)]
+        scratch_shapes=[pltpu.VMEM((two, CH, 2 * BL), f32)]
+        + [large] * 4
+        + [pltpu.VMEM((two, CH, 2 * BL), bf16)]
         + [big] * 3
         + [pltpu.VMEM((H, BL), f32), pltpu.VMEM((2, CH, BL), f32)],
         compiler_params=params(),
@@ -596,7 +616,7 @@
             jax.ShapeDtypeStruct((H, 2 * PS, D), bf16),
             jax.ShapeDtypeStruct((tokens, D), f32),
         ),
-        compiler_params=params(),
+        compiler_params=params(24),
         cost_estimate=cost(12),
         name="early_grad",
     )(dgate, result, nx, go, wg)
@@ -799,7 +819,7 @@
     return pl.pallas_call(
         key_pre_kernel,
         out_shape=jax.ShapeDtypeStruct(u.shape, f32),
-        compiler_params=pltpu.CompilerParams(vmem_limit_bytes=56 * 1024 * 1024),
+        compiler_params=pltpu.CompilerParams(vmem_limit_bytes=16 * 1024 * 1024),
         cost_estimate=cost(3),
         name="key_pre",
     )(dk, u, edge)
@@ -872,7 +892,7 @@
             ],
         ),
         out_shape=outs,
-        compiler_params=params(),
+        compiler_params=params(16),
         cost_estimate=cost(8),
         name="key_back",
     )(meta, *args)
@@ -981,7 +1001,7 @@
             out_specs=pl.BlockSpec((count, rows, width), lambda i, index: (0, 0, 0)),
         ),
         out_shape=jax.ShapeDtypeStruct((count, rows, width), sources[0].dtype),
-        compiler_params=params(),
+        compiler_params=params(16),
         cost_estimate=cost(3),
         name="pick",
     )(index, *sources)
@@ -1053,7 +1073,7 @@
             out_specs=[whole(x.shape) for x in shapes],
         ),
         out_shape=shapes,
-        compiler_params=params(),
+        compiler_params=params(16),
         cost_estimate=cost(3),
         name="deal",
     )(*plan, *args)
@@ -1111,7 +1131,7 @@
             scratch_shapes=[pltpu.VMEM((4 * NS, D), f32)],
         ),
         out_shape=outs,
-        compiler_params=params(),
+        compiler_params=params(16),
         cost_estimate=cost(5),
         name="finish_stage",
     )(code, *args)
@@ -1305,14 +1325,13 @@
         dpre, dx, dk = cross_back_stage(
             dvi, v, do_t, u, ds9, k4, rows, rci, rcc, x9, dki, cols, after
         )
-        if direct:
-            keep_go, dpre, dk = lax.optimization_barrier((keep_go, dpre, dk))
-            far_go = swap(keep_go[2:].astype(bf16), "dp", n_dp, 4)
         d_last, d_first = to_prev, to_next
         d_last = jnp.where(ends, 0.0, d_last)
         d_first = jnp.where(starts, 0.0, d_first)
         edge = jnp.transpose(jnp.concatenate([d_last, d_first, jnp.zeros((6, NS), f32)], axis=0))
-        dpre_k = key_pre_stage(dk, key_u, edge)
+        if direct:
+            keep_go, dpre, dk, edge = lax.optimization_barrier((keep_go, dpre, dk, edge))
+            far_go = swap(keep_go[2:].astype(bf16), "dp", n_dp, 4)
         grad_v, dn_value, tap_v = value_back_stage(dpre, taps_v, s, dx, nx, wv)
         if direct:
             far_go, grad_v = lax.optimization_barrier((far_go, grad_v))
@@ -1321,8 +1340,9 @@
             both = grad_v.reshape(n_mp, per * WV, D)
             got_v = swap(jnp.stack([both[1], both[3]]), "mp", n_mp, 1)
             away_v = (both[2].astype(f32) + got_v[1].astype(f32)).astype(bf16)
-            away_v, dpre_k = lax.optimization_barrier((away_v, dpre_k))
+            away_v, dk = lax.optimization_barrier((away_v, dk))
             far_v = swap(away_v, "mp", n_mp, 2)
+        dpre_k = key_pre_stage(dk, key_u, edge)
         grad_key, dn_key, tap_key = key_back_stage(meta, dpre_k, taps_k, key_proj, nx, key_low)
         if direct:
             far_v, last_go, grad_key, dn_key, tap_key = lax.optimization_barrier(
@@ -1402,9 +1422,8 @@
             previous[0], own_grad, previous[1], previous[2], previous[3], MATRIX_RATE
         )
         is_owner = jnp.any(owners == dp_index)
-        slot_outs = [
-            jnp.transpose(jnp.where(is_owner, renewed, before), (1, 2, 0))[None]
-            for renewed, before in zip(slot_new, previous)
+        slot_new = [
+            jnp.where(is_owner, renewed, before) for renewed, before in zip(slot_new, previous)
         ]
         if direct:
             share = jnp.concatenate(
@@ -1412,7 +1431,7 @@
                 axis=0,
             ).astype(bf16)
             shares, code = gather_all(share, mp_index, dp_index)
-            shares, slot_outs = lax.optimization_barrier((shares, slot_outs))
+            shares, slot_new = lax.optimization_barrier((shares, slot_new))
             *key_new, small_total, gain_total = finish_stage(
                 code, shares, bc_weight, bc_first, bc_second, bc_ema
             )
@@ -1425,6 +1444,7 @@
             key_new = adamw_update(
                 bc_weight, jnp.transpose(key_total), bc_first, bc_second, bc_ema, MATRIX_RATE
             )
+        slot_outs = [jnp.transpose(x, (1, 2, 0))[None] for x in slot_new]
         head_total = lax.dynamic_slice_in_dim(
             small_total[: H * 10 * PS].reshape(H, 10, PS), mp_index * per, per
         )

time: 413 us -> 391 us (0.947)
  Pallas kernels: 190 us -> 164 us
  local copies, waits for them, and re-layouts: 34.3 us -> 40.8 us
    unnamed x111 -> x149, local copies, waits for them, and re-layouts: 13.9 us -> 21.3 us
    pallas_call x1, Pallas kernels: 14 us -> 8.6 us  [early_grad_stage(): pl.pallas_call(early_grad_kernel, grid=(NG,), in_specs=[pl.BlockSpec((row...]
    pallas_call x2, Pallas kernels: 6.11 us -> 1.45 us  [deal(): pl.pallas_call(body, grid_spec=pltpu.PrefetchScalarGridSpec(num_scalar_pr...]
  transfers between devices with their start and end apart: 47 -> 47, of which waited for: 15 -> 15; matrix products, arithmetic and copies ran while one was open for 12% -> 13% of each run, Pallas kernels for 35% -> 32%
where the time goes in v3:
time: 391 us; the launch traced here: 384 us
  Pallas kernels  164 us (42%)
  starting transfers between devices  61.6 us (16%)
  waiting for transfers between devices  55.9 us (14%)
  other arithmetic  45.8 us (12%)
  local copies, waits for them, and re-layouts  40.8 us (10%)
  between operations  16.2 us (4%)
    ppermute x40, waiting for transfers between devices, swap(): return lax.ppermute(x, axis, [(i, i ^ bit) for i in range(size)])  53.2 us
    ppermute x40, starting transfers between devices, swap(): return lax.ppermute(x, axis, [(i, i ^ bit) for i in range(size)])  44 us
    pallas_call x1, Pallas kernels, token_stage(): pl.pallas_call(token_kernel, grid=(blocks // two,), in_specs=[chan, chan,...  32.3 us
    pallas_call x1, Pallas kernels, value_back_stage(): pl.pallas_call(value_back_kernel, grid=(NG,), in_specs=[pl.BlockSpec((row...  26.3 us
    unnamed x149, local copies, waits for them, and re-layouts  21.3 us
    pallas_call x1, Pallas kernels, value_stage(): pl.pallas_call(value_kernel, grid=(NG,), in_specs=[pl.BlockSpec((ext, D),...  19.3 us
    pallas_call x1, Pallas kernels, intra_back_stage(): pl.pallas_call(intra_back_kernel, grid=(tokens // BL,), in_specs=[chan, c...  15.8 us
    pallas_call x1, Pallas kernels, cross_back_stage(): pl.pallas_call(cross_back_kernel, grid=(tokens // BL,), in_specs=[chan, c...  15.3 us
  transfers between devices with their start and end apart: 47, of which 15 were waited for; matrix products, arithmetic and copies ran while one was open for 13% of the time, Pallas kernels for 32%

profile of v3, /device:TPU:1, one launch (start us, length us, event | category | flops | bytes accessed | tf_op | source)
XLA Modules:
  0.0 383.9 jit_solution(5562068414868585971)
XLA Ops:
  18.5 4.8 %collective-permute-start.1 = (bf16[8,768]{1,0:T(8,128)(2,1)S(1)}, bf16[8,768]{1,0:T(8,128)(2,1)S(1)}, u32[]{:S(2)}, u32[]{:S(2)}) collective-permute-start(bf16[8,768]{1,0:T(8,128)(2,1)S(1)} %get-tuple-element.330), channel_id=1, source_target_pairs={{0,1},{1,2},{2,3},{4,5},{5,6},{6,7},{8,9},{9,10},{10,11},{12,13},{... | collective-permute-start | bytes 36872 | tf_op jit(solution)/shard_map/ppermute | solution.py:1232
  28.7 3.3 collective-permute-start.7
  35.6 8.2 %collective-permute-done.6 = bf16[80,768]{1,0:T(8,128)(2,1)S(1)} collective-permute-done((bf16[80,768]{1,0:T(8,128)(2,1)S(1)}, bf16[80,768]{1,0:T(8,128)(2,1)S(1)}, u32[]{:S(2)}, u32[]{:S(2)}) %collective-permute-start.6) | collective-permute-done | bytes 122912 | tf_op jit(solution)/shard_map/ppermute | solution.py:1145
  46.6 3.4 key_stage.1
  54.0 14.2 %collective-permute-done.10 = bf16[6,80,768]{2,1,0:T(8,128)(2,1)} collective-permute-done((bf16[6,80,768]{2,1,0:T(8,128)(2,1)S(1)}, bf16[6,80,768]{2,1,0:T(8,128)(2,1)}, u32[]{:S(2)}, u32[]{:S(2)}) %collective-permute-start.10) | collective-permute-done | bytes 737312 | tf_op jit(solution)/shard_map/ppermute | solution.py:1145
  75.5 3.5 pad_maximum_fusion.wv_ref
  79.0 19.3 %value_stage.1 = (bf16[1536,1024]{1,0:T(8,128)(2,1)}, bf16[1536,1024]{1,0:T(8,128)(2,1)}, bf16[1536,1152]{1,0:T(8,128)(2,1)}, f32[12,24,1024]{2,1,0:T(8,128)}, f...) custom-call(bf16[1152,768]{1,0:T(8,128)(2,1)} %copy-done, ...), custom_call_target="tpu_custom_call" | custom-call | bytes 27000000 | tf_op jit(solution)/shard_map/value_stage/pallas_call | solution.py:223
  102.9 11.9 %intra_stage.1.oi_ref = bf16[1536,1024]{1,0:T(8,128)(2,1)} custom-call(bf16[1536,1024]{1,0:T(8,128)(2,1)} %get-tuple-element.110.v_ref, f32[12,24,1024]{2,1,0:T(8,128)} %get-tuple-element.111.rows_ref, f32[8,128,128]{2,1,0:T(8,128)} %copy-done.19), custom_call_target="tpu_custom_call" | custom-call | bytes 12000000 | tf_op jit(solution)/shard_map/intra_stage/pallas_call | solution.py:393
  117.4 6.7 %chain_stage.1.s_ref.refs_8_ = bf16[9,1536,128]{2,1,0:T(8,128)(2,1)} custom-call(s32[6]{0:T(128)} %pad_add_fusion.refs_0_.meta_ref, bf16[8,1536,128]{2,1,0:T(8,128)(2,1)} %get-tuple-element.114.refs_1_, f32[8,24,128]{2,1,0:T(8,128)} %get-tuple-element.115.refs_2_.tot_ref, f32[4,72,128]{2,1,0:T(8,128)} %maximum_convert_fusion.refs_3_, ...), custom_call_target="tpu_custom_call" | custom-call | bytes 7000000 | tf_op jit(solution)/shard_map/chain_stage/pallas_call | solution.py:349
  124.0 5.9 %pick_two.1 = (bf16[24,64,768]{2,1,0:T(8,128)(2,1)}, bf16[24,64,768]{2,1,0:T(8,128)(2,1)}) custom-call(s32[24]{0:T(128)} %fusion.39.index_ref, bf16[32,128,768]{2,1,0:T(8,128)(2,1)} %bitcast.171), custom_call_target="tpu_custom_call" | custom-call | bytes 6000000 | tf_op jit(solution)/shard_map/pick_two/pallas_call | solution.py:1018
  129.9 32.3 %token_stage.1 = (bf16[1024,768]{1,0:T(8,128)(2,1)}, bf16[1536,1024]{1,0:T(8,128)(2,1)}, bf16[1536,1024]{1,0:T(8,128)(2,1)}, bf16[1536,1024]{1,0:T(8,128)(2,1)},...) custom-call(bf16[1536,1024]{1,0:T(8,128)(2,1)} %intra_stage.1.oi_ref, ...), custom_call_target="tpu_custom_call" | custom-call | bytes 35000000 | tf_op jit(solution)/shard_map/token_stage/pallas_call | solution.py:531
  166.9 8.6 %early_grad.1 = (bf16[24,128,768]{2,1,0:T(8,128)(2,1)S(1)}, f32[1024,768]{1,0:T(8,128)S(1)}) custom-call(bf16[1536,1024]{1,0:T(8,128)(2,1)S(1)} %copy-done.14, bf16[1536,1024]{1,0:T(8,128)(2,1)S(1)} %copy-done.13, bf16[1152,768]{1,0:T(8,128)(2,1)S(1)} %copy-done.1, bf16[1024,768]{1,0:T(8,128)(2,1)S(1)} %copy-done.3, bf16[1536,768]{1,0:T(8,128)(2,1)S(1)} %bitcast.155), custom_call_target="tpu_custom_call" | custom-call | bytes 12000000 | tf_op jit(solution)/shard_map/early_grad/pallas_call | solution.py:601
  177.6 4.2 %collective-permute-done.19 = bf16[2,768,768]{2,1,0:T(8,128)(2,1)S(1)} collective-permute-done((bf16[2,768,768]{2,1,0:T(8,128)(2,1)S(1)}, bf16[2,768,768]{2,1,0:T(8,128)(2,1)S(1)}, u32[]{:S(2)}, u32[]{:S(2)}) %collective-permute-start.19) | collective-permute-done | bytes 2359328 | tf_op jit(solution)/shard_map/ppermute | solution.py:1145
  186.2 7.9 %chain_back.1 = (bf16[8,1536,128]{2,1,0:T(8,128)(2,1)}, f32[8,24,128]{2,1,0:T(8,128)}) custom-call(s32[6]{0:T(128)} %pad_add_fusion.refs_0_.meta_ref, bf16[8,1536,128]{2,1,0:T(8,128)(2,1)} %get-tuple-element.127.refs_1_, f32[8,24,128]{2,1,0:T(8,128)} %get-tuple-element.115.refs_2_.tot_ref, f32[4,72,128]{2,1,0:T(8,128)} %maximum_convert_fusion.refs_3_, ...), custom_call_target="tpu_custom_call" | custom-call | bytes 7000000 | tf_op jit(solution)/shard_map/chain_back/pallas_call | solution.py:349
  194.1 15.8 %intra_back.1 = (bf16[1536,1024]{1,0:T(8,128)(2,1)}, f32[4,24,1024]{2,1,0:T(8,128)}, f32[256,1024]{1,0:T(8,128)}) custom-call(bf16[1536,1024]{1,0:T(8,128)(2,1)} %get-tuple-element.110.v_ref, bf16[1536,1024]{1,0:T(8,128)(2,1)} %get-tuple-element.131.do_ref, f32[12,24,1024]{2,1,0:T(8,128)} %get-tuple-element.111.rows_ref, f32[8,128,128]{2,1,0:T(8,128)} %copy-done.19, ...), custom_call_target="tpu_custom_call" | custom-call | bytes 18000000 | tf_op jit(solution)/shard_map/intra_back/pallas_call | solution.py:679
  214.5 3.4 collective-permute-start.25
  220.6 2.7 collective-permute-done.24
  224.0 15.3 %cross_back.1 = (bf16[1536,1024]{1,0:T(8,128)(2,1)}, f32[2,24,1024]{2,1,0:T(8,128)}, f32[256,1024]{1,0:T(8,128)}) custom-call(bf16[1536,1024]{1,0:T(8,128)(2,1)} %get-tuple-element.139.dvi_ref, bf16[1536,1024]{1,0:T(8,128)(2,1)} %get-tuple-element.110.v_ref, bf16[1536,1024]{1,0:T(8,128)(2,1)} %get-tuple-element.131.do_ref, ...), custom_call_target="tpu_custom_call" | custom-call | bytes 16000000 | tf_op jit(solution)/shard_map/cross_back/pallas_call | solution.py:769
  243.0 3.1 collective-permute-start.26
  246.1 26.3 %value_back.1 = (bf16[24,80,768]{2,1,0:T(8,128)(2,1)}, f32[1152,768]{1,0:T(8,128)}, f32[3,8,512]{2,1,0:T(8,128)}) custom-call(bf16[1536,1024]{1,0:T(8,128)(2,1)} %get-tuple-element.149.dpre_ref, f32[1536,8]{1,0:T(8,128)} %pad.22.taps_ref, bf16[1536,1152]{1,0:T(8,128)(2,1)} %get-tuple-element.150.s_ref, f32[2,24,1024]{2,1,0:T(8,128)} %get-tuple-element.151.dx_ref, ...), custom_call_target="tpu_custom_call" | custom-call | bytes 27000000 | tf_op jit(solution)/shard_map/value_back/pallas_call | solution.py:946
  272.4 3.0 fusion.46
  292.3 4.3 %key_back.1 = (bf16[4,64,768]{2,1,0:T(8,128)(2,1)S(1)}, f32[1152,768]{1,0:T(8,128)S(1)}, f32[8,256]{1,0:T(8,128)S(1)}) custom-call(s32[6]{0:T(128)S(1)} %copy-done.28, f32[256,1024]{1,0:T(8,128)S(1)} %key_pre.1.dpre_ref, f32[256,8]{1,0:T(8,128)S(1)} %pad.21.taps_ref, f32[256,1152]{1,0:T(8,128)S(1)} %copy-done.21, bf16[1152,768]{1,0:T(8,128)(2,1)S(1)} %copy-done.2, ...), custom_call_target="tpu_custom_call" | custom-call | bytes 8000000 | tf_op jit(solution)/shard_map/key_back/pallas_call | solution.py:881
  297.3 3.3 collective-permute-done.28
  301.4 3.3 collective-permute-start.31
  313.2 3.1 collective-permute-done.33
  321.2 3.2 collective-permute-start.37
  327.2 3.8 fusion.8
  330.9 6.1 %collective-permute-done.38 = bf16[80,768]{1,0:T(8,128)(2,1)S(1)} collective-permute-done((bf16[80,768]{1,0:T(8,128)(2,1)S(1)}, bf16[80,768]{1,0:T(8,128)(2,1)S(1)}, u32[]{:S(2)}, u32[]{:S(2)}) %collective-permute-start.38) | collective-permute-done | bytes 122912 | tf_op jit(solution)/shard_map/ppermute | solution.py:1145
  343.3 3.0 collective-permute-done.42
  351.4 3.1 collective-permute-done.44
  354.5 8.9 %collective-permute-start.45 = (bf16[16,16,768]{2,1,0:T(8,128)(2,1)S(1)}, bf16[16,16,768]{2,1,0:T(8,128)(2,1)S(1)}, u32[]{:S(2)}, u32[]{:S(2)}) collective-permute-start(bf16[16,16,768]{2,1,0:T(8,128)(2,1)S(1)} %get-tuple-element.339), channel_id=1, source_target_pairs={{0,1},{1,0},{2,3},{3,2},{4,5},{5,4},{6,7},{7,6},{8,9},{9,8},{10,11... | collective-permute-start | bytes 1179656 | tf_op jit(solution)/shard_map/ppermute | solution.py:1145
  366.5 3.0 finish_stage.1
  (371 shorter events, 118.8 us)
Async XLA Ops:
  7.2 116.8 %all-gather.3.cloned.1.call-start = ((), (), s32[]{:S(2)}) async-start(), calls=%async_computation | async-start | bytes 6488064 | tf_op jit(solution)/shard_map/all_gather | solution.py:1214
  9.3 19.5 %collective-permute-start.2 = (bf16[80,768]{1,0:T(8,128)(2,1)S(1)}, bf16[80,768]{1,0:T(8,128)(2,1)S(1)}, u32[]{:S(2)}, u32[]{:S(2)}) collective-permute-start(bf16[80,768]{1,0:T(8,128)(2,1)S(1)} %get-tuple-element.343), channel_id=1, source_target_pairs={{0,4},{4,0},{8,12},{12,8},{16,20},{20,16},{24,28},{28,24},{1,5},{5... | collective-permute-start | bytes 368648 | tf_op jit(solution)/shard_map/ppermute | solution.py:1145
  11.4 20.6 %collective-permute-start.3 = (bf16[80,768]{1,0:T(8,128)(2,1)S(1)}, bf16[80,768]{1,0:T(8,128)(2,1)S(1)}, u32[]{:S(2)}, u32[]{:S(2)}) collective-permute-start(bf16[80,768]{1,0:T(8,128)(2,1)S(1)} %get-tuple-element.343), channel_id=1, source_target_pairs={{0,8},{4,12},{8,0},{12,4},{16,24},{20,28},{24,16},{28,20},{1,9},{5... | collective-permute-start | bytes 368648 | tf_op jit(solution)/shard_map/ppermute | solution.py:1145
  12.7 19.4 %collective-permute-start.4 = (bf16[80,768]{1,0:T(8,128)(2,1)S(1)}, bf16[80,768]{1,0:T(8,128)(2,1)S(1)}, u32[]{:S(2)}, u32[]{:S(2)}) collective-permute-start(bf16[80,768]{1,0:T(8,128)(2,1)S(1)} %get-tuple-element.343), channel_id=1, source_target_pairs={{0,12},{4,8},{8,4},{12,0},{16,28},{20,24},{24,20},{28,16},{1,13},{... | collective-permute-start | bytes 368648 | tf_op jit(solution)/shard_map/ppermute | solution.py:1145
  12.7 22.0 %collective-permute-start.5 = (bf16[80,768]{1,0:T(8,128)(2,1)S(1)}, bf16[80,768]{1,0:T(8,128)(2,1)S(1)}, u32[]{:S(2)}, u32[]{:S(2)}) collective-permute-start(bf16[80,768]{1,0:T(8,128)(2,1)S(1)} %get-tuple-element.343), channel_id=1, source_target_pairs={{0,16},{4,20},{8,24},{12,28},{16,0},{20,4},{24,8},{28,12},{1,17},{... | collective-permute-start | bytes 368648 | tf_op jit(solution)/shard_map/ppermute | solution.py:1145
  18.5 9.2 %collective-permute-start.1 = (bf16[8,768]{1,0:T(8,128)(2,1)S(1)}, bf16[8,768]{1,0:T(8,128)(2,1)S(1)}, u32[]{:S(2)}, u32[]{:S(2)}) collective-permute-start(bf16[8,768]{1,0:T(8,128)(2,1)S(1)} %get-tuple-element.330), channel_id=1, source_target_pairs={{0,1},{1,2},{2,3},{4,5},{5,6},{6,7},{8,9},{9,10},{10,11},{12,13},{... | collective-permute-start | bytes 36872 | tf_op jit(solution)/shard_map/ppermute | solution.py:1232
  27.7 16.1 %collective-permute-start.6 = (bf16[80,768]{1,0:T(8,128)(2,1)S(1)}, bf16[80,768]{1,0:T(8,128)(2,1)S(1)}, u32[]{:S(2)}, u32[]{:S(2)}) collective-permute-start(bf16[80,768]{1,0:T(8,128)(2,1)S(1)} %get-tuple-element.343), channel_id=1, source_target_pairs={{0,20},{4,16},{8,28},{12,24},{16,4},{20,0},{24,12},{28,8},{1,21},{... | collective-permute-start | bytes 368648 | tf_op jit(solution)/shard_map/ppermute | solution.py:1145
  28.7 15.1 %collective-permute-start.7 = (bf16[80,768]{1,0:T(8,128)(2,1)S(1)}, bf16[80,768]{1,0:T(8,128)(2,1)S(1)}, u32[]{:S(2)}, u32[]{:S(2)}) collective-permute-start(bf16[80,768]{1,0:T(8,128)(2,1)S(1)} %get-tuple-element.343), channel_id=1, source_target_pairs={{0,24},{4,28},{8,16},{12,20},{16,8},{20,12},{24,0},{28,4},{1,25},{... | collective-permute-start | bytes 368648 | tf_op jit(solution)/shard_map/ppermute | solution.py:1145
  32.1 11.7 %collective-permute-start.8 = (bf16[80,768]{1,0:T(8,128)(2,1)S(1)}, bf16[80,768]{1,0:T(8,128)(2,1)S(1)}, u32[]{:S(2)}, u32[]{:S(2)}) collective-permute-start(bf16[80,768]{1,0:T(8,128)(2,1)S(1)} %get-tuple-element.343), channel_id=1, source_target_pairs={{0,28},{4,24},{8,20},{12,16},{16,12},{20,8},{24,4},{28,0},{1,29},{... | collective-permute-start | bytes 368648 | tf_op jit(solution)/shard_map/ppermute | solution.py:1145
  32.1 13.5 %collective-permute-start = (bf16[8,768]{1,0:T(8,128)(2,1)S(1)}, bf16[8,768]{1,0:T(8,128)(2,1)S(1)}, u32[]{:S(2)}, u32[]{:S(2)}) collective-permute-start(bf16[8,768]{1,0:T(8,128)(2,1)S(1)} %get-tuple-element.329), channel_id=1, source_target_pairs={{1,0},{2,1},{3,2},{5,4},{6,5},{7,6},{9,8},{10,9},{11,10},{13,12},{... | collective-permute-start | bytes 36872 | tf_op jit(solution)/shard_map/ppermute | solution.py:1233
  34.7 35.5 %collective-permute-start.13 = (f32[6,10,64]{2,0,1:T(8,128)S(1)}, f32[6,10,64]{2,0,1:T(8,128)S(1)}, u32[]{:S(2)}, u32[]{:S(2)}) collective-permute-start(f32[6,10,64]{2,0,1:T(8,128)S(1)} %copy-done.39), channel_id=1, source_target_pairs={{0,2},{1,3},{2,0},{3,1},{4,6},{5,7},{6,4},{7,5},{8,10},{9,11},{10,... | collective-permute-start | bytes 46088 | tf_op jit(solution)/shard_map/ppermute | solution.py:1145
  43.8 27.1 %collective-permute-start.12 = (f32[6,10,64]{2,0,1:T(8,128)S(1)}, f32[6,10,64]{2,0,1:T(8,128)S(1)}, u32[]{:S(2)}, u32[]{:S(2)}) collective-permute-start(f32[6,10,64]{2,0,1:T(8,128)S(1)} %copy-done.39), channel_id=1, source_target_pairs={{0,1},{1,0},{2,3},{3,2},{4,5},{5,4},{6,7},{7,6},{8,9},{9,8},{10,11... | collective-permute-start | bytes 46088 | tf_op jit(solution)/shard_map/ppermute | solution.py:1145
  44.9 23.3 %collective-permute-start.10 = (bf16[6,80,768]{2,1,0:T(8,128)(2,1)S(1)}, bf16[6,80,768]{2,1,0:T(8,128)(2,1)}, u32[]{:S(2)}, u32[]{:S(2)}) collective-permute-start(bf16[6,80,768]{2,1,0:T(8,128)(2,1)S(1)} %pick.1), channel_id=1, source_target_pairs={{0,2},{1,3},{2,0},{3,1},{4,6},{5,7},{6,4},{7,5},{8,10},{9,11},{10,... | collective-permute-start | bytes 2211848 | tf_op jit(solution)/shard_map/ppermute | solution.py:1145
  53.7 21.7 %collective-permute-start.9 = (bf16[6,80,768]{2,1,0:T(8,128)(2,1)S(1)}, bf16[6,80,768]{2,1,0:T(8,128)(2,1)}, u32[]{:S(2)}, u32[]{:S(2)}) collective-permute-start(bf16[6,80,768]{2,1,0:T(8,128)(2,1)S(1)} %pick.1), channel_id=1, source_target_pairs={{0,1},{1,0},{2,3},{3,2},{4,5},{5,4},{6,7},{7,6},{8,9},{9,8},{10,11... | collective-permute-start | bytes 2211848 | tf_op jit(solution)/shard_map/ppermute | solution.py:1145
  100.1 14.7 %collective-permute-start.15 = (bf16[1608,128]{1,0:T(8,128)(2,1)S(1)}, bf16[1608,128]{1,0:T(8,128)(2,1)S(1)}, u32[]{:S(2)}, u32[]{:S(2)}) collective-permute-start(bf16[1608,128]{1,0:T(8,128)(2,1)S(1)} %pad_maximum_fusion.4.refs_4_), channel_id=1, source_target_pairs={{0,2},{1,3},{2,0},{3,1},{4,6},{5,7},{6,4},{7,5},{8,10},{9,11},{10,... | collective-permute-start | bytes 1234952 | tf_op jit(solution)/shard_map/ppermute | solution.py:1145
  100.9 13.9 %collective-permute-start.16 = (bf16[1608,128]{1,0:T(8,128)(2,1)S(1)}, bf16[1608,128]{1,0:T(8,128)(2,1)S(1)}, u32[]{:S(2)}, u32[]{:S(2)}) collective-permute-start(bf16[1608,128]{1,0:T(8,128)(2,1)S(1)} %pad_maximum_fusion.4.refs_4_), channel_id=1, source_target_pairs={{0,1},{1,0},{2,3},{3,2},{4,5},{5,4},{6,7},{7,6},{8,9},{9,8},{10,11... | collective-permute-start | bytes 1234952 | tf_op jit(solution)/shard_map/ppermute | solution.py:1145
  162.3 13.3 %collective-permute-start.18 = (bf16[1536,128]{1,0:T(8,128)(2,1)}, bf16[1536,128]{1,0:T(8,128)(2,1)S(1)}, u32[]{:S(2)}, u32[]{:S(2)}) collective-permute-start(bf16[1536,128]{1,0:T(8,128)(2,1)} %get-tuple-element.124.refs_4_), channel_id=1, source_target_pairs={{0,2},{1,3},{2,0},{3,1},{4,6},{5,7},{6,4},{7,5},{8,10},{9,11},{10,... | collective-permute-start | bytes 1179656 | tf_op jit(solution)/shard_map/ppermute | solution.py:1145
  182.1 27.8 %collective-permute-start.20 = (bf16[768,768]{1,0:T(8,128)(2,1)S(1)}, bf16[768,768]{1,0:T(8,128)(2,1)S(1)}, u32[]{:S(2)}, u32[]{:S(2)}) collective-permute-start(bf16[768,768]{1,0:T(8,128)(2,1)S(1)} %fusion.13), channel_id=1, source_target_pairs={{0,2},{1,3},{2,0},{3,1},{4,6},{5,7},{6,4},{7,5},{8,10},{9,11},{10,... | collective-permute-start | bytes 3538952 | tf_op jit(solution)/shard_map/ppermute | solution.py:1145
  212.3 27.0 %collective-permute-start.23 = (bf16[4,128,768]{2,1,0:T(8,128)(2,1)S(1)}, bf16[4,128,768]{2,1,0:T(8,128)(2,1)}, u32[]{:S(2)}, u32[]{:S(2)}) collective-permute-start(bf16[4,128,768]{2,1,0:T(8,128)(2,1)S(1)} %get-tuple-element.138), channel_id=1, source_target_pairs={{0,4},{4,0},{8,12},{12,8},{16,20},{20,16},{24,28},{28,24},{1,5},{5... | collective-permute-start | bytes 2359304 | tf_op jit(solution)/shard_map/ppermute | solution.py:1145
  243.0 29.4 %collective-permute-start.26 = (bf16[2,128,768]{2,1,0:T(8,128)(2,1)S(1)}, bf16[2,128,768]{2,1,0:T(8,128)(2,1)S(1)}, u32[]{:S(2)}, u32[]{:S(2)}) collective-permute-start(bf16[2,128,768]{2,1,0:T(8,128)(2,1)S(1)} %slice.354), channel_id=1, source_target_pairs={{0,16},{4,20},{8,24},{12,28},{16,0},{20,4},{24,8},{28,12},{1,17},{... | collective-permute-start | bytes 1179656 | tf_op jit(solution)/shard_map/ppermute | solution.py:1145
  282.8 17.9 %collective-permute-start.28 = (bf16[480,768]{1,0:T(8,128)(2,1)}, bf16[480,768]{1,0:T(8,128)(2,1)}, u32[]{:S(2)}, u32[]{:S(2)}) collective-permute-start(bf16[480,768]{1,0:T(8,128)(2,1)} %fusion.12), channel_id=1, source_target_pairs={{0,2},{1,3},{2,0},{3,1},{4,6},{5,7},{6,4},{7,5},{8,10},{9,11},{10,... | collective-permute-start | bytes 2211848 | tf_op jit(solution)/shard_map/ppermute | solution.py:1145
  286.9 10.5 %collective-permute-start.29 = (bf16[128,768]{1,0:T(8,128)(2,1)}, bf16[128,768]{1,0:T(8,128)(2,1)}, u32[]{:S(2)}, u32[]{:S(2)}) collective-permute-start(bf16[128,768]{1,0:T(8,128)(2,1)} %fusion.20), channel_id=1, source_target_pairs={{0,8},{4,12},{8,0},{12,4},{16,24},{20,28},{24,16},{28,20},{1,9},{5... | collective-permute-start | bytes 589832 | tf_op jit(solution)/shard_map/ppermute | solution.py:1145
  301.4 10.8 %collective-permute-start.31 = (f32[8,768]{1,0:T(8,128)S(1)}, f32[8,768]{1,0:T(8,128)S(1)}, u32[]{:S(2)}, u32[]{:S(2)}) collective-permute-start(f32[8,768]{1,0:T(8,128)S(1)} %get-tuple-element.322), channel_id=1, source_target_pairs={{1,0},{2,1},{3,2},{5,4},{6,5},{7,6},{9,8},{10,9},{11,10},{13,12},{... | collective-permute-start | bytes 73736 | tf_op jit(solution)/shard_map/ppermute | solution.py:1401
  304.7 15.8 %collective-permute-start.30 = (f32[8,768]{1,0:T(8,128)S(1)}, f32[8,768]{1,0:T(8,128)S(1)}, u32[]{:S(2)}, u32[]{:S(2)}) collective-permute-start(f32[8,768]{1,0:T(8,128)S(1)} %get-tuple-element.321), channel_id=1, source_target_pairs={{0,1},{1,2},{2,3},{4,5},{5,6},{6,7},{8,9},{9,10},{10,11},{12,13},{... | collective-permute-start | bytes 73736 | tf_op jit(solution)/shard_map/ppermute | solution.py:1400
  317.2 7.3 %collective-permute-start.40 = (bf16[80,768]{1,0:T(8,128)(2,1)S(1)}, bf16[80,768]{1,0:T(8,128)(2,1)S(1)}, u32[]{:S(2)}, u32[]{:S(2)}) collective-permute-start(bf16[80,768]{1,0:T(8,128)(2,1)S(1)} %get-tuple-element.179), channel_id=1, source_target_pairs={{0,28},{4,24},{8,20},{12,16},{16,12},{20,8},{24,4},{28,0},{1,29},{... | collective-permute-start | bytes 368648 | tf_op jit(solution)/shard_map/ppermute | solution.py:1145
  318.4 7.6 %collective-permute-start.39 = (bf16[80,768]{1,0:T(8,128)(2,1)S(1)}, bf16[80,768]{1,0:T(8,128)(2,1)S(1)}, u32[]{:S(2)}, u32[]{:S(2)}) collective-permute-start(bf16[80,768]{1,0:T(8,128)(2,1)S(1)} %get-tuple-element.178), channel_id=1, source_target_pairs={{0,24},{4,28},{8,16},{12,20},{16,8},{20,12},{24,0},{28,4},{1,25},{... | collective-permute-start | bytes 368648 | tf_op jit(solution)/shard_map/ppermute | solution.py:1145
  321.1 15.9 %collective-permute-start.38 = (bf16[80,768]{1,0:T(8,128)(2,1)S(1)}, bf16[80,768]{1,0:T(8,128)(2,1)S(1)}, u32[]{:S(2)}, u32[]{:S(2)}) collective-permute-start(bf16[80,768]{1,0:T(8,128)(2,1)S(1)} %get-tuple-element.177), channel_id=1, source_target_pairs={{0,20},{4,16},{8,28},{12,24},{16,4},{20,0},{24,12},{28,8},{1,21},{... | collective-permute-start | bytes 368648 | tf_op jit(solution)/shard_map/ppermute | solution.py:1145
  321.2 17.8 %collective-permute-start.37 = (bf16[80,768]{1,0:T(8,128)(2,1)S(1)}, bf16[80,768]{1,0:T(8,128)(2,1)S(1)}, u32[]{:S(2)}, u32[]{:S(2)}) collective-permute-start(bf16[80,768]{1,0:T(8,128)(2,1)S(1)} %get-tuple-element.176), channel_id=1, source_target_pairs={{0,16},{4,20},{8,24},{12,28},{16,0},{20,4},{24,8},{28,12},{1,17},{... | collective-permute-start | bytes 368648 | tf_op jit(solution)/shard_map/ppermute | solution.py:1145
  324.5 14.6 %collective-permute-start.36 = (bf16[80,768]{1,0:T(8,128)(2,1)S(1)}, bf16[80,768]{1,0:T(8,128)(2,1)S(1)}, u32[]{:S(2)}, u32[]{:S(2)}) collective-permute-start(bf16[80,768]{1,0:T(8,128)(2,1)S(1)} %get-tuple-element.175), channel_id=1, source_target_pairs={{0,12},{4,8},{8,4},{12,0},{16,28},{20,24},{24,20},{28,16},{1,13},{... | collective-permute-start | bytes 368648 | tf_op jit(solution)/shard_map/ppermute | solution.py:1145
  324.5 14.6 %collective-permute-start.35 = (bf16[80,768]{1,0:T(8,128)(2,1)S(1)}, bf16[80,768]{1,0:T(8,128)(2,1)S(1)}, u32[]{:S(2)}, u32[]{:S(2)}) collective-permute-start(bf16[80,768]{1,0:T(8,128)(2,1)S(1)} %get-tuple-element.174), channel_id=1, source_target_pairs={{0,8},{4,12},{8,0},{12,4},{16,24},{20,28},{24,16},{28,20},{1,9},{5... | collective-permute-start | bytes 368648 | tf_op jit(solution)/shard_map/ppermute | solution.py:1145
  325.9 13.1 %collective-permute-start.34 = (bf16[80,768]{1,0:T(8,128)(2,1)S(1)}, bf16[80,768]{1,0:T(8,128)(2,1)S(1)}, u32[]{:S(2)}, u32[]{:S(2)}) collective-permute-start(bf16[80,768]{1,0:T(8,128)(2,1)S(1)} %get-tuple-element.173), channel_id=1, source_target_pairs={{0,4},{4,0},{8,12},{12,8},{16,20},{20,16},{24,28},{28,24},{1,5},{5... | collective-permute-start | bytes 368648 | tf_op jit(solution)/shard_map/ppermute | solution.py:1145
  354.5 11.8 %collective-permute-start.45 = (bf16[16,16,768]{2,1,0:T(8,128)(2,1)S(1)}, bf16[16,16,768]{2,1,0:T(8,128)(2,1)S(1)}, u32[]{:S(2)}, u32[]{:S(2)}) collective-permute-start(bf16[16,16,768]{2,1,0:T(8,128)(2,1)S(1)} %get-tuple-element.339), channel_id=1, source_target_pairs={{0,1},{1,0},{2,3},{3,2},{4,5},{5,4},{6,7},{7,6},{8,9},{9,8},{10,11... | collective-permute-start | bytes 1179656 | tf_op jit(solution)/shard_map/ppermute | solution.py:1145
  (85 other events, 716.4 us)
Sparse Core Ops, SparseCore 0:
  10.9 84.3 all-gather.2

commit v4 on v3

--- a/solution.py
+++ b/solution.py
@@ -99,7 +99,7 @@
 
 
 def key_kernel(nx_ref, w_ref, taps_ref, p_ref, u_ref, k_ref, st_ref):
-    tokens = u_ref.shape[1]
+    tokens = k_ref.shape[1]
     proj = nt(w_ref[...], nx_ref[...])
     pre = conv_taps(proj, taps_ref[...], -1)
     key = pre * sigmoid(pre)
@@ -109,7 +109,7 @@
     b_r = key[2 * NS : 3 * NS, :tokens].astype(bf16)
     c_r = pltpu.roll(key[3 * NS :], ext - 1, axis=1)[:, :tokens].astype(bf16)
     p_ref[...] = proj
-    u_ref[...] = pre[:, :tokens]
+    u_ref[...] = pre
     k_ref[...] = jnp.concatenate([b_f, c_f, b_r, c_r], axis=0)
     lower, upper = causal_masks()
     for blk in range(tokens // BL):
@@ -126,7 +126,7 @@
         key_kernel,
         out_shape=(
             jax.ShapeDtypeStruct((4 * NS, ext), f32),
-            jax.ShapeDtypeStruct((4 * NS, tokens), f32),
+            jax.ShapeDtypeStruct((4 * NS, ext), f32),
             jax.ShapeDtypeStruct((4 * NS, tokens), bf16),
             jax.ShapeDtypeStruct((blocks, BL, BL), f32),
         ),
@@ -802,33 +802,34 @@
     )(dvi, v, do, u, ds9, k4, rows, rci, rcc, x9, dki, cols, after)
 
 
-def key_pre_kernel(dk_ref, u_ref, edge_ref, out_ref):
-    tokens = u_ref.shape[1]
-    lane = lax.broadcasted_iota(jnp.int32, (NS, tokens), 1)
-    d_cf = pltpu.roll(dk_ref[NS : 2 * NS, :], tokens - 1, axis=1)
-    d_cf = jnp.where(lane == tokens - 1, edge_ref[:, 0:1], d_cf)
-    d_cr = pltpu.roll(dk_ref[3 * NS :, :], 1, axis=1)
-    d_cr = jnp.where(lane == 0, edge_ref[:, 1:2], d_cr)
-    grad = jnp.concatenate([dk_ref[:NS, :], d_cf, dk_ref[2 * NS : 3 * NS, :], d_cr], axis=0)
+def key_pre_kernel(dk_ref, u_ref, out_ref):
+    ext = u_ref.shape[1]
+    tail = jnp.zeros((4 * NS, ext - dk_ref.shape[1]), f32)
+    wide = jnp.concatenate([dk_ref[...], tail], axis=1)
+    d_cf = pltpu.roll(wide[NS : 2 * NS], ext - 1, axis=1)
+    d_cr = pltpu.roll(wide[3 * NS :], 1, axis=1)
+    grad = jnp.concatenate([wide[:NS], d_cf, wide[2 * NS : 3 * NS], d_cr], axis=0)
     pre = u_ref[...]
     soft = sigmoid(pre)
     out_ref[...] = grad * (soft * (1.0 + pre * (1.0 - soft)))
 
 
-def key_pre_stage(dk, u, edge):
+def key_pre_stage(dk, u):
     return pl.pallas_call(
         key_pre_kernel,
         out_shape=jax.ShapeDtypeStruct(u.shape, f32),
         compiler_params=pltpu.CompilerParams(vmem_limit_bytes=16 * 1024 * 1024),
         cost_estimate=cost(3),
         name="key_pre",
-    )(dk, u, edge)
+    )(dk, u)
 
 
 def conv_back_rows(dpre, taps, signal):
     rows, tokens = dpre.shape
     ext = signal.shape[1]
-    wide = jnp.concatenate([dpre, jnp.zeros((rows, ext - tokens), dpre.dtype)], axis=1)
+    wide = dpre
+    if tokens < ext:
+        wide = jnp.concatenate([dpre, jnp.zeros((rows, ext - tokens), dpre.dtype)], axis=1)
     total = None
     sums = []
     for k in range(K):
@@ -1293,8 +1294,6 @@
         else:
             do_back = do_t
         dvi, rci, dki = intra_back_stage(v, do_back, rows, scores, k4, dkc)
-        to_prev = lax.ppermute(dki[NS : 2 * NS, :1].reshape(1, NS), "mp", prevs)
-        to_next = lax.ppermute(dki[3 * NS :, tokens - 1 :].reshape(1, NS), "mp", nexts)
         if direct:
             messages = [dsdev, near_d, far_d, swap(far_d, "mp", n_mp, 1)]
         else:
@@ -1325,12 +1324,8 @@
         dpre, dx, dk = cross_back_stage(
             dvi, v, do_t, u, ds9, k4, rows, rci, rcc, x9, dki, cols, after
         )
-        d_last, d_first = to_prev, to_next
-        d_last = jnp.where(ends, 0.0, d_last)
-        d_first = jnp.where(starts, 0.0, d_first)
-        edge = jnp.transpose(jnp.concatenate([d_last, d_first, jnp.zeros((6, NS), f32)], axis=0))
         if direct:
-            keep_go, dpre, dk, edge = lax.optimization_barrier((keep_go, dpre, dk, edge))
+            keep_go, dpre, dk = lax.optimization_barrier((keep_go, dpre, dk))
             far_go = swap(keep_go[2:].astype(bf16), "dp", n_dp, 4)
         grad_v, dn_value, tap_v = value_back_stage(dpre, taps_v, s, dx, nx, wv)
         if direct:
@@ -1342,7 +1337,7 @@
             away_v = (both[2].astype(f32) + got_v[1].astype(f32)).astype(bf16)
             away_v, dk = lax.optimization_barrier((away_v, dk))
             far_v = swap(away_v, "mp", n_mp, 2)
-        dpre_k = key_pre_stage(dk, key_u, edge)
+        dpre_k = key_pre_stage(dk, key_u)
         grad_key, dn_key, tap_key = key_back_stage(meta, dpre_k, taps_k, key_proj, nx, key_low)
         if direct:
             far_v, last_go, grad_key, dn_key, tap_key = lax.optimization_barrier(

time: 391 us -> 386 us (0.987)
    ppermute x2 -> x0, starting transfers between devices: 5.28 us -> none  [the longest x1 3.37 us: local(): lax.ppermute(dki[3 * NS:, tokens - 1:].reshape(1, NS), 'mp', nexts)]
    unnamed x149 -> x147, local copies, waits for them, and re-layouts: 21.3 us -> 21.4 us
  transfers between devices with their start and end apart: 47 -> 45, of which waited for: 15 -> 16; matrix products, arithmetic and copies ran while one was open for 13% -> 13% of each run, Pallas kernels for 32% -> 32%
where the time goes in v4:
time: 386 us; the launch traced here: 379 us
  Pallas kernels  164 us (42%)
  starting transfers between devices  58.9 us (15%)
  waiting for transfers between devices  56.8 us (15%)
  other arithmetic  43.6 us (11%)
  local copies, waits for them, and re-layouts  39.4 us (10%)
  between operations  16.1 us (4%)
    ppermute x40, waiting for transfers between devices, swap(): return lax.ppermute(x, axis, [(i, i ^ bit) for i in range(size)])  56.8 us
    ppermute x40, starting transfers between devices, swap(): return lax.ppermute(x, axis, [(i, i ^ bit) for i in range(size)])  46.5 us
    pallas_call x1, Pallas kernels, token_stage(): pl.pallas_call(token_kernel, grid=(blocks // two,), in_specs=[chan, chan,...  32.3 us
    pallas_call x1, Pallas kernels, value_back_stage(): pl.pallas_call(value_back_kernel, grid=(NG,), in_specs=[pl.BlockSpec((row...  26.3 us
    unnamed x147, local copies, waits for them, and re-layouts  21.4 us
    pallas_call x1, Pallas kernels, value_stage(): pl.pallas_call(value_kernel, grid=(NG,), in_specs=[pl.BlockSpec((ext, D),...  19.3 us
    pallas_call x1, Pallas kernels, intra_back_stage(): pl.pallas_call(intra_back_kernel, grid=(tokens // BL,), in_specs=[chan, c...  15.8 us
    pallas_call x1, Pallas kernels, cross_back_stage(): pl.pallas_call(cross_back_kernel, grid=(tokens // BL,), in_specs=[chan, c...  15.3 us
  transfers between devices with their start and end apart: 45, of which 16 were waited for; matrix products, arithmetic and copies ran while one was open for 13% of the time, Pallas kernels for 32%

profile of v4, /device:TPU:1, one launch (start us, length us, event | category | flops | bytes accessed | tf_op | source)
XLA Modules:
  0.0 378.6 jit_solution(1400314119674473478)
XLA Ops:
  17.9 4.8 %collective-permute-start.1 = (bf16[8,768]{1,0:T(8,128)(2,1)S(1)}, bf16[8,768]{1,0:T(8,128)(2,1)S(1)}, u32[]{:S(2)}, u32[]{:S(2)}) collective-permute-start(bf16[8,768]{1,0:T(8,128)(2,1)S(1)} %get-tuple-element.326), channel_id=1, source_target_pairs={{0,1},{1,2},{2,3},{4,5},{5,6},{6,7},{8,9},{9,10},{10,11},{12,13},{... | collective-permute-start | bytes 36872 | tf_op jit(solution)/shard_map/ppermute | solution.py:1233
  28.0 3.3 collective-permute-start.7
  34.8 8.7 %collective-permute-done.6 = bf16[80,768]{1,0:T(8,128)(2,1)S(1)} collective-permute-done((bf16[80,768]{1,0:T(8,128)(2,1)S(1)}, bf16[80,768]{1,0:T(8,128)(2,1)S(1)}, u32[]{:S(2)}, u32[]{:S(2)}) %collective-permute-start.6) | collective-permute-done | bytes 122912 | tf_op jit(solution)/shard_map/ppermute | solution.py:1146
  46.1 3.5 key_stage.1
  53.4 14.5 %collective-permute-done.10 = bf16[6,80,768]{2,1,0:T(8,128)(2,1)} collective-permute-done((bf16[6,80,768]{2,1,0:T(8,128)(2,1)S(1)}, bf16[6,80,768]{2,1,0:T(8,128)(2,1)}, u32[]{:S(2)}, u32[]{:S(2)}) %collective-permute-start.10) | collective-permute-done | bytes 737312 | tf_op jit(solution)/shard_map/ppermute | solution.py:1146
  75.8 3.5 pad_maximum_fusion.wv_ref
  79.3 19.3 %value_stage.1 = (bf16[1536,1024]{1,0:T(8,128)(2,1)}, bf16[1536,1024]{1,0:T(8,128)(2,1)}, bf16[1536,1152]{1,0:T(8,128)(2,1)}, f32[12,24,1024]{2,1,0:T(8,128)}, f...) custom-call(bf16[1152,768]{1,0:T(8,128)(2,1)} %copy-done, ...), custom_call_target="tpu_custom_call" | custom-call | bytes 27000000 | tf_op jit(solution)/shard_map/value_stage/pallas_call | solution.py:223
  103.1 11.9 %intra_stage.1.oi_ref = bf16[1536,1024]{1,0:T(8,128)(2,1)} custom-call(bf16[1536,1024]{1,0:T(8,128)(2,1)} %get-tuple-element.109.v_ref, f32[12,24,1024]{2,1,0:T(8,128)} %get-tuple-element.110.rows_ref, f32[8,128,128]{2,1,0:T(8,128)} %copy-done.19), custom_call_target="tpu_custom_call" | custom-call | bytes 12000000 | tf_op jit(solution)/shard_map/intra_stage/pallas_call | solution.py:393
  117.6 6.6 %chain_stage.1.s_ref.refs_8_ = bf16[9,1536,128]{2,1,0:T(8,128)(2,1)} custom-call(s32[6]{0:T(128)} %pad_add_fusion.refs_0_.meta_ref, bf16[8,1536,128]{2,1,0:T(8,128)(2,1)} %get-tuple-element.113.refs_1_, f32[8,24,128]{2,1,0:T(8,128)} %get-tuple-element.114.refs_2_.tot_ref, f32[4,72,128]{2,1,0:T(8,128)} %maximum_convert_fusion.refs_3_, ...), custom_call_target="tpu_custom_call" | custom-call | bytes 7000000 | tf_op jit(solution)/shard_map/chain_stage/pallas_call | solution.py:349
  124.2 5.9 %pick_two.1 = (bf16[24,64,768]{2,1,0:T(8,128)(2,1)}, bf16[24,64,768]{2,1,0:T(8,128)(2,1)}) custom-call(s32[24]{0:T(128)} %fusion.39.index_ref, bf16[32,128,768]{2,1,0:T(8,128)(2,1)} %bitcast.167), custom_call_target="tpu_custom_call" | custom-call | bytes 6000000 | tf_op jit(solution)/shard_map/pick_two/pallas_call | solution.py:1019
  130.1 32.3 %token_stage.1 = (bf16[1024,768]{1,0:T(8,128)(2,1)}, bf16[1536,1024]{1,0:T(8,128)(2,1)}, bf16[1536,1024]{1,0:T(8,128)(2,1)}, bf16[1536,1024]{1,0:T(8,128)(2,1)},...) custom-call(bf16[1536,1024]{1,0:T(8,128)(2,1)} %intra_stage.1.oi_ref, ...), custom_call_target="tpu_custom_call" | custom-call | bytes 35000000 | tf_op jit(solution)/shard_map/token_stage/pallas_call | solution.py:531
  167.4 8.6 %early_grad.1 = (bf16[24,128,768]{2,1,0:T(8,128)(2,1)S(1)}, f32[1024,768]{1,0:T(8,128)S(1)}) custom-call(bf16[1536,1024]{1,0:T(8,128)(2,1)S(1)} %copy-done.14, bf16[1536,1024]{1,0:T(8,128)(2,1)S(1)} %copy-done.13, bf16[1152,768]{1,0:T(8,128)(2,1)S(1)} %copy-done.1, bf16[1024,768]{1,0:T(8,128)(2,1)S(1)} %copy-done.3, bf16[1536,768]{1,0:T(8,128)(2,1)S(1)} %bitcast.152), custom_call_target="tpu_custom_call" | custom-call | bytes 12000000 | tf_op jit(solution)/shard_map/early_grad/pallas_call | solution.py:601
  178.1 4.2 %collective-permute-done.19 = bf16[2,768,768]{2,1,0:T(8,128)(2,1)S(1)} collective-permute-done((bf16[2,768,768]{2,1,0:T(8,128)(2,1)S(1)}, bf16[2,768,768]{2,1,0:T(8,128)(2,1)S(1)}, u32[]{:S(2)}, u32[]{:S(2)}) %collective-permute-start.19) | collective-permute-done | bytes 2359328 | tf_op jit(solution)/shard_map/ppermute | solution.py:1146
  186.4 7.9 %chain_back.1 = (bf16[8,1536,128]{2,1,0:T(8,128)(2,1)}, f32[8,24,128]{2,1,0:T(8,128)}) custom-call(s32[6]{0:T(128)} %pad_add_fusion.refs_0_.meta_ref, bf16[8,1536,128]{2,1,0:T(8,128)(2,1)} %get-tuple-element.126.refs_1_, f32[8,24,128]{2,1,0:T(8,128)} %get-tuple-element.114.refs_2_.tot_ref, f32[4,72,128]{2,1,0:T(8,128)} %maximum_convert_fusion.refs_3_, ...), custom_call_target="tpu_custom_call" | custom-call | bytes 7000000 | tf_op jit(solution)/shard_map/chain_back/pallas_call | solution.py:349
  194.3 15.8 %intra_back.1 = (bf16[1536,1024]{1,0:T(8,128)(2,1)}, f32[4,24,1024]{2,1,0:T(8,128)}, f32[256,1024]{1,0:T(8,128)}) custom-call(bf16[1536,1024]{1,0:T(8,128)(2,1)} %get-tuple-element.109.v_ref, bf16[1536,1024]{1,0:T(8,128)(2,1)} %get-tuple-element.130.do_ref, f32[12,24,1024]{2,1,0:T(8,128)} %get-tuple-element.110.rows_ref, f32[8,128,128]{2,1,0:T(8,128)} %copy-done.19, ...), custom_call_target="tpu_custom_call" | custom-call | bytes 18000000 | tf_op jit(solution)/shard_map/intra_back/pallas_call | solution.py:679
  214.5 15.3 %cross_back.1 = (bf16[1536,1024]{1,0:T(8,128)(2,1)}, f32[2,24,1024]{2,1,0:T(8,128)}, f32[256,1024]{1,0:T(8,128)}) custom-call(bf16[1536,1024]{1,0:T(8,128)(2,1)} %get-tuple-element.138.dvi_ref, bf16[1536,1024]{1,0:T(8,128)(2,1)} %get-tuple-element.109.v_ref, bf16[1536,1024]{1,0:T(8,128)(2,1)} %get-tuple-element.130.do_ref, ...), custom_call_target="tpu_custom_call" | custom-call | bytes 16000000 | tf_op jit(solution)/shard_map/cross_back/pallas_call | solution.py:769
  231.0 3.5 collective-permute-start.24
  234.6 26.3 %value_back.1 = (bf16[24,80,768]{2,1,0:T(8,128)(2,1)}, f32[1152,768]{1,0:T(8,128)}, f32[3,8,512]{2,1,0:T(8,128)}) custom-call(bf16[1536,1024]{1,0:T(8,128)(2,1)} %get-tuple-element.148.dpre_ref, f32[1536,8]{1,0:T(8,128)} %pad.22.taps_ref, bf16[1536,1152]{1,0:T(8,128)(2,1)} %get-tuple-element.149.s_ref, f32[2,24,1024]{2,1,0:T(8,128)} %get-tuple-element.150.dx_ref, ...), custom_call_target="tpu_custom_call" | custom-call | bytes 27000000 | tf_op jit(solution)/shard_map/value_back/pallas_call | solution.py:947
  260.9 3.0 fusion.46
  285.2 4.5 %key_back.1 = (bf16[4,64,768]{2,1,0:T(8,128)(2,1)S(1)}, f32[1152,768]{1,0:T(8,128)S(1)}, f32[8,256]{1,0:T(8,128)S(1)}) custom-call(s32[6]{0:T(128)S(1)} %copy-done.28, f32[256,1152]{1,0:T(8,128)S(1)} %key_pre.1.dpre_ref, f32[256,8]{1,0:T(8,128)S(1)} %pad.21.taps_ref, f32[256,1152]{1,0:T(8,128)S(1)} %copy-done.21, bf16[1152,768]{1,0:T(8,128)(2,1)S(1)} %copy-done.2, ...), custom_call_target="tpu_custom_call" | custom-call | bytes 8000000 | tf_op jit(solution)/shard_map/key_back/pallas_call | solution.py:882
  290.4 2.6 collective-permute-done.26
  293.8 2.7 collective-permute-start.29
  296.5 3.0 collective-permute-start.28
  307.3 2.9 collective-permute-done.31
  320.9 3.8 fusion.8
  324.7 6.7 %collective-permute-done.36 = bf16[80,768]{1,0:T(8,128)(2,1)S(1)} collective-permute-done((bf16[80,768]{1,0:T(8,128)(2,1)S(1)}, bf16[80,768]{1,0:T(8,128)(2,1)S(1)}, u32[]{:S(2)}, u32[]{:S(2)}) %collective-permute-start.36) | collective-permute-done | bytes 122912 | tf_op jit(solution)/shard_map/ppermute | solution.py:1146
  331.4 3.0 collective-permute-done.35
  338.6 2.7 collective-permute-done.40
  341.6 3.3 collective-permute-done.41
  345.7 3.8 %collective-permute-done.42 = bf16[8,16,768]{2,1,0:T(8,128)(2,1)S(1)} collective-permute-done((bf16[8,16,768]{2,1,0:T(8,128)(2,1)S(1)}, bf16[8,16,768]{2,1,0:T(8,128)(2,1)S(1)}, u32[]{:S(2)}, u32[]{:S(2)}) %collective-permute-start.42) | collective-permute-done | bytes 196640 | tf_op jit(solution)/shard_map/ppermute | solution.py:1146
  349.5 8.6 %collective-permute-start.43 = (bf16[16,16,768]{2,1,0:T(8,128)(2,1)S(1)}, bf16[16,16,768]{2,1,0:T(8,128)(2,1)S(1)}, u32[]{:S(2)}, u32[]{:S(2)}) collective-permute-start(bf16[16,16,768]{2,1,0:T(8,128)(2,1)S(1)} %get-tuple-element.335), channel_id=1, source_target_pairs={{0,1},{1,0},{2,3},{3,2},{4,5},{5,4},{6,7},{7,6},{8,9},{9,8},{10,11... | collective-permute-start | bytes 1179656 | tf_op jit(solution)/shard_map/ppermute | solution.py:1146
  361.2 3.0 finish_stage.1
  (358 shorter events, 113.2 us)
Async XLA Ops:
  7.2 117.0 %all-gather.3.cloned.1.call-start = ((), (), s32[]{:S(2)}) async-start(), calls=%async_computation | async-start | bytes 6488064 | tf_op jit(solution)/shard_map/all_gather | solution.py:1215
  9.3 18.7 %collective-permute-start.2 = (bf16[80,768]{1,0:T(8,128)(2,1)S(1)}, bf16[80,768]{1,0:T(8,128)(2,1)S(1)}, u32[]{:S(2)}, u32[]{:S(2)}) collective-permute-start(bf16[80,768]{1,0:T(8,128)(2,1)S(1)} %get-tuple-element.339), channel_id=1, source_target_pairs={{0,4},{4,0},{8,12},{12,8},{16,20},{20,16},{24,28},{28,24},{1,5},{5... | collective-permute-start | bytes 368648 | tf_op jit(solution)/shard_map/ppermute | solution.py:1146
  11.4 19.9 %collective-permute-start.3 = (bf16[80,768]{1,0:T(8,128)(2,1)S(1)}, bf16[80,768]{1,0:T(8,128)(2,1)S(1)}, u32[]{:S(2)}, u32[]{:S(2)}) collective-permute-start(bf16[80,768]{1,0:T(8,128)(2,1)S(1)} %get-tuple-element.339), channel_id=1, source_target_pairs={{0,8},{4,12},{8,0},{12,4},{16,24},{20,28},{24,16},{28,20},{1,9},{5... | collective-permute-start | bytes 368648 | tf_op jit(solution)/shard_map/ppermute | solution.py:1146
  12.7 18.6 %collective-permute-start.4 = (bf16[80,768]{1,0:T(8,128)(2,1)S(1)}, bf16[80,768]{1,0:T(8,128)(2,1)S(1)}, u32[]{:S(2)}, u32[]{:S(2)}) collective-permute-start(bf16[80,768]{1,0:T(8,128)(2,1)S(1)} %get-tuple-element.339), channel_id=1, source_target_pairs={{0,12},{4,8},{8,4},{12,0},{16,28},{20,24},{24,20},{28,16},{1,13},{... | collective-permute-start | bytes 368648 | tf_op jit(solution)/shard_map/ppermute | solution.py:1146
  12.7 21.2 %collective-permute-start.5 = (bf16[80,768]{1,0:T(8,128)(2,1)S(1)}, bf16[80,768]{1,0:T(8,128)(2,1)S(1)}, u32[]{:S(2)}, u32[]{:S(2)}) collective-permute-start(bf16[80,768]{1,0:T(8,128)(2,1)S(1)} %get-tuple-element.339), channel_id=1, source_target_pairs={{0,16},{4,20},{8,24},{12,28},{16,0},{20,4},{24,8},{28,12},{1,17},{... | collective-permute-start | bytes 368648 | tf_op jit(solution)/shard_map/ppermute | solution.py:1146
  17.9 9.1 %collective-permute-start.1 = (bf16[8,768]{1,0:T(8,128)(2,1)S(1)}, bf16[8,768]{1,0:T(8,128)(2,1)S(1)}, u32[]{:S(2)}, u32[]{:S(2)}) collective-permute-start(bf16[8,768]{1,0:T(8,128)(2,1)S(1)} %get-tuple-element.326), channel_id=1, source_target_pairs={{0,1},{1,2},{2,3},{4,5},{5,6},{6,7},{8,9},{9,10},{10,11},{12,13},{... | collective-permute-start | bytes 36872 | tf_op jit(solution)/shard_map/ppermute | solution.py:1233
  26.9 16.6 %collective-permute-start.6 = (bf16[80,768]{1,0:T(8,128)(2,1)S(1)}, bf16[80,768]{1,0:T(8,128)(2,1)S(1)}, u32[]{:S(2)}, u32[]{:S(2)}) collective-permute-start(bf16[80,768]{1,0:T(8,128)(2,1)S(1)} %get-tuple-element.339), channel_id=1, source_target_pairs={{0,20},{4,16},{8,28},{12,24},{16,4},{20,0},{24,12},{28,8},{1,21},{... | collective-permute-start | bytes 368648 | tf_op jit(solution)/shard_map/ppermute | solution.py:1146
  28.0 15.5 %collective-permute-start.7 = (bf16[80,768]{1,0:T(8,128)(2,1)S(1)}, bf16[80,768]{1,0:T(8,128)(2,1)S(1)}, u32[]{:S(2)}, u32[]{:S(2)}) collective-permute-start(bf16[80,768]{1,0:T(8,128)(2,1)S(1)} %get-tuple-element.339), channel_id=1, source_target_pairs={{0,24},{4,28},{8,16},{12,20},{16,8},{20,12},{24,0},{28,4},{1,25},{... | collective-permute-start | bytes 368648 | tf_op jit(solution)/shard_map/ppermute | solution.py:1146
  31.3 12.2 %collective-permute-start.8 = (bf16[80,768]{1,0:T(8,128)(2,1)S(1)}, bf16[80,768]{1,0:T(8,128)(2,1)S(1)}, u32[]{:S(2)}, u32[]{:S(2)}) collective-permute-start(bf16[80,768]{1,0:T(8,128)(2,1)S(1)} %get-tuple-element.339), channel_id=1, source_target_pairs={{0,28},{4,24},{8,20},{12,16},{16,12},{20,8},{24,4},{28,0},{1,29},{... | collective-permute-start | bytes 368648 | tf_op jit(solution)/shard_map/ppermute | solution.py:1146
  31.3 13.7 %collective-permute-start = (bf16[8,768]{1,0:T(8,128)(2,1)S(1)}, bf16[8,768]{1,0:T(8,128)(2,1)S(1)}, u32[]{:S(2)}, u32[]{:S(2)}) collective-permute-start(bf16[8,768]{1,0:T(8,128)(2,1)S(1)} %get-tuple-element.325), channel_id=1, source_target_pairs={{1,0},{2,1},{3,2},{5,4},{6,5},{7,6},{9,8},{10,9},{11,10},{13,12},{... | collective-permute-start | bytes 36872 | tf_op jit(solution)/shard_map/ppermute | solution.py:1234
  34.0 36.0 %collective-permute-start.13 = (f32[6,10,64]{2,0,1:T(8,128)S(1)}, f32[6,10,64]{2,0,1:T(8,128)S(1)}, u32[]{:S(2)}, u32[]{:S(2)}) collective-permute-start(f32[6,10,64]{2,0,1:T(8,128)S(1)} %copy-done.40), channel_id=1, source_target_pairs={{0,2},{1,3},{2,0},{3,1},{4,6},{5,7},{6,4},{7,5},{8,10},{9,11},{10,... | collective-permute-start | bytes 46088 | tf_op jit(solution)/shard_map/ppermute | solution.py:1146
  43.5 27.0 %collective-permute-start.12 = (f32[6,10,64]{2,0,1:T(8,128)S(1)}, f32[6,10,64]{2,0,1:T(8,128)S(1)}, u32[]{:S(2)}, u32[]{:S(2)}) collective-permute-start(f32[6,10,64]{2,0,1:T(8,128)S(1)} %copy-done.40), channel_id=1, source_target_pairs={{0,1},{1,0},{2,3},{3,2},{4,5},{5,4},{6,7},{7,6},{8,9},{9,8},{10,11... | collective-permute-start | bytes 46088 | tf_op jit(solution)/shard_map/ppermute | solution.py:1146
  44.6 23.3 %collective-permute-start.10 = (bf16[6,80,768]{2,1,0:T(8,128)(2,1)S(1)}, bf16[6,80,768]{2,1,0:T(8,128)(2,1)}, u32[]{:S(2)}, u32[]{:S(2)}) collective-permute-start(bf16[6,80,768]{2,1,0:T(8,128)(2,1)S(1)} %pick.1), channel_id=1, source_target_pairs={{0,2},{1,3},{2,0},{3,1},{4,6},{5,7},{6,4},{7,5},{8,10},{9,11},{10,... | collective-permute-start | bytes 2211848 | tf_op jit(solution)/shard_map/ppermute | solution.py:1146
  53.1 22.7 %collective-permute-start.9 = (bf16[6,80,768]{2,1,0:T(8,128)(2,1)S(1)}, bf16[6,80,768]{2,1,0:T(8,128)(2,1)}, u32[]{:S(2)}, u32[]{:S(2)}) collective-permute-start(bf16[6,80,768]{2,1,0:T(8,128)(2,1)S(1)} %pick.1), channel_id=1, source_target_pairs={{0,1},{1,0},{2,3},{3,2},{4,5},{5,4},{6,7},{7,6},{8,9},{9,8},{10,11... | collective-permute-start | bytes 2211848 | tf_op jit(solution)/shard_map/ppermute | solution.py:1146
  67.9 7.9 %collective-permute-start.11 = (bf16[6,80,768]{2,1,0:T(8,128)(2,1)}, bf16[6,80,768]{2,1,0:T(8,128)(2,1)}, u32[]{:S(2)}, u32[]{:S(2)}) collective-permute-start(bf16[6,80,768]{2,1,0:T(8,128)(2,1)} %collective-permute-done.10), channel_id=1, source_target_pairs={{0,1},{1,0},{2,3},{3,2},{4,5},{5,4},{6,7},{7,6},{8,9},{9,8},{10,11... | collective-permute-start | bytes 2211848 | tf_op jit(solution)/shard_map/ppermute | solution.py:1146
  100.4 14.6 %collective-permute-start.15 = (bf16[1608,128]{1,0:T(8,128)(2,1)S(1)}, bf16[1608,128]{1,0:T(8,128)(2,1)S(1)}, u32[]{:S(2)}, u32[]{:S(2)}) collective-permute-start(bf16[1608,128]{1,0:T(8,128)(2,1)S(1)} %pad_maximum_fusion.4.refs_4_), channel_id=1, source_target_pairs={{0,2},{1,3},{2,0},{3,1},{4,6},{5,7},{6,4},{7,5},{8,10},{9,11},{10,... | collective-permute-start | bytes 1234952 | tf_op jit(solution)/shard_map/ppermute | solution.py:1146
  101.1 13.9 %collective-permute-start.16 = (bf16[1608,128]{1,0:T(8,128)(2,1)S(1)}, bf16[1608,128]{1,0:T(8,128)(2,1)S(1)}, u32[]{:S(2)}, u32[]{:S(2)}) collective-permute-start(bf16[1608,128]{1,0:T(8,128)(2,1)S(1)} %pad_maximum_fusion.4.refs_4_), channel_id=1, source_target_pairs={{0,1},{1,0},{2,3},{3,2},{4,5},{5,4},{6,7},{7,6},{8,9},{9,8},{10,11... | collective-permute-start | bytes 1234952 | tf_op jit(solution)/shard_map/ppermute | solution.py:1146
  162.4 13.6 %collective-permute-start.18 = (bf16[1536,128]{1,0:T(8,128)(2,1)}, bf16[1536,128]{1,0:T(8,128)(2,1)S(1)}, u32[]{:S(2)}, u32[]{:S(2)}) collective-permute-start(bf16[1536,128]{1,0:T(8,128)(2,1)} %get-tuple-element.123.refs_4_), channel_id=1, source_target_pairs={{0,2},{1,3},{2,0},{3,1},{4,6},{5,7},{6,4},{7,5},{8,10},{9,11},{10,... | collective-permute-start | bytes 1179656 | tf_op jit(solution)/shard_map/ppermute | solution.py:1146
  182.6 27.5 %collective-permute-start.20 = (bf16[768,768]{1,0:T(8,128)(2,1)S(1)}, bf16[768,768]{1,0:T(8,128)(2,1)S(1)}, u32[]{:S(2)}, u32[]{:S(2)}) collective-permute-start(bf16[768,768]{1,0:T(8,128)(2,1)S(1)} %fusion.13), channel_id=1, source_target_pairs={{0,2},{1,3},{2,0},{3,1},{4,6},{5,7},{6,4},{7,5},{8,10},{9,11},{10,... | collective-permute-start | bytes 3538952 | tf_op jit(solution)/shard_map/ppermute | solution.py:1146
  212.6 18.2 %collective-permute-start.23 = (bf16[4,128,768]{2,1,0:T(8,128)(2,1)S(1)}, bf16[4,128,768]{2,1,0:T(8,128)(2,1)S(1)}, u32[]{:S(2)}, u32[]{:S(2)}) collective-permute-start(bf16[4,128,768]{2,1,0:T(8,128)(2,1)S(1)} %get-tuple-element.137), channel_id=1, source_target_pairs={{0,4},{4,0},{8,12},{12,8},{16,20},{20,16},{24,28},{28,24},{1,5},{5... | collective-permute-start | bytes 2359304 | tf_op jit(solution)/shard_map/ppermute | solution.py:1146
  231.0 29.8 %collective-permute-start.24 = (bf16[2,128,768]{2,1,0:T(8,128)(2,1)S(1)}, bf16[2,128,768]{2,1,0:T(8,128)(2,1)S(1)}, u32[]{:S(2)}, u32[]{:S(2)}) collective-permute-start(bf16[2,128,768]{2,1,0:T(8,128)(2,1)S(1)} %slice.344), channel_id=1, source_target_pairs={{0,16},{4,20},{8,24},{12,28},{16,0},{20,4},{24,8},{28,12},{1,17},{... | collective-permute-start | bytes 1179656 | tf_op jit(solution)/shard_map/ppermute | solution.py:1146
  274.6 18.4 %collective-permute-start.26 = (bf16[480,768]{1,0:T(8,128)(2,1)}, bf16[480,768]{1,0:T(8,128)(2,1)}, u32[]{:S(2)}, u32[]{:S(2)}) collective-permute-start(bf16[480,768]{1,0:T(8,128)(2,1)} %fusion.12), channel_id=1, source_target_pairs={{0,2},{1,3},{2,0},{3,1},{4,6},{5,7},{6,4},{7,5},{8,10},{9,11},{10,... | collective-permute-start | bytes 2211848 | tf_op jit(solution)/shard_map/ppermute | solution.py:1146
  279.6 10.8 %collective-permute-start.27 = (bf16[128,768]{1,0:T(8,128)(2,1)}, bf16[128,768]{1,0:T(8,128)(2,1)}, u32[]{:S(2)}, u32[]{:S(2)}) collective-permute-start(bf16[128,768]{1,0:T(8,128)(2,1)} %fusion.20), channel_id=1, source_target_pairs={{0,8},{4,12},{8,0},{12,4},{16,24},{20,28},{24,16},{28,20},{1,9},{5... | collective-permute-start | bytes 589832 | tf_op jit(solution)/shard_map/ppermute | solution.py:1146
  293.8 12.9 %collective-permute-start.29 = (f32[8,768]{1,0:T(8,128)S(1)}, f32[8,768]{1,0:T(8,128)S(1)}, u32[]{:S(2)}, u32[]{:S(2)}) collective-permute-start(f32[8,768]{1,0:T(8,128)S(1)} %get-tuple-element.318), channel_id=1, source_target_pairs={{1,0},{2,1},{3,2},{5,4},{6,5},{7,6},{9,8},{10,9},{11,10},{13,12},{... | collective-permute-start | bytes 73736 | tf_op jit(solution)/shard_map/ppermute | solution.py:1396
  296.5 18.7 %collective-permute-start.28 = (f32[8,768]{1,0:T(8,128)S(1)}, f32[8,768]{1,0:T(8,128)S(1)}, u32[]{:S(2)}, u32[]{:S(2)}) collective-permute-start(f32[8,768]{1,0:T(8,128)S(1)} %get-tuple-element.317), channel_id=1, source_target_pairs={{0,1},{1,2},{2,3},{4,5},{5,6},{6,7},{8,9},{9,10},{10,11},{12,13},{... | collective-permute-start | bytes 73736 | tf_op jit(solution)/shard_map/ppermute | solution.py:1395
  313.1 7.6 %collective-permute-start.37 = (bf16[80,768]{1,0:T(8,128)(2,1)S(1)}, bf16[80,768]{1,0:T(8,128)(2,1)S(1)}, u32[]{:S(2)}, u32[]{:S(2)}) collective-permute-start(bf16[80,768]{1,0:T(8,128)(2,1)S(1)} %get-tuple-element.176), channel_id=1, source_target_pairs={{0,24},{4,28},{8,16},{12,20},{16,8},{20,12},{24,0},{28,4},{1,25},{... | collective-permute-start | bytes 368648 | tf_op jit(solution)/shard_map/ppermute | solution.py:1146
  315.8 15.6 %collective-permute-start.36 = (bf16[80,768]{1,0:T(8,128)(2,1)S(1)}, bf16[80,768]{1,0:T(8,128)(2,1)S(1)}, u32[]{:S(2)}, u32[]{:S(2)}) collective-permute-start(bf16[80,768]{1,0:T(8,128)(2,1)S(1)} %get-tuple-element.175), channel_id=1, source_target_pairs={{0,20},{4,16},{8,28},{12,24},{16,4},{20,0},{24,12},{28,8},{1,21},{... | collective-permute-start | bytes 368648 | tf_op jit(solution)/shard_map/ppermute | solution.py:1146
  315.9 18.5 %collective-permute-start.35 = (bf16[80,768]{1,0:T(8,128)(2,1)S(1)}, bf16[80,768]{1,0:T(8,128)(2,1)S(1)}, u32[]{:S(2)}, u32[]{:S(2)}) collective-permute-start(bf16[80,768]{1,0:T(8,128)(2,1)S(1)} %get-tuple-element.174), channel_id=1, source_target_pairs={{0,16},{4,20},{8,24},{12,28},{16,0},{20,4},{24,8},{28,12},{1,17},{... | collective-permute-start | bytes 368648 | tf_op jit(solution)/shard_map/ppermute | solution.py:1146
  318.3 16.1 %collective-permute-start.34 = (bf16[80,768]{1,0:T(8,128)(2,1)S(1)}, bf16[80,768]{1,0:T(8,128)(2,1)S(1)}, u32[]{:S(2)}, u32[]{:S(2)}) collective-permute-start(bf16[80,768]{1,0:T(8,128)(2,1)S(1)} %get-tuple-element.173), channel_id=1, source_target_pairs={{0,12},{4,8},{8,4},{12,0},{16,28},{20,24},{24,20},{28,16},{1,13},{... | collective-permute-start | bytes 368648 | tf_op jit(solution)/shard_map/ppermute | solution.py:1146
  318.3 16.1 %collective-permute-start.33 = (bf16[80,768]{1,0:T(8,128)(2,1)S(1)}, bf16[80,768]{1,0:T(8,128)(2,1)S(1)}, u32[]{:S(2)}, u32[]{:S(2)}) collective-permute-start(bf16[80,768]{1,0:T(8,128)(2,1)S(1)} %get-tuple-element.172), channel_id=1, source_target_pairs={{0,8},{4,12},{8,0},{12,4},{16,24},{20,28},{24,16},{28,20},{1,9},{5... | collective-permute-start | bytes 368648 | tf_op jit(solution)/shard_map/ppermute | solution.py:1146
  320.6 13.7 %collective-permute-start.32 = (bf16[80,768]{1,0:T(8,128)(2,1)S(1)}, bf16[80,768]{1,0:T(8,128)(2,1)S(1)}, u32[]{:S(2)}, u32[]{:S(2)}) collective-permute-start(bf16[80,768]{1,0:T(8,128)(2,1)S(1)} %get-tuple-element.171), channel_id=1, source_target_pairs={{0,4},{4,0},{8,12},{12,8},{16,20},{20,16},{24,28},{28,24},{1,5},{5... | collective-permute-start | bytes 368648 | tf_op jit(solution)/shard_map/ppermute | solution.py:1146
  349.5 11.6 %collective-permute-start.43 = (bf16[16,16,768]{2,1,0:T(8,128)(2,1)S(1)}, bf16[16,16,768]{2,1,0:T(8,128)(2,1)S(1)}, u32[]{:S(2)}, u32[]{:S(2)}) collective-permute-start(bf16[16,16,768]{2,1,0:T(8,128)(2,1)S(1)} %get-tuple-element.335), channel_id=1, source_target_pairs={{0,1},{1,0},{2,3},{3,2},{4,5},{5,4},{6,7},{7,6},{8,9},{9,8},{10,11... | collective-permute-start | bytes 1179656 | tf_op jit(solution)/shard_map/ppermute | solution.py:1146
  (82 other events, 725.0 us)
Sparse Core Ops, SparseCore 0:
  10.9 84.4 all-gather.2
